TPU v7x, 512 devices: a whole 4x4x16 slice. The times are simulated.
512 devices in a mesh: blk: 16 (over y, x_hi, core), group: 32 (over x_lo, z).
Axes of the slice: x: 4 (x_hi: 2, x_lo: 2; x = x_hi * 2 + x_lo), y: 4, z: 16, core: 2. Of those that a mesh axis runs over, the one named last changes fastest.
Arguments:
- student_features: bfloat16 [65536, 768], P(('blk', 'group')), may hold values from -8 to 8
- teacher_image: bfloat16 [65536, 1152], P(('blk', 'group')), may hold values from -8 to 8
- text_embeds: bfloat16 [65536, 1152], P(('blk', 'group')), may hold values from -8 to 8
- pair_ids: int32 [65536], replicated, may hold values from 0 to 8191
- head_weights: bfloat16 [1152, 768], replicated, may hold values from -1 to 1
- moment_first: float32 [1152, 768], P('group'), may hold values from -4 to 4
- moment_second: float32 [1152, 768], P('group'), may hold values from 0.01 to 0.3
Outputs:
- row_loss: float32 [65536], P(('blk', 'group'))
- new_first: float32 [1152, 768], P('group')
- new_second: float32 [1152, 768], P('group')
- new_weights: bfloat16 [1152, 768], replicated
All inputs are finite; a program needn't handle non-finite values.
Results may differ from a plain program's by a relative error of at most 0.0025.
The roundings to bfloat16 on the way count: a program that leaves them out, or rounds other values in their place, can miss the bound.
Values may be sent and summed in bfloat16 or wider, within the bound.
No kernel may reach another device: no remote copies, remote signals or barrier semaphores. Data moves between devices by JAX's collectives and lax.ppermute only.
A program may use at most 64 MiB of HBM per device.

v0:
```python
import jax
import jax.numpy as jnp
from jax import lax
from jax.experimental import pallas as pl
from jax.experimental.pallas import tpu as pltpu
from jax.sharding import PartitionSpec as P


student_scale = 20.0
student_bias = -1.0
teacher_scale = 25.0
teacher_bias = -1.5
label_mix = 0.5
norm_eps = 1e-06
beta_one = 0.9
beta_two = 0.95
learn_rate = 0.01
weight_decay = 0.0001
adam_eps = 1e-08
adam_step = 100.0

AXES = ("blk", "group")


def device(X, y, core, z):
    return (y * 4 + X % 2 * 2 + core) * 32 + X // 2 * 16 + z


def x_line(y, core, z):
    return [device(X, y, core, z) for X in range(4)]


def y_line(X, core, z):
    return [device(X, y, core, z) for y in range(4)]


def lines(along_x):
    groups = []
    for core in range(2):
        line = x_line if (core == 0) == along_x else y_line
        groups += [line(i, core, z) for z in range(16) for i in range(4)]
    return groups


FIRST = lines(True)
SECOND = lines(False)
PLANE = [
    [device(X, y, core, z) for X in range(4) for y in range(4)]
    for core in range(2)
    for z in range(16)
]
COLUMN = [
    [device(X, y, core, z) for z in range(16)]
    for X in range(4)
    for y in range(4)
    for core in range(2)
]
TWIN = [(i, i ^ 32) for i in range(512)]


def hop(step):
    pairs = []
    for i in range(512):
        blk, group = divmod(i, 32)
        y, xh, core = blk // 4, blk // 2 % 2, blk % 2
        xl, z = divmod(group, 16)
        x = xh * 2 + xl
        if core == 0:
            y = (y + step) % 4
        else:
            x = (x + step) % 4
        pairs.append((i, device(x % 2 * 2 + x // 2, y, core, z)))
    return pairs


FORTH = hop(1)
BACK = hop(-1)


def exchange(pieces, groups):
    return lax.all_to_all(pieces, AXES, 0, 0, axis_index_groups=groups, tiled=True)


def share(block, groups):
    return exchange(jnp.broadcast_to(block[None], (len(groups[0]), *block.shape)), groups)


def from_twin(shard):
    return lax.ppermute(shard, AXES, TWIN)


def unit_rows(values):
    values = values.astype(jnp.float32)
    return values * lax.rsqrt(jnp.sum(values * values, axis=-1, keepdims=True) + norm_eps)


def copies_kernel(values_ref, out_ref):
    rows = unit_rows(values_ref[...]).astype(jnp.bfloat16)
    for i in range(out_ref.shape[0]):
        out_ref[i] = rows


def unit_copies(values, count):
    return pl.pallas_call(
        copies_kernel,
        out_shape=jax.ShapeDtypeStruct((count, *values.shape), jnp.bfloat16),
        in_specs=[pl.BlockSpec(memory_space=pltpu.VMEM)],
        out_specs=pl.BlockSpec(memory_space=pltpu.VMEM),
    )(values)


def pair_terms(student_rows, teacher_rows, left_ids, text_rows, right_ids):
    dims = (((1,), (1,)), ((), ()))
    student_logit = (
        student_scale
        * lax.dot_general(student_rows, text_rows, dims, preferred_element_type=jnp.float32)
        + student_bias
    )
    teacher_logit = (
        teacher_scale
        * lax.dot_general(teacher_rows, text_rows, dims, preferred_element_type=jnp.float32)
        + teacher_bias
    )
    labels = (left_ids[:, None] == right_ids[None, :]).astype(jnp.float32)
    target = (1.0 - label_mix) * labels + label_mix * jax.nn.sigmoid(teacher_logit)
    losses = jnp.sum(jax.nn.softplus(student_logit) - target * student_logit, axis=1)
    coeff = (jax.nn.sigmoid(student_logit) - target).astype(jnp.bfloat16)
    pulled = jnp.dot(coeff, text_rows, preferred_element_type=jnp.float32)
    return (losses, pulled)


def row_order(core):
    place = lax.iota(jnp.int32, 1280)
    first, second = place // 320, place // 80 % 4
    X = jnp.where(core == 0, first, second)
    y = jnp.where(core == 0, second, first)
    row = (X % 2 * 4 + y) * 5 + place % 5
    return jnp.where(row < 36, X // 2 * 576 + place // 5 % 16 * 36 + row, -1)


def weight_order():
    row = lax.iota(jnp.int32, 576)
    q = row % 36
    return q // 5 * 96 + row // 36 * 5 + q % 5


def grad_order():
    part = lax.iota(jnp.int32, 120)
    q = part % 40
    return q // 5 * 96 + 80 + part // 40 * 5 + q % 5


def one_hot(index, width):
    return (index[:, None] == lax.iota(jnp.int32, width)[None, :]).astype(jnp.bfloat16)


def rounded(values):
    return lax.reduce_precision(values, 8, 7)


def per_device(
    student_features,
    teacher_image,
    text_embeds,
    pair_ids,
    head_weights,
    moment_first,
    moment_second,
):
    rows = student_features.shape[0]
    blk_index = lax.axis_index("blk")
    group_index = lax.axis_index("group")
    y, xh, core = blk_index // 4, blk_index // 2 % 2, blk_index % 2
    xl, z = group_index // 16, group_index % 16

    copies, teacher_image, twin_features = lax.optimization_barrier(
        (unit_copies(text_embeds, 4), teacher_image, student_features)
    )
    bundle = exchange(copies, FIRST).reshape(4 * rows, 1152)
    top, bottom = bundle[: 2 * rows], bundle[2 * rows :]
    before_top = lax.ppermute(top, AXES, FORTH)
    after_bottom = lax.ppermute(bottom, AXES, BACK)
    before_bottom = lax.ppermute(bottom, AXES, FORTH)
    after_top = lax.ppermute(top, AXES, BACK)
    far_top = lax.ppermute(before_top, AXES, FORTH)
    far_bottom = lax.ppermute(after_bottom, AXES, BACK)
    own_features, before_top, after_bottom = lax.optimization_barrier(
        (student_features, before_top, after_bottom)
    )
    features = share(own_features, FIRST)

    both_features = jnp.concatenate([student_features, from_twin(twin_features)], axis=0)
    both_teacher = jnp.concatenate([teacher_image, from_twin(teacher_image)], axis=0)
    projected = lax.dot_general(
        both_features, head_weights, (((1,), (1,)), ((), ())), preferred_element_type=jnp.float32
    )
    inverse = lax.rsqrt(jnp.sum(projected * projected, axis=-1, keepdims=True) + norm_eps)
    student = projected * inverse
    student_b = student.astype(jnp.bfloat16)
    teacher_b = unit_rows(both_teacher).astype(jnp.bfloat16)

    ids_grid = pair_ids.reshape(4, 2, 2, 2, 16, rows)
    ids_plane = lax.dynamic_index_in_dim(ids_grid, z, 4, keepdims=False)
    ids_core = lax.dynamic_index_in_dim(ids_plane, core, 2, keepdims=False)
    ids_yx = ids_core.transpose(0, 2, 1, 3).reshape(4, 4, rows)
    ids_xy = ids_core.transpose(1, 2, 0, 3).reshape(4, 4, rows)
    text_ids = jnp.where(core == 0, ids_yx, ids_xy)
    place = jnp.where(core == 0, y, xh * 2 + xl)

    def ids_at(step):
        return lax.dynamic_index_in_dim(text_ids, (place + step) % 4, 0, keepdims=False)

    ids_rows = pair_ids.reshape(512, rows)
    left_ids = jnp.concatenate(
        [
            lax.dynamic_index_in_dim(ids_rows, blk_index * 32 + group_index, 0, keepdims=False),
            lax.dynamic_index_in_dim(ids_rows, (blk_index ^ 1) * 32 + group_index, 0, keepdims=False),
        ]
    )
    chunks = (
        (bundle, ids_at(0)),
        (before_top, ids_at(3)[:2]),
        (after_bottom, ids_at(1)[2:]),
        (before_bottom, ids_at(3)[2:]),
        (after_top, ids_at(1)[:2]),
        (far_top, ids_at(2)[:2]),
        (far_bottom, ids_at(2)[2:]),
    )
    terms = [
        pair_terms(student_b, teacher_b, left_ids, chunk, ids.reshape(-1)) for chunk, ids in chunks
    ]
    losses, pulled = (sum(term) for term in zip(*terms))
    features, pulled = lax.optimization_barrier((features, pulled))

    pulled = pulled[:rows] + from_twin(pulled[rows:])
    student, inverse = student[:rows], inverse[:rows]
    grad_student = student_scale / rows * pulled
    grad_projected = (
        inverse * (grad_student - student * jnp.sum(student * grad_student, axis=-1, keepdims=True))
    ).astype(jnp.bfloat16)

    grad_rows = lax.dot_general(
        one_hot(row_order(core), 1152),
        grad_projected,
        (((1,), (1,)), ((), ())),
        preferred_element_type=jnp.float32,
    ).astype(jnp.bfloat16)
    grad_rows = exchange(grad_rows.reshape(4, 320, rows), FIRST)
    line_grad = lax.dot_general(
        grad_rows, features, (((0, 2), (0, 1)), ((), ())), preferred_element_type=jnp.float32
    )
    core_grad = jnp.sum(exchange(line_grad.reshape(4, 80, 768), SECOND), axis=0)
    left, right = core_grad[:, :384], core_grad[:, 384:]
    other_losses = jnp.pad(losses[rows:].reshape(1, rows), ((0, 7), (0, 256)))
    arrived = from_twin(jnp.concatenate([jnp.where(core == 0, right, left), other_losses], axis=0))
    chip_grad = jnp.where(core == 0, left, right) + arrived[:80]
    row_loss = (losses[:rows] + arrived[80, :rows]) / rows

    column_grad = jnp.pad(chip_grad.reshape(16, 15, 128), ((0, 0), (0, 1), (0, 0)))
    own_grad = jnp.sum(exchange(column_grad, COLUMN), axis=0)[:15].reshape(5, 384)

    def adam(head_grad, first, second, weights):
        new_first = beta_one * first + (1.0 - beta_one) * head_grad
        new_second = beta_two * second + (1.0 - beta_two) * head_grad * head_grad
        first_hat = new_first / (1.0 - beta_one**adam_step)
        second_hat = new_second / (1.0 - beta_two**adam_step)
        weights = weights.astype(jnp.float32)
        updated = weights - learn_rate * (
            first_hat / (jnp.sqrt(second_hat) + adam_eps) + weight_decay * weights
        )
        return updated.astype(jnp.bfloat16)

    def piece(values, start):
        group_rows = lax.dynamic_slice_in_dim(values, start, 36, 0)
        padded = jnp.pad(group_rows, ((0, 4), (0, 0)))
        return lax.dynamic_slice(padded, ((xh * 4 + y) * 5, core * 384), (5, 384))

    own_weights = adam(
        own_grad,
        piece(moment_first, 0),
        piece(moment_second, 0),
        piece(head_weights, group_index * 36),
    )
    chip_weights = share(own_weights, COLUMN).reshape(80, 384)
    high = rounded(own_grad)
    middle = rounded(own_grad - high)
    low = own_grad - high - middle
    spare = jnp.zeros((1, 384), jnp.float32)
    grad_parts = jnp.concatenate([high, middle, low, spare], axis=0).astype(jnp.bfloat16)
    plane = share(jnp.concatenate([chip_weights, grad_parts], axis=0), PLANE).reshape(2, 768, 384)
    select_weights = one_hot(weight_order(), 768)
    halves = [
        jnp.dot(select_weights, plane[i], preferred_element_type=jnp.float32) for i in range(2)
    ]
    group_parts = jnp.dot(
        one_hot(grad_order(), 768),
        lax.dynamic_index_in_dim(plane, xl, 0, keepdims=False),
        preferred_element_type=jnp.float32,
    )
    half = jnp.concatenate([*halves, group_parts], axis=0).astype(jnp.bfloat16)
    twin_half = from_twin(half)
    whole = jnp.concatenate(
        [jnp.where(core == 0, half, twin_half), jnp.where(core == 0, twin_half, half)], axis=1
    )
    new_weights = whole[:1152]
    parts = whole[1152:].reshape(3, 40, 768).astype(jnp.float32)
    head_grad = ((parts[0] + parts[1]) + parts[2])[:36]
    new_first = beta_one * moment_first + (1.0 - beta_one) * head_grad
    new_second = beta_two * moment_second + (1.0 - beta_two) * head_grad * head_grad
    return (row_loss, new_first, new_second, new_weights)


def solution(mesh):
    placed = (
        P(("blk", "group"), None),
        P(("blk", "group"), None),
        P(("blk", "group"), None),
        P(),
        P(),
        P("group", None),
        P("group", None),
    )
    return jax.shard_map(
        per_device,
        mesh=mesh,
        in_specs=placed,
        out_specs=(P(("blk", "group")), P("group", None), P("group", None), P()),
        check_vma=False,
    )
```

profile of v0, /device:TPU:1, one launch (start us, length us, event | category | flops | bytes accessed | tf_op | source)
XLA Modules:
  0.0 195.0 jit_solution(6038223795710069721)
XLA Ops:
  0.7 2.3 %shard_map.102 = bf16[4,128,1152]{2,1,0:T(8,128)(2,1)} custom-call(bf16[128,1152]{1,0:T(8,128)(2,1)} %values_ref.1), custom_call_target="tpu_custom_call" | custom-call | tf_op jit(solution)/shard_map/pallas_call | solution.py:104
  3.0 8.7 %collective-permute-start.1 = (bf16[128,1152]{1,0:T(8,128)(2,1)S(1)}, bf16[128,1152]{1,0:T(8,128)(2,1)S(1)}, u32[]{:S(2)}, u32[]{:S(2)}) collective-permute-start(bf16[128,1152]{1,0:T(8,128)(2,1)S(1)} %copy-done.7), channel_id=1, source_target_pairs={{0,32},{1,33},{2,34},{3,35},{4,36},{5,37},{6,38},{7,39},{8,40},{9,... | collective-permute-start | bytes 884744 | tf_op jit(solution)/shard_map/ppermute | solution.py:89
  11.7 3.5 %all-to-all-start = ((bf16[4,128,1152]{2,1,0:T(8,128)(2,1)}), bf16[4,128,1152]{2,1,0:T(8,128)(2,1)S(1)}, u32[]{:S(2)}, u32[]{:S(2)}) async-start(bf16[4,128,1152]{2,1,0:T(8,128)(2,1)} %shard_map.102), calls=%async_computation | async-start | bytes 2359296 | tf_op jit(solution)/shard_map/all_to_all | solution.py:81
  26.8 3.3 %collective-permute-start.3 = (bf16[256,1152]{1,0:T(8,128)(2,1)}, bf16[256,1152]{1,0:T(8,128)(2,1)}, u32[]{:S(2)}, u32[]{:S(2)}) collective-permute-start(bf16[256,1152]{1,0:T(8,128)(2,1)} %bitcast.12), channel_id=1, source_target_pairs={{0,384},{1,385},{2,386},{3,387},{4,388},{5,389},{6,390},{7,391},{8... | collective-permute-start | bytes 1769480 | tf_op jit(solution)/shard_map/ppermute | solution.py:182
  30.1 1.9 collective-permute-start.4
  32.1 2.1 %collective-permute-start.2 = (bf16[256,1152]{1,0:T(8,128)(2,1)}, bf16[256,1152]{1,0:T(8,128)(2,1)}, u32[]{:S(2)}, u32[]{:S(2)}) collective-permute-start(bf16[256,1152]{1,0:T(8,128)(2,1)} %bitcast.11), channel_id=1, source_target_pairs={{0,128},{1,129},{2,130},{3,131},{4,132},{5,133},{6,134},{7,135},{8... | collective-permute-start | bytes 1769480 | tf_op jit(solution)/shard_map/ppermute | solution.py:181
  34.2 4.4 %collective-permute-start.5 = (bf16[256,1152]{1,0:T(8,128)(2,1)}, bf16[256,1152]{1,0:T(8,128)(2,1)S(1)}, u32[]{:S(2)}, u32[]{:S(2)}) collective-permute-start(bf16[256,1152]{1,0:T(8,128)(2,1)} %bitcast.11), channel_id=1, source_target_pairs={{0,384},{1,385},{2,386},{3,387},{4,388},{5,389},{6,390},{7,391},{8... | collective-permute-start | bytes 1769480 | tf_op jit(solution)/shard_map/ppermute | solution.py:184
  43.3 5.6 %collective-permute-done.2 = bf16[256,1152]{1,0:T(8,128)(2,1)} collective-permute-done((bf16[256,1152]{1,0:T(8,128)(2,1)}, bf16[256,1152]{1,0:T(8,128)(2,1)}, u32[]{:S(2)}, u32[]{:S(2)}) %collective-permute-start.2) | collective-permute-done | bytes 589856 | tf_op jit(solution)/shard_map/ppermute | solution.py:181
  49.8 4.2 %all-to-all-start.1 = ((bf16[4,128,768]{2,1,0:T(8,128)(2,1)}), bf16[4,128,768]{2,1,0:T(8,128)(2,1)}, u32[]{:S(2)}, u32[]{:S(2)}) async-start(bf16[4,128,768]{2,1,0:T(8,128)(2,1)} %broadcast_in_dim.9), calls=%async_computation.1 | async-start | bytes 1572864 | tf_op jit(solution)/shard_map/all_to_all | solution.py:81
  56.0 3.4 %collective-permute-start.6 = (bf16[256,1152]{1,0:T(8,128)(2,1)}, bf16[256,1152]{1,0:T(8,128)(2,1)S(1)}, u32[]{:S(2)}, u32[]{:S(2)}) collective-permute-start(bf16[256,1152]{1,0:T(8,128)(2,1)} %collective-permute-done.2), channel_id=1, source_target_pairs={{0,128},{1,129},{2,130},{3,131},{4,132},{5,133},{6,134},{7,135},{8... | collective-permute-start | bytes 1769480 | tf_op jit(solution)/shard_map/ppermute | solution.py:185
  61.0 2.1 %fusion.82 = (f32[256]{0:T(256)}, f32[256,256]{0,1:T(8,128)S(1)}) fusion(f32[256,256]{0,1:T(8,128)S(1)} %fusion.66, bf16[256,1152]{1,0:T(8,128)(2,1)S(1)} %copy-done.4, bf16[256,1152]{1,0:T(8,128)(2,1)} %collective-permute-done.2), kind=kOutput, calls=%fused_computation.123 | convolution fusion | flops 151715584 | bytes 1704960 | tf_op jit(solution)/shard_map/dot_general | solution.py:116
  64.7 2.1 %fusion.86 = (f32[256]{0:T(256)}, f32[256,256]{0,1:T(8,128)S(1)}) fusion(f32[256,256]{0,1:T(8,128)S(1)} %fusion.50, bf16[256,1152]{1,0:T(8,128)(2,1)S(1)} %copy-done.4, bf16[256,1152]{1,0:T(8,128)(2,1)} %collective-permute-done.4), kind=kOutput, calls=%fused_computation.127 | convolution fusion | flops 151715584 | bytes 1704960 | tf_op jit(solution)/shard_map/dot_general | solution.py:116
  80.1 4.1 %collective-permute-start.8 = (f32[128,1152]{1,0:T(8,128)S(1)}, f32[128,1152]{1,0:T(8,128)S(1)}, u32[]{:S(2)}, u32[]{:S(2)}) collective-permute-start(f32[128,1152]{1,0:T(8,128)S(1)} %slice.112), channel_id=1, source_target_pairs={{0,32},{1,33},{2,34},{3,35},{4,36},{5,37},{6,38},{7,39},{8,40},{9,... | collective-permute-start | bytes 1769480 | tf_op jit(solution)/shard_map/ppermute | solution.py:89
  87.2 8.3 %all_to_all.35 = bf16[4,320,128]{2,1,0:T(8,128)(2,1)S(1)} all-to-all(bf16[4,320,128]{2,1,0:T(8,128)(2,1)S(1)} %bitcast.90), channel_id=1, replica_groups={{0,64,16,80},{128,192,144,208},{256,320,272,336},{384,448,400,464},{1,6..., dimensions={0} | all-to-all | bytes 655360 | tf_op jit(solution)/shard_map/all_to_all | solution.py:81
  95.6 2.5 %fusion.188 = f32[320,768,1]{1,0,2:T(8,128)} fusion(bf16[4,320,128]{2,1,0:T(8,128)(2,1)S(1)} %all_to_all.35, bf16[4,128,768]{2,1,0:T(8,128)(2,1)} %all-to-all-done.1), kind=kOutput, calls=%fused_computation.303 | convolution fusion | flops 251658240 | bytes 2097152 | tf_op jit(solution)/shard_map/dot_general | solution.py:249
  98.1 4.4 %all-to-all-start.3 = ((f32[4,80,768]{2,1,0:T(8,128)}), f32[4,80,768]{2,1,0:T(8,128)S(1)}, u32[]{:S(2)}, u32[]{:S(2)}) async-start(f32[4,80,768]{2,1,0:T(8,128)} %bitcast.87), calls=%async_computation.3 | async-start | bytes 1966080 | tf_op jit(solution)/shard_map/all_to_all | solution.py:81
  102.5 9.3 %all-to-all-done.3 = f32[4,80,768]{2,1,0:T(8,128)S(1)} async-done(((f32[4,80,768]{2,1,0:T(8,128)}), f32[4,80,768]{2,1,0:T(8,128)S(1)}, u32[]{:S(2)}, u32[]{:S(2)}) %all-to-all-start.3) | async-done | bytes 983072 | tf_op jit(solution)/shard_map/all_to_all | solution.py:81
  112.0 5.7 %collective-permute-start.9 = (f32[88,384]{1,0:T(8,128)S(1)}, f32[88,384]{1,0:T(8,128)S(1)}, u32[]{:S(2)}, u32[]{:S(2)}) collective-permute-start(f32[88,384]{1,0:T(8,128)S(1)} %select_maximum_fusion), channel_id=1, source_target_pairs={{0,32},{1,33},{2,34},{3,35},{4,36},{5,37},{6,38},{7,39},{8,40},{9,... | collective-permute-start | bytes 405512 | tf_op jit(solution)/shard_map/ppermute | solution.py:89
  119.4 12.3 %all-to-all-start.4 = ((f32[16,16,128]{2,1,0:T(8,128)}), f32[16,16,128]{2,1,0:T(8,128)S(1)}, u32[]{:S(2)}, u32[]{:S(2)}) async-start(f32[16,16,128]{2,1,0:T(8,128)} %pad.22), calls=%async_computation.4 | async-start | bytes 262144 | tf_op jit(solution)/shard_map/all_to_all | solution.py:81
  131.8 12.0 %all-to-all-done.4 = f32[16,16,128]{2,1,0:T(8,128)S(1)} async-done(((f32[16,16,128]{2,1,0:T(8,128)}), f32[16,16,128]{2,1,0:T(8,128)S(1)}, u32[]{:S(2)}, u32[]{:S(2)}) %all-to-all-start.4) | async-done | bytes 131104 | tf_op jit(solution)/shard_map/all_to_all | solution.py:81
  144.0 18.2 %all_to_all.36 = bf16[16,5,384]{2,1,0:T(8,128)(2,1)S(1)} all-to-all(bf16[16,5,384]{2,1,0:T(8,128)(2,1)S(1)} %broadcast_in_dim.10), channel_id=1, replica_groups={{0,1,2,3,4,5,6,7,8,9,10,11,12,13,14,15},{32,33,34,35,36,37,38,39,40,41,..., dimensions={0} | all-to-all | bytes 122880 | tf_op jit(solution)/shard_map/all_to_all | solution.py:81
  163.5 3.7 %all-to-all-start.6 = ((bf16[16,96,384]{2,1,0:T(8,128)(2,1)}), bf16[16,96,384]{2,1,0:T(8,128)(2,1)S(1)}, u32[]{:S(2)}, u32[]{:S(2)}) async-start(bf16[16,96,384]{2,1,0:T(8,128)(2,1)} %broadcast_in_dim.12), calls=%async_computation.6 | async-start | bytes 2359296 | tf_op jit(solution)/shard_map/all_to_all | solution.py:81
  167.3 14.3 %all-to-all-done.6 = bf16[16,96,384]{2,1,0:T(8,128)(2,1)S(1)} async-done(((bf16[16,96,384]{2,1,0:T(8,128)(2,1)}), bf16[16,96,384]{2,1,0:T(8,128)(2,1)S(1)}, u32[]{:S(2)}, u32[]{:S(2)}) %all-to-all-start.6) | async-done | bytes 1179680 | tf_op jit(solution)/shard_map/all_to_all | solution.py:81
  183.4 6.8 %collective-permute-start.10 = (bf16[1272,384]{1,0:T(8,128)(2,1)S(1)}, bf16[1272,384]{1,0:T(8,128)(2,1)S(1)}, u32[]{:S(2)}, u32[]{:S(2)}) collective-permute-start(bf16[1272,384]{1,0:T(8,128)(2,1)S(1)} %pad_maximum_fusion.1), channel_id=1, source_target_pairs={{0,32},{1,33},{2,34},{3,35},{4,36},{5,37},{6,38},{7,39},{8,40},{9,... | collective-permute-start | bytes 2930696 | tf_op jit(solution)/shard_map/ppermute | solution.py:89
  (139 shorter events, 48.1 us)
Async XLA Ops:
  0.6 20.1 %copy-start = (bf16[1152,768]{1,0:T(8,128)(2,1)S(1)}, bf16[1152,768]{1,0:T(8,128)(2,1)}, u32[]{:S(2)}) copy-start(bf16[1152,768]{1,0:T(8,128)(2,1)} %param.11) | copy-start | bytes 5308420
  3.0 21.0 %collective-permute-start.1 = (bf16[128,1152]{1,0:T(8,128)(2,1)S(1)}, bf16[128,1152]{1,0:T(8,128)(2,1)S(1)}, u32[]{:S(2)}, u32[]{:S(2)}) collective-permute-start(bf16[128,1152]{1,0:T(8,128)(2,1)S(1)} %copy-done.7), channel_id=1, source_target_pairs={{0,32},{1,33},{2,34},{3,35},{4,36},{5,37},{6,38},{7,39},{8,40},{9,... | collective-permute-start | bytes 884744 | tf_op jit(solution)/shard_map/ppermute | solution.py:89
  11.7 14.0 %all-to-all-start = ((bf16[4,128,1152]{2,1,0:T(8,128)(2,1)}), bf16[4,128,1152]{2,1,0:T(8,128)(2,1)S(1)}, u32[]{:S(2)}, u32[]{:S(2)}) async-start(bf16[4,128,1152]{2,1,0:T(8,128)(2,1)} %shard_map.102), calls=%async_computation | async-start | bytes 2359296 | tf_op jit(solution)/shard_map/all_to_all | solution.py:81
  15.3 5.5 %collective-permute-start = (bf16[128,768]{1,0:T(8,128)(2,1)}, bf16[128,768]{1,0:T(8,128)(2,1)}, u32[]{:S(2)}, u32[]{:S(2)}) collective-permute-start(bf16[128,768]{1,0:T(8,128)(2,1)} %param.7), channel_id=1, source_target_pairs={{0,32},{1,33},{2,34},{3,35},{4,36},{5,37},{6,38},{7,39},{8,40},{9,... | collective-permute-start | bytes 589832 | tf_op jit(solution)/shard_map/ppermute | solution.py:89
  22.6 61.8 %copy-start.16 = (f32[256]{0:T(256)}, f32[256]{0:T(256)S(1)}, u32[]{:S(2)}) copy-start(f32[256]{0:T(256)S(1)} %add_rsqrt_fusion.1) | copy-start | bytes 3076
  26.8 22.1 %collective-permute-start.3 = (bf16[256,1152]{1,0:T(8,128)(2,1)}, bf16[256,1152]{1,0:T(8,128)(2,1)}, u32[]{:S(2)}, u32[]{:S(2)}) collective-permute-start(bf16[256,1152]{1,0:T(8,128)(2,1)} %bitcast.12), channel_id=1, source_target_pairs={{0,384},{1,385},{2,386},{3,387},{4,388},{5,389},{6,390},{7,391},{8... | collective-permute-start | bytes 1769480 | tf_op jit(solution)/shard_map/ppermute | solution.py:182
  30.1 33.0 %collective-permute-start.4 = (bf16[256,1152]{1,0:T(8,128)(2,1)}, bf16[256,1152]{1,0:T(8,128)(2,1)}, u32[]{:S(2)}, u32[]{:S(2)}) collective-permute-start(bf16[256,1152]{1,0:T(8,128)(2,1)} %bitcast.12), channel_id=1, source_target_pairs={{0,128},{1,129},{2,130},{3,131},{4,132},{5,133},{6,134},{7,135},{8... | collective-permute-start | bytes 1769480 | tf_op jit(solution)/shard_map/ppermute | solution.py:183
  32.1 16.8 %collective-permute-start.2 = (bf16[256,1152]{1,0:T(8,128)(2,1)}, bf16[256,1152]{1,0:T(8,128)(2,1)}, u32[]{:S(2)}, u32[]{:S(2)}) collective-permute-start(bf16[256,1152]{1,0:T(8,128)(2,1)} %bitcast.11), channel_id=1, source_target_pairs={{0,128},{1,129},{2,130},{3,131},{4,132},{5,133},{6,134},{7,135},{8... | collective-permute-start | bytes 1769480 | tf_op jit(solution)/shard_map/ppermute | solution.py:181
  34.2 35.8 %collective-permute-start.5 = (bf16[256,1152]{1,0:T(8,128)(2,1)}, bf16[256,1152]{1,0:T(8,128)(2,1)S(1)}, u32[]{:S(2)}, u32[]{:S(2)}) collective-permute-start(bf16[256,1152]{1,0:T(8,128)(2,1)} %bitcast.11), channel_id=1, source_target_pairs={{0,384},{1,385},{2,386},{3,387},{4,388},{5,389},{6,390},{7,391},{8... | collective-permute-start | bytes 1769480 | tf_op jit(solution)/shard_map/ppermute | solution.py:184
  43.3 16.0 %copy-start.9 = (bf16[128,1152]{1,0:T(8,128)(2,1)S(1)}, bf16[128,1152]{1,0:T(8,128)(2,1)}, u32[]{:S(2)}) copy-start(bf16[128,1152]{1,0:T(8,128)(2,1)} %param.8) | copy-start | bytes 884740
  43.3 16.0 %copy-start.12 = (bf16[128,1152]{1,0:T(8,128)(2,1)S(1)}, bf16[128,1152]{1,0:T(8,128)(2,1)}, u32[]{:S(2)}) copy-start(bf16[128,1152]{1,0:T(8,128)(2,1)} %copy-done.11) | copy-start | bytes 884740
  43.3 16.0 %copy-start.22 = (s32[256]{0:T(256)S(1)}, s32[256]{0:T(256)}, u32[]{:S(2)}) copy-start(s32[256]{0:T(256)} %get-tuple-element.43) | copy-start | bytes 3076
  49.8 30.2 %all-to-all-start.1 = ((bf16[4,128,768]{2,1,0:T(8,128)(2,1)}), bf16[4,128,768]{2,1,0:T(8,128)(2,1)}, u32[]{:S(2)}, u32[]{:S(2)}) async-start(bf16[4,128,768]{2,1,0:T(8,128)(2,1)} %broadcast_in_dim.9), calls=%async_computation.1 | async-start | bytes 1572864 | tf_op jit(solution)/shard_map/all_to_all | solution.py:81
  54.0 22.9 %collective-permute-start.7 = (bf16[256,1152]{1,0:T(8,128)(2,1)}, bf16[256,1152]{1,0:T(8,128)(2,1)S(1)}, u32[]{:S(2)}, u32[]{:S(2)}) collective-permute-start(bf16[256,1152]{1,0:T(8,128)(2,1)} %collective-permute-done.3), channel_id=1, source_target_pairs={{0,384},{1,385},{2,386},{3,387},{4,388},{5,389},{6,390},{7,391},{8... | collective-permute-start | bytes 1769480 | tf_op jit(solution)/shard_map/ppermute | solution.py:186
  56.0 22.4 %collective-permute-start.6 = (bf16[256,1152]{1,0:T(8,128)(2,1)}, bf16[256,1152]{1,0:T(8,128)(2,1)S(1)}, u32[]{:S(2)}, u32[]{:S(2)}) collective-permute-start(bf16[256,1152]{1,0:T(8,128)(2,1)} %collective-permute-done.2), channel_id=1, source_target_pairs={{0,128},{1,129},{2,130},{3,131},{4,132},{5,133},{6,134},{7,135},{8... | collective-permute-start | bytes 1769480 | tf_op jit(solution)/shard_map/ppermute | solution.py:185
  80.1 5.6 %collective-permute-start.8 = (f32[128,1152]{1,0:T(8,128)S(1)}, f32[128,1152]{1,0:T(8,128)S(1)}, u32[]{:S(2)}, u32[]{:S(2)}) collective-permute-start(f32[128,1152]{1,0:T(8,128)S(1)} %slice.112), channel_id=1, source_target_pairs={{0,32},{1,33},{2,34},{3,35},{4,36},{5,37},{6,38},{7,39},{8,40},{9,... | collective-permute-start | bytes 1769480 | tf_op jit(solution)/shard_map/ppermute | solution.py:89
  98.1 13.8 %all-to-all-start.3 = ((f32[4,80,768]{2,1,0:T(8,128)}), f32[4,80,768]{2,1,0:T(8,128)S(1)}, u32[]{:S(2)}, u32[]{:S(2)}) async-start(f32[4,80,768]{2,1,0:T(8,128)} %bitcast.87), calls=%async_computation.3 | async-start | bytes 1966080 | tf_op jit(solution)/shard_map/all_to_all | solution.py:81
  111.9 31.9 %copy-start.5 = (f32[36,768]{1,0:T(8,128)S(1)}, f32[36,768]{1,0:T(8,128)}, u32[]{:S(2)}) copy-start(f32[36,768]{1,0:T(8,128)} %param.13) | copy-start | bytes 331780
  111.9 31.9 %copy-start.6 = (f32[36,768]{1,0:T(8,128)S(1)}, f32[36,768]{1,0:T(8,128)}, u32[]{:S(2)}) copy-start(f32[36,768]{1,0:T(8,128)} %param.12) | copy-start | bytes 331780
  112.0 6.7 %collective-permute-start.9 = (f32[88,384]{1,0:T(8,128)S(1)}, f32[88,384]{1,0:T(8,128)S(1)}, u32[]{:S(2)}, u32[]{:S(2)}) collective-permute-start(f32[88,384]{1,0:T(8,128)S(1)} %select_maximum_fusion), channel_id=1, source_target_pairs={{0,32},{1,33},{2,34},{3,35},{4,36},{5,37},{6,38},{7,39},{8,40},{9,... | collective-permute-start | bytes 405512 | tf_op jit(solution)/shard_map/ppermute | solution.py:89
  118.7 43.5 %copy-start.15 = (f32[88,384]{1,0:T(8,128)}, f32[88,384]{1,0:T(8,128)S(1)}, u32[]{:S(2)}) copy-start(f32[88,384]{1,0:T(8,128)S(1)} %collective-permute-done.9) | copy-start | bytes 405508
  119.4 24.4 %all-to-all-start.4 = ((f32[16,16,128]{2,1,0:T(8,128)}), f32[16,16,128]{2,1,0:T(8,128)S(1)}, u32[]{:S(2)}, u32[]{:S(2)}) async-start(f32[16,16,128]{2,1,0:T(8,128)} %pad.22), calls=%async_computation.4 | async-start | bytes 262144 | tf_op jit(solution)/shard_map/all_to_all | solution.py:81
  163.5 18.0 %all-to-all-start.6 = ((bf16[16,96,384]{2,1,0:T(8,128)(2,1)}), bf16[16,96,384]{2,1,0:T(8,128)(2,1)S(1)}, u32[]{:S(2)}, u32[]{:S(2)}) async-start(bf16[16,96,384]{2,1,0:T(8,128)(2,1)} %broadcast_in_dim.12), calls=%async_computation.6 | async-start | bytes 2359296 | tf_op jit(solution)/shard_map/all_to_all | solution.py:81
  183.4 9.0 %collective-permute-start.10 = (bf16[1272,384]{1,0:T(8,128)(2,1)S(1)}, bf16[1272,384]{1,0:T(8,128)(2,1)S(1)}, u32[]{:S(2)}, u32[]{:S(2)}) collective-permute-start(bf16[1272,384]{1,0:T(8,128)(2,1)S(1)} %pad_maximum_fusion.1), channel_id=1, source_target_pairs={{0,32},{1,33},{2,34},{3,35},{4,36},{5,37},{6,38},{7,39},{8,40},{9,... | collective-permute-start | bytes 2930696 | tf_op jit(solution)/shard_map/ppermute | solution.py:89
  (20 other events, 69.9 us)
where the time goes:
time: 196 us; the launch traced here: 195 us
  starting transfers between devices  72.5 us (37%)
  waiting for transfers between devices  46 us (23%)
  matrix products  31.9 us (16%)
  blocking collectives  26.5 us (14%)
  local copies, waits for them, and re-layouts  8.24 us (4%)
  other arithmetic  6.04 us (3%)
  Pallas kernels  2.3 us (1%)
    all_to_all x5, waiting for transfers between devices, exchange(): lax.all_to_all(pieces, AXES, 0, 0, axis_index_groups=groups, tiled=True)  37.1 us
    all_to_all x5, starting transfers between devices, exchange(): lax.all_to_all(pieces, AXES, 0, 0, axis_index_groups=groups, tiled=True)  28.1 us
    ppermute x5, starting transfers between devices, from_twin(): return lax.ppermute(shard, AXES, TWIN)  27.3 us
    all_to_all x2, blocking collectives, exchange(): lax.all_to_all(pieces, AXES, 0, 0, axis_index_groups=groups, tiled=True)  26.5 us
    dot_general x7, matrix products, pair_terms(): lax.dot_general(student_rows, text_rows, dims, preferred_element_type=jnp...  9.46 us
    dot_general x7, matrix products, pair_terms(): lax.dot_general(teacher_rows, text_rows, dims, preferred_element_type=jnp...  7.84 us
    dot_general x7, matrix products, pair_terms(): pulled = jnp.dot(coeff, text_rows, preferred_element_type=jnp.float32)  7.35 us
    ppermute x1, waiting for transfers between devices, per_device(): before_top = lax.ppermute(top, AXES, FORTH)  5.57 us
  transfers between devices with their start and end apart: 16, of which 8 were waited for; matrix products, arithmetic and copies ran while one was open for 17% of the time, Pallas kernels for 0%

commit v1 on v0

--- a/solution.py
+++ b/solution.py
@@ -1,3 +1,5 @@
+import functools
+
 import jax
 import jax.numpy as jnp
 from jax import lax
@@ -94,19 +96,28 @@
     return values * lax.rsqrt(jnp.sum(values * values, axis=-1, keepdims=True) + norm_eps)
 
 
-def copies_kernel(values_ref, out_ref):
+def copies_kernel(values_ref, others_ref, out_ref):
+    width = values_ref.shape[1]
     rows = unit_rows(values_ref[...]).astype(jnp.bfloat16)
     for i in range(out_ref.shape[0]):
-        out_ref[i] = rows
-
-
-def unit_copies(values, count):
+        out_ref[i, :, :width] = rows
+        out_ref[i, :, width:] = others_ref[...]
+
+
+def unit_copies(values, others, count):
+    width = values.shape[1] + others.shape[1]
     return pl.pallas_call(
         copies_kernel,
-        out_shape=jax.ShapeDtypeStruct((count, *values.shape), jnp.bfloat16),
-        in_specs=[pl.BlockSpec(memory_space=pltpu.VMEM)],
+        out_shape=jax.ShapeDtypeStruct((count, values.shape[0], width), jnp.bfloat16),
+        in_specs=[pl.BlockSpec(memory_space=pltpu.VMEM)] * 2,
         out_specs=pl.BlockSpec(memory_space=pltpu.VMEM),
-    )(values)
+        compiler_params=pltpu.CompilerParams(vmem_limit_bytes=8 << 20),
+        cost_estimate=pl.CostEstimate(
+            flops=4 * values.size,
+            bytes_accessed=2 * values.size + 2 * count * values.shape[0] * width,
+            transcendentals=0,
+        ),
+    )(values, others)
 
 
 def pair_terms(student_rows, teacher_rows, left_ids, text_rows, right_ids):
@@ -121,12 +132,57 @@
         * lax.dot_general(teacher_rows, text_rows, dims, preferred_element_type=jnp.float32)
         + teacher_bias
     )
-    labels = (left_ids[:, None] == right_ids[None, :]).astype(jnp.float32)
+    labels = (left_ids == right_ids).astype(jnp.float32)
     target = (1.0 - label_mix) * labels + label_mix * jax.nn.sigmoid(teacher_logit)
-    losses = jnp.sum(jax.nn.softplus(student_logit) - target * student_logit, axis=1)
-    coeff = (jax.nn.sigmoid(student_logit) - target).astype(jnp.bfloat16)
-    pulled = jnp.dot(coeff, text_rows, preferred_element_type=jnp.float32)
-    return (losses, pulled)
+    tail = jnp.exp(-jnp.abs(student_logit))
+    softplus = jnp.maximum(student_logit, 0.0) + jnp.log1p(tail)
+    chance = jnp.where(student_logit >= 0.0, 1.0, tail) / (1.0 + tail)
+    losses = jnp.sum(softplus - target * student_logit, axis=1, keepdims=True)
+    return losses, (chance - target).astype(jnp.bfloat16)
+
+
+def pair_kernel(parts, carried, *refs):
+    student_ref, teacher_ref, left_ref = refs[:3]
+    chunks, ids = refs[3 : 3 + parts], refs[3 + parts : 3 + 2 * parts]
+    rest = refs[3 + 2 * parts :]
+    pulled_ref, losses_ref = rest[-2:]
+    if carried:
+        pulled_ref[...] = rest[0][...]
+        losses_ref[...] = rest[1][...]
+    else:
+        pulled_ref[...] = jnp.zeros_like(pulled_ref)
+        losses_ref[...] = jnp.zeros_like(losses_ref)
+    for chunk_ref, ids_ref in zip(chunks, ids):
+        texts = chunk_ref[...]
+        losses, coeff = pair_terms(
+            student_ref[...], teacher_ref[...], left_ref[...], texts, ids_ref[...]
+        )
+        losses_ref[...] += losses
+        pulled_ref[...] += jnp.dot(coeff, texts, preferred_element_type=jnp.float32)
+
+
+def pair_sums(student_rows, teacher_rows, left_ids, chunks, carried=()):
+    rows, width = student_rows.shape
+    texts = [chunk for chunk, _ in chunks]
+    ids = [ids.reshape(1, -1) for _, ids in chunks]
+    count = sum(chunk.shape[0] for chunk in texts)
+    operands = (student_rows, teacher_rows, left_ids, *texts, *ids, *carried)
+    whole = pl.BlockSpec(memory_space=pltpu.VMEM)
+    return pl.pallas_call(
+        functools.partial(pair_kernel, len(texts), bool(carried)),
+        out_shape=(
+            jax.ShapeDtypeStruct((rows, width), jnp.float32),
+            jax.ShapeDtypeStruct((rows, 1), jnp.float32),
+        ),
+        in_specs=[whole] * len(operands),
+        out_specs=(whole, whole),
+        compiler_params=pltpu.CompilerParams(vmem_limit_bytes=20 << 20),
+        cost_estimate=pl.CostEstimate(
+            flops=6 * rows * count * width,
+            bytes_accessed=2 * count * width,
+            transcendentals=4 * rows * count,
+        ),
+    )(*operands)
 
 
 def row_order(core):
@@ -174,23 +230,22 @@
     xl, z = group_index // 16, group_index % 16
 
     copies, teacher_image, twin_features = lax.optimization_barrier(
-        (unit_copies(text_embeds, 4), teacher_image, student_features)
-    )
-    bundle = exchange(copies, FIRST).reshape(4 * rows, 1152)
-    top, bottom = bundle[: 2 * rows], bundle[2 * rows :]
+        (unit_copies(text_embeds, student_features, 4), teacher_image, student_features)
+    )
+    near = exchange(copies, FIRST)
+    top = near[:2, :, :1152].reshape(2 * rows, 1152)
+    bottom = near[2:, :, :1152].reshape(2 * rows, 1152)
+    features = near[:, :, 1152:]
     before_top = lax.ppermute(top, AXES, FORTH)
     after_bottom = lax.ppermute(bottom, AXES, BACK)
     before_bottom = lax.ppermute(bottom, AXES, FORTH)
     after_top = lax.ppermute(top, AXES, BACK)
     far_top = lax.ppermute(before_top, AXES, FORTH)
     far_bottom = lax.ppermute(after_bottom, AXES, BACK)
-    own_features, before_top, after_bottom = lax.optimization_barrier(
-        (student_features, before_top, after_bottom)
-    )
-    features = share(own_features, FIRST)
-
-    both_features = jnp.concatenate([student_features, from_twin(twin_features)], axis=0)
-    both_teacher = jnp.concatenate([teacher_image, from_twin(teacher_image)], axis=0)
+
+    far_features, far_teacher = from_twin(twin_features), from_twin(teacher_image)
+    both_features = jnp.concatenate([student_features, far_features], axis=0)
+    both_teacher = jnp.concatenate([teacher_image, far_teacher], axis=0)
     projected = lax.dot_general(
         both_features, head_weights, (((1,), (1,)), ((), ())), preferred_element_type=jnp.float32
     )
@@ -217,20 +272,20 @@
             lax.dynamic_index_in_dim(ids_rows, (blk_index ^ 1) * 32 + group_index, 0, keepdims=False),
         ]
     )
-    chunks = (
-        (bundle, ids_at(0)),
+    images = (student_b, teacher_b, left_ids.reshape(-1, 1))
+    own_chunks = [(top, ids_at(0)[:2]), (bottom, ids_at(0)[2:])]
+    sums = pair_sums(*images, own_chunks)
+    near_chunks = [
         (before_top, ids_at(3)[:2]),
         (after_bottom, ids_at(1)[2:]),
         (before_bottom, ids_at(3)[2:]),
         (after_top, ids_at(1)[:2]),
-        (far_top, ids_at(2)[:2]),
-        (far_bottom, ids_at(2)[2:]),
-    )
-    terms = [
-        pair_terms(student_b, teacher_b, left_ids, chunk, ids.reshape(-1)) for chunk, ids in chunks
     ]
-    losses, pulled = (sum(term) for term in zip(*terms))
-    features, pulled = lax.optimization_barrier((features, pulled))
+    sums = pair_sums(*images, near_chunks, sums)
+    pulled, losses = pair_sums(
+        *images, [(far_top, ids_at(2)[:2]), (far_bottom, ids_at(2)[2:])], sums
+    )
+    losses = losses.reshape(-1)
 
     pulled = pulled[:rows] + from_twin(pulled[rows:])
     student, inverse = student[:rows], inverse[:rows]

time: 196 us -> 179 us (0.913)
  matrix products: 31.9 us -> 7.22 us
  Pallas kernels: 2.3 us -> 8.14 us
  waiting for transfers between devices: 46 us -> 51.2 us
  starting transfers between devices: 72.5 us -> 67.8 us
  blocking collectives: 26.5 us -> 28.5 us
    dot_general x21 -> x0, matrix products: 24.6 us -> none  [the longest x7 9.46 us: pair_terms(): lax.dot_general(student_rows, text_rows, dims, preferred_element_type=jnp...]
    all_to_all x5 -> x4, waiting for transfers between devices: 37.1 us -> 46.5 us  [exchange(): lax.all_to_all(pieces, AXES, 0, 0, axis_index_groups=groups, tiled=True)]
    all_to_all x5 -> x4, starting transfers between devices: 28.1 us -> 21.4 us  [exchange(): lax.all_to_all(pieces, AXES, 0, 0, axis_index_groups=groups, tiled=True)]
    pallas_call x1 -> x4, Pallas kernels: 2.3 us -> 8.14 us  [the longest x3 6.95 us: pair_sums(): pl.pallas_call(functools.partial(pair_kernel, len(texts), bool(carried)),...]
    ppermute x1, waiting for transfers between devices: 5.57 us -> 0.01 us  [per_device(): before_top = lax.ppermute(top, AXES, FORTH)]
    ppermute x1, starting transfers between devices: 1.92 us -> 4.57 us  [per_device(): far_bottom = lax.ppermute(after_bottom, AXES, BACK)]
    all_to_all x2, blocking collectives: 26.5 us -> 28.5 us  [exchange(): lax.all_to_all(pieces, AXES, 0, 0, axis_index_groups=groups, tiled=True)]
  transfers between devices with their start and end apart: 16 -> 15, of which waited for: 8 -> 8; matrix products, arithmetic and copies ran while one was open for 17% -> 5% of each run, Pallas kernels for 0% -> 3%
where the time goes in v1:
time: 179 us; the launch traced here: 178 us
  starting transfers between devices  67.8 us (38%)
  waiting for transfers between devices  51.2 us (29%)
  blocking collectives  28.5 us (16%)
  Pallas kernels  8.14 us (5%)
  local copies, waits for them, and re-layouts  7.82 us (4%)
  matrix products  7.22 us (4%)
  other arithmetic  6.1 us (3%)
    all_to_all x4, waiting for transfers between devices, exchange(): lax.all_to_all(pieces, AXES, 0, 0, axis_index_groups=groups, tiled=True)  46.5 us
    all_to_all x2, blocking collectives, exchange(): lax.all_to_all(pieces, AXES, 0, 0, axis_index_groups=groups, tiled=True)  28.5 us
    ppermute x5, starting transfers between devices, from_twin(): return lax.ppermute(shard, AXES, TWIN)  26.9 us
    all_to_all x4, starting transfers between devices, exchange(): lax.all_to_all(pieces, AXES, 0, 0, axis_index_groups=groups, tiled=True)  21.4 us
    pallas_call x3, Pallas kernels, pair_sums(): pl.pallas_call(functools.partial(pair_kernel, len(texts), bool(carried)),...  6.95 us
    ppermute x1, starting transfers between devices, per_device(): after_top = lax.ppermute(top, AXES, BACK)  4.57 us
    ppermute x1, starting transfers between devices, per_device(): far_bottom = lax.ppermute(after_bottom, AXES, BACK)  4.57 us
    ppermute x1, starting transfers between devices, per_device(): after_bottom = lax.ppermute(bottom, AXES, BACK)  4.57 us
  transfers between devices with their start and end apart: 15, of which 8 were waited for; matrix products, arithmetic and copies ran while one was open for 5% of the time, Pallas kernels for 3%

profile of v1, /device:TPU:1, one launch (start us, length us, event | category | flops | bytes accessed | tf_op | source)
XLA Modules:
  0.0 178.1 jit_solution(6401793808202507757)
XLA Ops:
  4.2 8.7 %collective-permute-start.1 = (bf16[128,1152]{1,0:T(8,128)(2,1)S(1)}, bf16[128,1152]{1,0:T(8,128)(2,1)}, u32[]{:S(2)}, u32[]{:S(2)}) collective-permute-start(bf16[128,1152]{1,0:T(8,128)(2,1)S(1)} %copy-done.3), channel_id=1, source_target_pairs={{0,32},{1,33},{2,34},{3,35},{4,36},{5,37},{6,38},{7,39},{8,40},{9,... | collective-permute-start | bytes 884744 | tf_op jit(solution)/shard_map/ppermute | solution.py:91
  13.0 1.9 %collective-permute-start = (bf16[128,768]{1,0:T(8,128)(2,1)}, bf16[128,768]{1,0:T(8,128)(2,1)}, u32[]{:S(2)}, u32[]{:S(2)}) collective-permute-start(bf16[128,768]{1,0:T(8,128)(2,1)} %others_ref.1), channel_id=1, source_target_pairs={{0,32},{1,33},{2,34},{3,35},{4,36},{5,37},{6,38},{7,39},{8,40},{9,... | collective-permute-start | bytes 589832 | tf_op jit(solution)/shard_map/ppermute | solution.py:91
  14.9 4.4 %all-to-all-start = ((bf16[4,128,1920]{2,1,0:T(8,128)(2,1)}), bf16[4,128,1920]{2,1,0:T(8,128)(2,1)}, u32[]{:S(2)}, u32[]{:S(2)}) async-start(bf16[4,128,1920]{2,1,0:T(8,128)(2,1)} %copy-done.1), calls=%async_computation | async-start | bytes 3932160 | tf_op jit(solution)/shard_map/all_to_all | solution.py:83
  23.1 11.0 %all-to-all-done = bf16[4,128,1920]{2,1,0:T(8,128)(2,1)} async-done(((bf16[4,128,1920]{2,1,0:T(8,128)(2,1)}), bf16[4,128,1920]{2,1,0:T(8,128)(2,1)}, u32[]{:S(2)}, u32[]{:S(2)}) %all-to-all-start) | async-done | bytes 1966112 | tf_op jit(solution)/shard_map/all_to_all | solution.py:83
  35.4 1.9 %collective-permute-start.2 = (bf16[256,1152]{1,0:T(8,128)(2,1)S(1)}, bf16[256,1152]{1,0:T(8,128)(2,1)S(1)}, u32[]{:S(2)}, u32[]{:S(2)}) collective-permute-start(bf16[256,1152]{1,0:T(8,128)(2,1)S(1)} %bitcast.47), channel_id=1, source_target_pairs={{0,128},{1,129},{2,130},{3,131},{4,132},{5,133},{6,134},{7,135},{8... | collective-permute-start | bytes 1769480 | tf_op jit(solution)/shard_map/ppermute | solution.py:239
  37.3 4.6 %collective-permute-start.4 = (bf16[256,1152]{1,0:T(8,128)(2,1)S(1)}, bf16[256,1152]{1,0:T(8,128)(2,1)S(1)}, u32[]{:S(2)}, u32[]{:S(2)}) collective-permute-start(bf16[256,1152]{1,0:T(8,128)(2,1)S(1)} %bitcast.50), channel_id=1, source_target_pairs={{0,384},{1,385},{2,386},{3,387},{4,388},{5,389},{6,390},{7,391},{8... | collective-permute-start | bytes 1769480 | tf_op jit(solution)/shard_map/ppermute | solution.py:240
  43.3 1.9 %collective-permute-start.6 = (bf16[256,1152]{1,0:T(8,128)(2,1)S(1)}, bf16[256,1152]{1,0:T(8,128)(2,1)S(1)}, u32[]{:S(2)}, u32[]{:S(2)}) collective-permute-start(bf16[256,1152]{1,0:T(8,128)(2,1)S(1)} %bitcast.51), channel_id=1, source_target_pairs={{0,128},{1,129},{2,130},{3,131},{4,132},{5,133},{6,134},{7,135},{8... | collective-permute-start | bytes 1769480 | tf_op jit(solution)/shard_map/ppermute | solution.py:241
  45.2 4.6 %collective-permute-start.7 = (bf16[256,1152]{1,0:T(8,128)(2,1)S(1)}, bf16[256,1152]{1,0:T(8,128)(2,1)S(1)}, u32[]{:S(2)}, u32[]{:S(2)}) collective-permute-start(bf16[256,1152]{1,0:T(8,128)(2,1)S(1)} %bitcast.48), channel_id=1, source_target_pairs={{0,384},{1,385},{2,386},{3,387},{4,388},{5,389},{6,390},{7,391},{8... | collective-permute-start | bytes 1769480 | tf_op jit(solution)/shard_map/ppermute | solution.py:242
  49.8 1.9 %collective-permute-start.3 = (bf16[256,1152]{1,0:T(8,128)(2,1)S(1)}, bf16[256,1152]{1,0:T(8,128)(2,1)S(1)}, u32[]{:S(2)}, u32[]{:S(2)}) collective-permute-start(bf16[256,1152]{1,0:T(8,128)(2,1)S(1)} %collective-permute-done.2.refs_3_), channel_id=1, source_target_pairs={{0,128},{1,129},{2,130},{3,131},{4,132},{5,133},{6,134},{7,135},{8... | collective-permute-start | bytes 1769480 | tf_op jit(solution)/shard_map/ppermute | solution.py:243
  51.8 4.6 %collective-permute-start.5 = (bf16[256,1152]{1,0:T(8,128)(2,1)S(1)}, bf16[256,1152]{1,0:T(8,128)(2,1)S(1)}, u32[]{:S(2)}, u32[]{:S(2)}) collective-permute-start(bf16[256,1152]{1,0:T(8,128)(2,1)S(1)} %collective-permute-done.4.refs_4_), channel_id=1, source_target_pairs={{0,384},{1,385},{2,386},{3,387},{4,388},{5,389},{6,390},{7,391},{8... | collective-permute-start | bytes 1769480 | tf_op jit(solution)/shard_map/ppermute | solution.py:244
  59.3 3.3 %shard_map.104 = (f32[256,1152]{1,0:T(8,128)S(1)}, f32[256,1]{1,0:T(8,128)S(1)}) custom-call(bf16[256,1152]{1,0:T(8,128)(2,1)S(1)} %get-tuple-element.24.refs_0_, bf16[256,1152]{1,0:T(8,128)(2,1)S(1)} %fusion.8.refs_1_, s32[256,1]{1,0:T(8,128)S(1)} %copy.24.refs_2_, bf16[256,1152]{1,0:T(8,128)(2,1)S(1)} %collective-permute-done.2.refs_3_, ...), custom_call_target="tpu_custom_call" | custom-call | flops 1811939328 | bytes 2359296 | tf_op jit(solution)/shard_map/pallas_call | solution.py:171
  63.1 1.8 %shard_map.105 = (f32[256,1152]{1,0:T(8,128)S(1)}, f32[256,1]{1,0:T(8,128)S(1)}) custom-call(bf16[256,1152]{1,0:T(8,128)(2,1)S(1)} %get-tuple-element.24.refs_0_, bf16[256,1152]{1,0:T(8,128)(2,1)S(1)} %fusion.8.refs_1_, s32[256,1]{1,0:T(8,128)S(1)} %copy.24.refs_2_, bf16[256,1152]{1,0:T(8,128)(2,1)S(1)} %collective-permute-done.3.refs_3_, ...), custom_call_target="tpu_custom_call" | custom-call | flops 905969664 | bytes 1179648 | tf_op jit(solution)/shard_map/pallas_call | solution.py:171
  65.0 5.5 %collective-permute-start.8 = (f32[128,1152]{1,0:T(8,128)S(1)}, f32[128,1152]{1,0:T(8,128)S(1)}, u32[]{:S(2)}, u32[]{:S(2)}) collective-permute-start(f32[128,1152]{1,0:T(8,128)S(1)} %slice.122), channel_id=1, source_target_pairs={{0,32},{1,33},{2,34},{3,35},{4,36},{5,37},{6,38},{7,39},{8,40},{9,... | collective-permute-start | bytes 1769480 | tf_op jit(solution)/shard_map/ppermute | solution.py:91
  73.6 10.4 %all_to_all.30 = bf16[4,320,128]{2,1,0:T(8,128)(2,1)S(1)} all-to-all(bf16[4,320,128]{2,1,0:T(8,128)(2,1)S(1)} %bitcast.65), channel_id=1, replica_groups={{0,64,16,80},{128,192,144,208},{256,320,272,336},{384,448,400,464},{1,6..., dimensions={0} | all-to-all | bytes 655360 | tf_op jit(solution)/shard_map/all_to_all | solution.py:83
  84.0 2.5 %fusion.11 = f32[320,768,1]{1,0,2:T(8,128)} fusion(bf16[4,320,128]{2,1,0:T(8,128)(2,1)S(1)} %all_to_all.30, bf16[4,128,1920]{2,1,0:T(8,128)(2,1)} %all-to-all-done), kind=kOutput, calls=%fused_computation.21 | convolution fusion | flops 251658240 | bytes 2097152 | tf_op jit(solution)/shard_map/dot_general | solution.py:304
  86.5 3.5 %all-to-all-start.2 = ((f32[4,80,768]{2,1,0:T(8,128)}), f32[4,80,768]{2,1,0:T(8,128)S(1)}, u32[]{:S(2)}, u32[]{:S(2)}) async-start(f32[4,80,768]{2,1,0:T(8,128)} %bitcast.62), calls=%async_computation.2 | async-start | bytes 1966080 | tf_op jit(solution)/shard_map/all_to_all | solution.py:83
  90.1 9.2 %all-to-all-done.2 = f32[4,80,768]{2,1,0:T(8,128)S(1)} async-done(((f32[4,80,768]{2,1,0:T(8,128)}), f32[4,80,768]{2,1,0:T(8,128)S(1)}, u32[]{:S(2)}, u32[]{:S(2)}) %all-to-all-start.2) | async-done | bytes 983072 | tf_op jit(solution)/shard_map/all_to_all | solution.py:83
  99.5 4.0 %collective-permute-start.9 = (f32[88,384]{1,0:T(8,128)S(1)}, f32[88,384]{1,0:T(8,128)S(1)}, u32[]{:S(2)}, u32[]{:S(2)}) collective-permute-start(f32[88,384]{1,0:T(8,128)S(1)} %select_maximum_fusion), channel_id=1, source_target_pairs={{0,32},{1,33},{2,34},{3,35},{4,36},{5,37},{6,38},{7,39},{8,40},{9,... | collective-permute-start | bytes 405512 | tf_op jit(solution)/shard_map/ppermute | solution.py:91
  105.1 9.6 %all-to-all-start.3 = ((f32[16,16,128]{2,1,0:T(8,128)}), f32[16,16,128]{2,1,0:T(8,128)S(1)}, u32[]{:S(2)}, u32[]{:S(2)}) async-start(f32[16,16,128]{2,1,0:T(8,128)} %pad.22), calls=%async_computation.3 | async-start | bytes 262144 | tf_op jit(solution)/shard_map/all_to_all | solution.py:83
  114.8 12.0 %all-to-all-done.3 = f32[16,16,128]{2,1,0:T(8,128)S(1)} async-done(((f32[16,16,128]{2,1,0:T(8,128)}), f32[16,16,128]{2,1,0:T(8,128)S(1)}, u32[]{:S(2)}, u32[]{:S(2)}) %all-to-all-start.3) | async-done | bytes 131104 | tf_op jit(solution)/shard_map/all_to_all | solution.py:83
  127.0 18.2 %all_to_all.31 = bf16[16,5,384]{2,1,0:T(8,128)(2,1)S(1)} all-to-all(bf16[16,5,384]{2,1,0:T(8,128)(2,1)S(1)} %broadcast_in_dim.8), channel_id=1, replica_groups={{0,1,2,3,4,5,6,7,8,9,10,11,12,13,14,15},{32,33,34,35,36,37,38,39,40,41,..., dimensions={0} | all-to-all | bytes 122880 | tf_op jit(solution)/shard_map/all_to_all | solution.py:83
  146.5 3.9 %all-to-all-start.5 = ((bf16[16,96,384]{2,1,0:T(8,128)(2,1)}), bf16[16,96,384]{2,1,0:T(8,128)(2,1)S(1)}, u32[]{:S(2)}, u32[]{:S(2)}) async-start(bf16[16,96,384]{2,1,0:T(8,128)(2,1)} %broadcast_in_dim.10), calls=%async_computation.5 | async-start | bytes 2359296 | tf_op jit(solution)/shard_map/all_to_all | solution.py:83
  150.4 14.3 %all-to-all-done.5 = bf16[16,96,384]{2,1,0:T(8,128)(2,1)S(1)} async-done(((bf16[16,96,384]{2,1,0:T(8,128)(2,1)}), bf16[16,96,384]{2,1,0:T(8,128)(2,1)S(1)}, u32[]{:S(2)}, u32[]{:S(2)}) %all-to-all-start.5) | async-done | bytes 1179680 | tf_op jit(solution)/shard_map/all_to_all | solution.py:83
  166.6 6.8 %collective-permute-start.10 = (bf16[1272,384]{1,0:T(8,128)(2,1)S(1)}, bf16[1272,384]{1,0:T(8,128)(2,1)S(1)}, u32[]{:S(2)}, u32[]{:S(2)}) collective-permute-start(bf16[1272,384]{1,0:T(8,128)(2,1)S(1)} %pad_maximum_fusion.1), channel_id=1, source_target_pairs={{0,32},{1,33},{2,34},{3,35},{4,36},{5,37},{6,38},{7,39},{8,40},{9,... | collective-permute-start | bytes 2930696 | tf_op jit(solution)/shard_map/ppermute | solution.py:91
  (78 shorter events, 26.3 us)
Async XLA Ops:
  0.6 20.6 %copy-start = (bf16[1152,768]{1,0:T(8,128)(2,1)S(1)}, bf16[1152,768]{1,0:T(8,128)(2,1)}, u32[]{:S(2)}) copy-start(bf16[1152,768]{1,0:T(8,128)(2,1)} %param.11) | copy-start | bytes 5308420
  0.6 1.1 copy-start.2
  1.7 2.5 %copy-start.3 = (bf16[128,1152]{1,0:T(8,128)(2,1)S(1)}, bf16[128,1152]{1,0:T(8,128)(2,1)}, u32[]{:S(2)}) copy-start(bf16[128,1152]{1,0:T(8,128)(2,1)} %param.8) | copy-start | bytes 884740
  2.9 1.3 copy-start.1
  4.2 37.9 %collective-permute-start.1 = (bf16[128,1152]{1,0:T(8,128)(2,1)S(1)}, bf16[128,1152]{1,0:T(8,128)(2,1)}, u32[]{:S(2)}, u32[]{:S(2)}) collective-permute-start(bf16[128,1152]{1,0:T(8,128)(2,1)S(1)} %copy-done.3), channel_id=1, source_target_pairs={{0,32},{1,33},{2,34},{3,35},{4,36},{5,37},{6,38},{7,39},{8,40},{9,... | collective-permute-start | bytes 884744 | tf_op jit(solution)/shard_map/ppermute | solution.py:91
  13.0 8.3 %collective-permute-start = (bf16[128,768]{1,0:T(8,128)(2,1)}, bf16[128,768]{1,0:T(8,128)(2,1)}, u32[]{:S(2)}, u32[]{:S(2)}) collective-permute-start(bf16[128,768]{1,0:T(8,128)(2,1)} %others_ref.1), channel_id=1, source_target_pairs={{0,32},{1,33},{2,34},{3,35},{4,36},{5,37},{6,38},{7,39},{8,40},{9,... | collective-permute-start | bytes 589832 | tf_op jit(solution)/shard_map/ppermute | solution.py:91
  14.9 19.2 %all-to-all-start = ((bf16[4,128,1920]{2,1,0:T(8,128)(2,1)}), bf16[4,128,1920]{2,1,0:T(8,128)(2,1)}, u32[]{:S(2)}, u32[]{:S(2)}) async-start(bf16[4,128,1920]{2,1,0:T(8,128)(2,1)} %copy-done.1), calls=%async_computation | async-start | bytes 3932160 | tf_op jit(solution)/shard_map/all_to_all | solution.py:83
  23.1 47.5 %copy-start.6 = (f32[256]{0:T(256)}, f32[256]{0:T(256)S(1)}, u32[]{:S(2)}) copy-start(f32[256]{0:T(256)S(1)} %add_rsqrt_fusion.1) | copy-start | bytes 3076
  35.4 14.4 %collective-permute-start.2 = (bf16[256,1152]{1,0:T(8,128)(2,1)S(1)}, bf16[256,1152]{1,0:T(8,128)(2,1)S(1)}, u32[]{:S(2)}, u32[]{:S(2)}) collective-permute-start(bf16[256,1152]{1,0:T(8,128)(2,1)S(1)} %bitcast.47), channel_id=1, source_target_pairs={{0,128},{1,129},{2,130},{3,131},{4,132},{5,133},{6,134},{7,135},{8... | collective-permute-start | bytes 1769480 | tf_op jit(solution)/shard_map/ppermute | solution.py:239
  37.3 14.4 %collective-permute-start.4 = (bf16[256,1152]{1,0:T(8,128)(2,1)S(1)}, bf16[256,1152]{1,0:T(8,128)(2,1)S(1)}, u32[]{:S(2)}, u32[]{:S(2)}) collective-permute-start(bf16[256,1152]{1,0:T(8,128)(2,1)S(1)} %bitcast.50), channel_id=1, source_target_pairs={{0,384},{1,385},{2,386},{3,387},{4,388},{5,389},{6,390},{7,391},{8... | collective-permute-start | bytes 1769480 | tf_op jit(solution)/shard_map/ppermute | solution.py:240
  43.3 16.0 %collective-permute-start.6 = (bf16[256,1152]{1,0:T(8,128)(2,1)S(1)}, bf16[256,1152]{1,0:T(8,128)(2,1)S(1)}, u32[]{:S(2)}, u32[]{:S(2)}) collective-permute-start(bf16[256,1152]{1,0:T(8,128)(2,1)S(1)} %bitcast.51), channel_id=1, source_target_pairs={{0,128},{1,129},{2,130},{3,131},{4,132},{5,133},{6,134},{7,135},{8... | collective-permute-start | bytes 1769480 | tf_op jit(solution)/shard_map/ppermute | solution.py:241
  45.2 14.1 %collective-permute-start.7 = (bf16[256,1152]{1,0:T(8,128)(2,1)S(1)}, bf16[256,1152]{1,0:T(8,128)(2,1)S(1)}, u32[]{:S(2)}, u32[]{:S(2)}) collective-permute-start(bf16[256,1152]{1,0:T(8,128)(2,1)S(1)} %bitcast.48), channel_id=1, source_target_pairs={{0,384},{1,385},{2,386},{3,387},{4,388},{5,389},{6,390},{7,391},{8... | collective-permute-start | bytes 1769480 | tf_op jit(solution)/shard_map/ppermute | solution.py:242
  49.8 12.8 %collective-permute-start.3 = (bf16[256,1152]{1,0:T(8,128)(2,1)S(1)}, bf16[256,1152]{1,0:T(8,128)(2,1)S(1)}, u32[]{:S(2)}, u32[]{:S(2)}) collective-permute-start(bf16[256,1152]{1,0:T(8,128)(2,1)S(1)} %collective-permute-done.2.refs_3_), channel_id=1, source_target_pairs={{0,128},{1,129},{2,130},{3,131},{4,132},{5,133},{6,134},{7,135},{8... | collective-permute-start | bytes 1769480 | tf_op jit(solution)/shard_map/ppermute | solution.py:243
  51.8 11.4 %collective-permute-start.5 = (bf16[256,1152]{1,0:T(8,128)(2,1)S(1)}, bf16[256,1152]{1,0:T(8,128)(2,1)S(1)}, u32[]{:S(2)}, u32[]{:S(2)}) collective-permute-start(bf16[256,1152]{1,0:T(8,128)(2,1)S(1)} %collective-permute-done.4.refs_4_), channel_id=1, source_target_pairs={{0,384},{1,385},{2,386},{3,387},{4,388},{5,389},{6,390},{7,391},{8... | collective-permute-start | bytes 1769480 | tf_op jit(solution)/shard_map/ppermute | solution.py:244
  65.0 7.1 %collective-permute-start.8 = (f32[128,1152]{1,0:T(8,128)S(1)}, f32[128,1152]{1,0:T(8,128)S(1)}, u32[]{:S(2)}, u32[]{:S(2)}) collective-permute-start(f32[128,1152]{1,0:T(8,128)S(1)} %slice.122), channel_id=1, source_target_pairs={{0,32},{1,33},{2,34},{3,35},{4,36},{5,37},{6,38},{7,39},{8,40},{9,... | collective-permute-start | bytes 1769480 | tf_op jit(solution)/shard_map/ppermute | solution.py:91
  70.6 1.7 slice-start
  86.5 12.9 %all-to-all-start.2 = ((f32[4,80,768]{2,1,0:T(8,128)}), f32[4,80,768]{2,1,0:T(8,128)S(1)}, u32[]{:S(2)}, u32[]{:S(2)}) async-start(f32[4,80,768]{2,1,0:T(8,128)} %bitcast.62), calls=%async_computation.2 | async-start | bytes 1966080 | tf_op jit(solution)/shard_map/all_to_all | solution.py:83
  90.1 36.7 %copy-start.4 = (f32[36,768]{1,0:T(8,128)S(1)}, f32[36,768]{1,0:T(8,128)}, u32[]{:S(2)}) copy-start(f32[36,768]{1,0:T(8,128)} %param.13) | copy-start | bytes 331780
  90.1 36.7 %copy-start.5 = (f32[36,768]{1,0:T(8,128)S(1)}, f32[36,768]{1,0:T(8,128)}, u32[]{:S(2)}) copy-start(f32[36,768]{1,0:T(8,128)} %param.12) | copy-start | bytes 331780
  99.5 4.9 %collective-permute-start.9 = (f32[88,384]{1,0:T(8,128)S(1)}, f32[88,384]{1,0:T(8,128)S(1)}, u32[]{:S(2)}, u32[]{:S(2)}) collective-permute-start(f32[88,384]{1,0:T(8,128)S(1)} %select_maximum_fusion), channel_id=1, source_target_pairs={{0,32},{1,33},{2,34},{3,35},{4,36},{5,37},{6,38},{7,39},{8,40},{9,... | collective-permute-start | bytes 405512 | tf_op jit(solution)/shard_map/ppermute | solution.py:91
  105.1 21.7 %all-to-all-start.3 = ((f32[16,16,128]{2,1,0:T(8,128)}), f32[16,16,128]{2,1,0:T(8,128)S(1)}, u32[]{:S(2)}, u32[]{:S(2)}) async-start(f32[16,16,128]{2,1,0:T(8,128)} %pad.22), calls=%async_computation.3 | async-start | bytes 262144 | tf_op jit(solution)/shard_map/all_to_all | solution.py:83
  146.5 18.2 %all-to-all-start.5 = ((bf16[16,96,384]{2,1,0:T(8,128)(2,1)}), bf16[16,96,384]{2,1,0:T(8,128)(2,1)S(1)}, u32[]{:S(2)}, u32[]{:S(2)}) async-start(bf16[16,96,384]{2,1,0:T(8,128)(2,1)} %broadcast_in_dim.10), calls=%async_computation.5 | async-start | bytes 2359296 | tf_op jit(solution)/shard_map/all_to_all | solution.py:83
  166.6 9.0 %collective-permute-start.10 = (bf16[1272,384]{1,0:T(8,128)(2,1)S(1)}, bf16[1272,384]{1,0:T(8,128)(2,1)S(1)}, u32[]{:S(2)}, u32[]{:S(2)}) collective-permute-start(bf16[1272,384]{1,0:T(8,128)(2,1)S(1)} %pad_maximum_fusion.1), channel_id=1, source_target_pairs={{0,32},{1,33},{2,34},{3,35},{4,36},{5,37},{6,38},{7,39},{8,40},{9,... | collective-permute-start | bytes 2930696 | tf_op jit(solution)/shard_map/ppermute | solution.py:91

commit v2 on v1

--- a/solution.py
+++ b/solution.py
@@ -28,24 +28,6 @@
     return (y * 4 + X % 2 * 2 + core) * 32 + X // 2 * 16 + z
 
 
-def x_line(y, core, z):
-    return [device(X, y, core, z) for X in range(4)]
-
-
-def y_line(X, core, z):
-    return [device(X, y, core, z) for y in range(4)]
-
-
-def lines(along_x):
-    groups = []
-    for core in range(2):
-        line = x_line if (core == 0) == along_x else y_line
-        groups += [line(i, core, z) for z in range(16) for i in range(4)]
-    return groups
-
-
-FIRST = lines(True)
-SECOND = lines(False)
 PLANE = [
     [device(X, y, core, z) for X in range(4) for y in range(4)]
     for core in range(2)
@@ -60,23 +42,27 @@
 TWIN = [(i, i ^ 32) for i in range(512)]
 
 
-def hop(step):
+def hop(step, first):
     pairs = []
     for i in range(512):
         blk, group = divmod(i, 32)
         y, xh, core = blk // 4, blk // 2 % 2, blk % 2
         xl, z = divmod(group, 16)
         x = xh * 2 + xl
-        if core == 0:
+        if (core == 0) == first:
+            x = (x + step) % 4
+        else:
             y = (y + step) % 4
-        else:
-            x = (x + step) % 4
         pairs.append((i, device(x % 2 * 2 + x // 2, y, core, z)))
     return pairs
 
 
-FORTH = hop(1)
-BACK = hop(-1)
+FIRST = {step: hop(step, True) for step in (1, 2, 3)}
+SECOND = {step: hop(step, False) for step in (1, 2, 3)}
+
+
+def moved(shard, pairs):
+    return lax.ppermute(shard, AXES, pairs)
 
 
 def exchange(pieces, groups):
@@ -96,28 +82,50 @@
     return values * lax.rsqrt(jnp.sum(values * values, axis=-1, keepdims=True) + norm_eps)
 
 
-def copies_kernel(values_ref, others_ref, out_ref):
-    width = values_ref.shape[1]
-    rows = unit_rows(values_ref[...]).astype(jnp.bfloat16)
-    for i in range(out_ref.shape[0]):
-        out_ref[i, :, :width] = rows
-        out_ref[i, :, width:] = others_ref[...]
-
-
-def unit_copies(values, others, count):
-    width = values.shape[1] + others.shape[1]
+def head_kernel(texts_ref, teacher_ref, features_ref, near_ref, images_ref):
+    width = texts_ref.shape[1]
+    depth = features_ref.shape[1]
+    near_ref[:, :width] = unit_rows(texts_ref[...]).astype(jnp.bfloat16)
+    near_ref[:, width:] = features_ref[...]
+    images_ref[:, :depth] = features_ref[...]
+    images_ref[:, depth:] = unit_rows(teacher_ref[...]).astype(jnp.bfloat16)
+
+
+def head(texts, teacher, features):
+    shape = (texts.shape[0], texts.shape[1] + features.shape[1])
+    whole = pl.BlockSpec(memory_space=pltpu.VMEM)
     return pl.pallas_call(
-        copies_kernel,
-        out_shape=jax.ShapeDtypeStruct((count, values.shape[0], width), jnp.bfloat16),
-        in_specs=[pl.BlockSpec(memory_space=pltpu.VMEM)] * 2,
-        out_specs=pl.BlockSpec(memory_space=pltpu.VMEM),
+        head_kernel,
+        out_shape=(jax.ShapeDtypeStruct(shape, jnp.bfloat16),) * 2,
+        in_specs=[whole] * 3,
+        out_specs=(whole, whole),
         compiler_params=pltpu.CompilerParams(vmem_limit_bytes=8 << 20),
         cost_estimate=pl.CostEstimate(
-            flops=4 * values.size,
-            bytes_accessed=2 * values.size + 2 * count * values.shape[0] * width,
-            transcendentals=0,
+            flops=8 * texts.size, bytes_accessed=8 * shape[0] * shape[1], transcendentals=0
         ),
-    )(values, others)
+    )(texts, teacher, features)
+
+
+def line_kernel(*refs):
+    grads, nears, out_ref = refs[:4], refs[4:8], refs[8]
+    total = jnp.zeros(out_ref.shape, jnp.float32)
+    for grad_ref, near_ref in zip(grads, nears):
+        total += jnp.dot(grad_ref[...], near_ref[:, 1152:], preferred_element_type=jnp.float32)
+    out_ref[...] = total
+
+
+def line_sum(grads, nears):
+    whole = pl.BlockSpec(memory_space=pltpu.VMEM)
+    return pl.pallas_call(
+        line_kernel,
+        out_shape=jax.ShapeDtypeStruct((320, 768), jnp.float32),
+        in_specs=[whole] * 8,
+        out_specs=whole,
+        compiler_params=pltpu.CompilerParams(vmem_limit_bytes=12 << 20),
+        cost_estimate=pl.CostEstimate(
+            flops=8 * 320 * 128 * 768, bytes_accessed=4 << 20, transcendentals=0
+        ),
+    )(*grads, *nears)
 
 
 def pair_terms(student_rows, teacher_rows, left_ids, text_rows, right_ids):
@@ -185,13 +193,13 @@
     )(*operands)
 
 
-def row_order(core):
+def row_order(x, y, core):
     place = lax.iota(jnp.int32, 1280)
     first, second = place // 320, place // 80 % 4
-    X = jnp.where(core == 0, first, second)
-    y = jnp.where(core == 0, second, first)
-    row = (X % 2 * 4 + y) * 5 + place % 5
-    return jnp.where(row < 36, X // 2 * 576 + place // 5 % 16 * 36 + row, -1)
+    x = (x + jnp.where(core == 0, first, second)) % 4
+    y = (y + jnp.where(core == 0, second, first)) % 4
+    row = (x // 2 * 4 + y) * 5 + place % 5
+    return jnp.where(row < 36, x % 2 * 576 + place // 5 % 16 * 36 + row, -1)
 
 
 def weight_order():
@@ -229,41 +237,44 @@
     y, xh, core = blk_index // 4, blk_index // 2 % 2, blk_index % 2
     xl, z = group_index // 16, group_index % 16
 
-    copies, teacher_image, twin_features = lax.optimization_barrier(
-        (unit_copies(text_embeds, student_features, 4), teacher_image, student_features)
-    )
-    near = exchange(copies, FIRST)
-    top = near[:2, :, :1152].reshape(2 * rows, 1152)
-    bottom = near[2:, :, :1152].reshape(2 * rows, 1152)
-    features = near[:, :, 1152:]
-    before_top = lax.ppermute(top, AXES, FORTH)
-    after_bottom = lax.ppermute(bottom, AXES, BACK)
-    before_bottom = lax.ppermute(bottom, AXES, FORTH)
-    after_top = lax.ppermute(top, AXES, BACK)
-    far_top = lax.ppermute(before_top, AXES, FORTH)
-    far_bottom = lax.ppermute(after_bottom, AXES, BACK)
-
-    far_features, far_teacher = from_twin(twin_features), from_twin(teacher_image)
-    both_features = jnp.concatenate([student_features, far_features], axis=0)
-    both_teacher = jnp.concatenate([teacher_image, far_teacher], axis=0)
+    x = xh * 2 + xl
+    near, images = head(text_embeds, teacher_image, student_features)
+    near_before = moved(near, FIRST[1])
+    near_after = moved(near, FIRST[3])
+    near_far = moved(near, FIRST[2])
+    far_images = from_twin(images)
+    width = text_embeds.shape[1]
+    top = jnp.concatenate([near[:, :width], near_before[:, :width]], axis=0)
+    bottom = jnp.concatenate([near_after[:, :width], near_far[:, :width]], axis=0)
+    before_top = moved(top, SECOND[1])
+    after_top = moved(top, SECOND[3])
+    after_bottom = moved(bottom, SECOND[3])
+    before_bottom = moved(bottom, SECOND[1])
+    far_top = moved(before_top, SECOND[1])
+    far_bottom = moved(after_bottom, SECOND[3])
+
+    depth = student_features.shape[1]
+    both_features = jnp.concatenate([student_features, far_images[:, :depth]], axis=0)
+    teacher_b = jnp.concatenate([images[:, depth:], far_images[:, depth:]], axis=0)
     projected = lax.dot_general(
         both_features, head_weights, (((1,), (1,)), ((), ())), preferred_element_type=jnp.float32
     )
     inverse = lax.rsqrt(jnp.sum(projected * projected, axis=-1, keepdims=True) + norm_eps)
     student = projected * inverse
     student_b = student.astype(jnp.bfloat16)
-    teacher_b = unit_rows(both_teacher).astype(jnp.bfloat16)
 
     ids_grid = pair_ids.reshape(4, 2, 2, 2, 16, rows)
     ids_plane = lax.dynamic_index_in_dim(ids_grid, z, 4, keepdims=False)
     ids_core = lax.dynamic_index_in_dim(ids_plane, core, 2, keepdims=False)
-    ids_yx = ids_core.transpose(0, 2, 1, 3).reshape(4, 4, rows)
-    ids_xy = ids_core.transpose(1, 2, 0, 3).reshape(4, 4, rows)
-    text_ids = jnp.where(core == 0, ids_yx, ids_xy)
-    place = jnp.where(core == 0, y, xh * 2 + xl)
-
-    def ids_at(step):
-        return lax.dynamic_index_in_dim(text_ids, (place + step) % 4, 0, keepdims=False)
+    ids_yx = ids_core.reshape(4, 4, rows)
+    text_ids = jnp.where(core == 0, ids_yx, ids_yx.transpose(1, 0, 2))
+    first, second = jnp.where(core == 0, x, y), jnp.where(core == 0, y, x)
+    text_ids = jnp.concatenate([text_ids, text_ids], axis=0)
+    text_ids = lax.dynamic_slice_in_dim(text_ids, second, 4, 0)
+    text_ids = jnp.concatenate([text_ids, text_ids], axis=1)
+    text_ids = lax.dynamic_slice_in_dim(text_ids, first, 4, 1)
+    top_ids = jnp.concatenate([text_ids[:, 0], text_ids[:, 3]], axis=1)
+    bottom_ids = jnp.concatenate([text_ids[:, 1], text_ids[:, 2]], axis=1)
 
     ids_rows = pair_ids.reshape(512, rows)
     left_ids = jnp.concatenate(
@@ -272,19 +283,18 @@
             lax.dynamic_index_in_dim(ids_rows, (blk_index ^ 1) * 32 + group_index, 0, keepdims=False),
         ]
     )
-    images = (student_b, teacher_b, left_ids.reshape(-1, 1))
-    own_chunks = [(top, ids_at(0)[:2]), (bottom, ids_at(0)[2:])]
-    sums = pair_sums(*images, own_chunks)
+    pair_rows = (student_b, teacher_b, left_ids.reshape(-1, 1))
+    own_chunks = [(top, top_ids[0]), (bottom, bottom_ids[0])]
+    sums = pair_sums(*pair_rows, own_chunks)
     near_chunks = [
-        (before_top, ids_at(3)[:2]),
-        (after_bottom, ids_at(1)[2:]),
-        (before_bottom, ids_at(3)[2:]),
-        (after_top, ids_at(1)[:2]),
+        (before_top, top_ids[3]),
+        (after_top, top_ids[1]),
+        (after_bottom, bottom_ids[1]),
+        (before_bottom, bottom_ids[3]),
     ]
-    sums = pair_sums(*images, near_chunks, sums)
-    pulled, losses = pair_sums(
-        *images, [(far_top, ids_at(2)[:2]), (far_bottom, ids_at(2)[2:])], sums
-    )
+    sums = pair_sums(*pair_rows, near_chunks, sums)
+    far_chunks = [(far_top, top_ids[2]), (far_bottom, bottom_ids[2])]
+    pulled, losses = pair_sums(*pair_rows, far_chunks, sums)
     losses = losses.reshape(-1)
 
     pulled = pulled[:rows] + from_twin(pulled[rows:])
@@ -295,16 +305,22 @@
     ).astype(jnp.bfloat16)
 
     grad_rows = lax.dot_general(
-        one_hot(row_order(core), 1152),
+        one_hot(row_order(x, y, core), 1152),
         grad_projected,
         (((1,), (1,)), ((), ())),
         preferred_element_type=jnp.float32,
     ).astype(jnp.bfloat16)
-    grad_rows = exchange(grad_rows.reshape(4, 320, rows), FIRST)
-    line_grad = lax.dot_general(
-        grad_rows, features, (((0, 2), (0, 1)), ((), ())), preferred_element_type=jnp.float32
-    )
-    core_grad = jnp.sum(exchange(line_grad.reshape(4, 80, 768), SECOND), axis=0)
+    grad_rows = grad_rows.reshape(4, 320, rows)
+    grads = (
+        grad_rows[0],
+        moved(grad_rows[1], FIRST[1]),
+        moved(grad_rows[3], FIRST[3]),
+        moved(grad_rows[2], FIRST[2]),
+    )
+    line_grad = line_sum(grads, (near, near_before, near_after, near_far)).reshape(4, 80, 768)
+    core_grad = (line_grad[0] + moved(line_grad[1], SECOND[1])) + (
+        moved(line_grad[2], SECOND[2]) + moved(line_grad[3], SECOND[3])
+    )
     left, right = core_grad[:, :384], core_grad[:, 384:]
     other_losses = jnp.pad(losses[rows:].reshape(1, rows), ((0, 7), (0, 256)))
     arrived = from_twin(jnp.concatenate([jnp.where(core == 0, right, left), other_losses], axis=0))

time: 179 us -> 180 us (level)
  starting transfers between devices: 67.8 us -> 85.5 us
  blocking collectives: 28.5 us -> 18.3 us
  waiting for transfers between devices: 51.2 us -> 43.9 us
  local copies, waits for them, and re-layouts: 7.82 us -> 12.6 us
  matrix products: 7.22 us -> 3.71 us
  other arithmetic: 6.1 us -> 4.07 us
    ppermute x6 -> x15, starting transfers between devices: 19.5 us -> 45.3 us  [moved(): return lax.ppermute(shard, AXES, pairs)]
    all_to_all x4 -> x2, waiting for transfers between devices: 46.5 us -> 26.3 us  [exchange(): lax.all_to_all(pieces, AXES, 0, 0, axis_index_groups=groups, tiled=True)]
    ppermute x6 -> x15, waiting for transfers between devices: 0.53 us -> 13.5 us  [moved(): return lax.ppermute(shard, AXES, pairs)]
    all_to_all x2 -> x1, blocking collectives: 28.5 us -> 18.3 us  [exchange(): lax.all_to_all(pieces, AXES, 0, 0, axis_index_groups=groups, tiled=True)]
    all_to_all x4 -> x2, starting transfers between devices: 21.4 us -> 17.2 us  [exchange(): lax.all_to_all(pieces, AXES, 0, 0, axis_index_groups=groups, tiled=True)]
    slice x3 -> x9, local copies, waits for them, and re-layouts: 1.35 us -> 5.48 us  [the longest x2 1.73 us: per_device(): top = jnp.concatenate([near[:, :width], near_before[:, :width]], axis=0)]
    ppermute x5 -> x4, starting transfers between devices: 26.9 us -> 23 us  [from_twin(): return lax.ppermute(shard, AXES, TWIN)]
    dot_general x2 -> x1, matrix products: 3.77 us -> 1.27 us  [per_device(): lax.dot_general(one_hot(row_order(x, y, core), 1152), grad_projected, (((...]
  transfers between devices with their start and end apart: 15 -> 21, of which waited for: 8 -> 10; matrix products, arithmetic and copies ran while one was open for 5% -> 5% of each run, Pallas kernels for 3% -> 3%
where the time goes in v2:
time: 180 us; the launch traced here: 179 us
  starting transfers between devices  85.5 us (48%)
  waiting for transfers between devices  43.9 us (24%)
  blocking collectives  18.3 us (10%)
  local copies, waits for them, and re-layouts  12.6 us (7%)
  Pallas kernels  9.66 us (5%)
  other arithmetic  4.07 us (2%)
  matrix products  3.71 us (2%)
    ppermute x15, starting transfers between devices, moved(): return lax.ppermute(shard, AXES, pairs)  45.3 us
    all_to_all x2, waiting for transfers between devices, exchange(): lax.all_to_all(pieces, AXES, 0, 0, axis_index_groups=groups, tiled=True)  26.3 us
    ppermute x4, starting transfers between devices, from_twin(): return lax.ppermute(shard, AXES, TWIN)  23 us
    all_to_all x1, blocking collectives, exchange(): lax.all_to_all(pieces, AXES, 0, 0, axis_index_groups=groups, tiled=True)  18.3 us
    all_to_all x2, starting transfers between devices, exchange(): lax.all_to_all(pieces, AXES, 0, 0, axis_index_groups=groups, tiled=True)  17.2 us
    ppermute x15, waiting for transfers between devices, moved(): return lax.ppermute(shard, AXES, pairs)  13.5 us
    pallas_call x3, Pallas kernels, pair_sums(): pl.pallas_call(functools.partial(pair_kernel, len(texts), bool(carried)),...  7.02 us
    ppermute x4, waiting for transfers between devices, from_twin(): return lax.ppermute(shard, AXES, TWIN)  4.16 us
  transfers between devices with their start and end apart: 21, of which 10 were waited for; matrix products, arithmetic and copies ran while one was open for 5% of the time, Pallas kernels for 3%

profile of v2, /device:TPU:1, one launch (start us, length us, event | category | flops | bytes accessed | tf_op | source)
XLA Modules:
  0.0 179.2 jit_solution(18056281824765686704)
XLA Ops:
  4.6 5.4 %collective-permute-start.4 = (bf16[128,1920]{1,0:T(8,128)(2,1)S(1)}, bf16[128,1920]{1,0:T(8,128)(2,1)S(1)}, u32[]{:S(2)}, u32[]{:S(2)}) collective-permute-start(bf16[128,1920]{1,0:T(8,128)(2,1)S(1)} %get-tuple-element.13.refs_4_), channel_id=1, source_target_pairs={{0,80},{1,81},{2,82},{3,83},{4,84},{5,85},{6,86},{7,87},{8,88},{9,... | collective-permute-start | bytes 1474568 | tf_op jit(solution)/shard_map/ppermute | solution.py:65
  10.0 2.3 %collective-permute-start.5 = (bf16[128,1920]{1,0:T(8,128)(2,1)S(1)}, bf16[128,1920]{1,0:T(8,128)(2,1)S(1)}, u32[]{:S(2)}, u32[]{:S(2)}) collective-permute-start(bf16[128,1920]{1,0:T(8,128)(2,1)S(1)} %get-tuple-element.13.refs_4_), channel_id=1, source_target_pairs={{0,64},{1,65},{2,66},{3,67},{4,68},{5,69},{6,70},{7,71},{8,72},{9,... | collective-permute-start | bytes 1474568 | tf_op jit(solution)/shard_map/ppermute | solution.py:65
  12.3 2.6 %collective-permute-start.1 = (bf16[128,1920]{1,0:T(8,128)(2,1)S(1)}, bf16[128,1920]{1,0:T(8,128)(2,1)}, u32[]{:S(2)}, u32[]{:S(2)}) collective-permute-start(bf16[128,1920]{1,0:T(8,128)(2,1)S(1)} %get-tuple-element.13.refs_4_), channel_id=1, source_target_pairs={{0,16},{1,17},{2,18},{3,19},{4,20},{5,21},{6,22},{7,23},{8,24},{9,... | collective-permute-start | bytes 1474568 | tf_op jit(solution)/shard_map/ppermute | solution.py:65
  14.9 6.2 %collective-permute-start = (bf16[128,1920]{1,0:T(8,128)(2,1)}, bf16[128,1920]{1,0:T(8,128)(2,1)}, u32[]{:S(2)}, u32[]{:S(2)}) collective-permute-start(bf16[128,1920]{1,0:T(8,128)(2,1)} %get-tuple-element.12), channel_id=1, source_target_pairs={{0,32},{1,33},{2,34},{3,35},{4,36},{5,37},{6,38},{7,39},{8,40},{9,... | collective-permute-start | bytes 1474568 | tf_op jit(solution)/shard_map/ppermute | solution.py:77
  25.6 4.4 %collective-permute-start.6 = (bf16[256,1152]{1,0:T(8,128)(2,1)S(1)}, bf16[256,1152]{1,0:T(8,128)(2,1)S(1)}, u32[]{:S(2)}, u32[]{:S(2)}) collective-permute-start(bf16[256,1152]{1,0:T(8,128)(2,1)S(1)} %pad_maximum_fusion.4.refs_4_), channel_id=1, source_target_pairs={{0,384},{1,385},{2,386},{3,387},{4,388},{5,389},{6,390},{7,391},{8... | collective-permute-start | bytes 1769480 | tf_op jit(solution)/shard_map/ppermute | solution.py:65
  33.1 3.0 %collective-permute-start.9 = (bf16[256,1152]{1,0:T(8,128)(2,1)S(1)}, bf16[256,1152]{1,0:T(8,128)(2,1)S(1)}, u32[]{:S(2)}, u32[]{:S(2)}) collective-permute-start(bf16[256,1152]{1,0:T(8,128)(2,1)S(1)} %pad_maximum_fusion.4.refs_4_), channel_id=1, source_target_pairs={{0,128},{1,129},{2,130},{3,131},{4,132},{5,133},{6,134},{7,135},{8... | collective-permute-start | bytes 1769480 | tf_op jit(solution)/shard_map/ppermute | solution.py:65
  36.1 3.5 %collective-permute-start.8 = (bf16[256,1152]{1,0:T(8,128)(2,1)S(1)}, bf16[256,1152]{1,0:T(8,128)(2,1)S(1)}, u32[]{:S(2)}, u32[]{:S(2)}) collective-permute-start(bf16[256,1152]{1,0:T(8,128)(2,1)S(1)} %pad_maximum_fusion.3.refs_3_), channel_id=1, source_target_pairs={{0,384},{1,385},{2,386},{3,387},{4,388},{5,389},{6,390},{7,391},{8... | collective-permute-start | bytes 1769480 | tf_op jit(solution)/shard_map/ppermute | solution.py:65
  41.4 3.4 %collective-permute-start.7 = (bf16[256,1152]{1,0:T(8,128)(2,1)S(1)}, bf16[256,1152]{1,0:T(8,128)(2,1)S(1)}, u32[]{:S(2)}, u32[]{:S(2)}) collective-permute-start(bf16[256,1152]{1,0:T(8,128)(2,1)S(1)} %collective-permute-done.6.refs_5_), channel_id=1, source_target_pairs={{0,384},{1,385},{2,386},{3,387},{4,388},{5,389},{6,390},{7,391},{8... | collective-permute-start | bytes 1769480 | tf_op jit(solution)/shard_map/ppermute | solution.py:65
  49.8 3.4 %shard_map.104 = (f32[256,1152]{1,0:T(8,128)S(1)}, f32[256,1]{1,0:T(8,128)S(1)}) custom-call(bf16[256,1152]{1,0:T(8,128)(2,1)S(1)} %get-tuple-element.22.refs_0_, bf16[256,1152]{1,0:T(8,128)(2,1)S(1)} %pad_maximum_fusion.2.refs_1_, s32[256,1]{1,0:T(8,128)S(1)} %copy.15.refs_2_, bf16[256,1152]{1,0:T(8,128)(2,1)S(1)} %collective-permute-done.2.refs_3_, ...), custom_call_target="tpu_custom_call" | custom-call | flops 1811939328 | bytes 2359296 | tf_op jit(solution)/shard_map/pallas_call | solution.py:179
  53.4 3.5 %collective-permute-done.3.refs_3_ = bf16[256,1152]{1,0:T(8,128)(2,1)S(1)} collective-permute-done((bf16[256,1152]{1,0:T(8,128)(2,1)S(1)}, bf16[256,1152]{1,0:T(8,128)(2,1)S(1)}, u32[]{:S(2)}, u32[]{:S(2)}) %collective-permute-start.3) | collective-permute-done | bytes 589856 | tf_op jit(solution)/shard_map/ppermute | solution.py:65
  58.8 4.7 %collective-permute-start.10 = (f32[128,1152]{1,0:T(8,128)S(1)}, f32[128,1152]{1,0:T(8,128)S(1)}, u32[]{:S(2)}, u32[]{:S(2)}) collective-permute-start(f32[128,1152]{1,0:T(8,128)S(1)} %slice.179), channel_id=1, source_target_pairs={{0,32},{1,33},{2,34},{3,35},{4,36},{5,37},{6,38},{7,39},{8,40},{9,... | collective-permute-start | bytes 1769480 | tf_op jit(solution)/shard_map/ppermute | solution.py:77
  68.6 4.6 %collective-permute-start.12 = (bf16[320,128]{1,0:T(8,128)(2,1)S(1)}, bf16[320,128]{1,0:T(8,128)(2,1)S(1)}, u32[]{:S(2)}, u32[]{:S(2)}) collective-permute-start(bf16[320,128]{1,0:T(8,128)(2,1)S(1)} %get-tuple-element.37), channel_id=1, source_target_pairs={{0,80},{1,81},{2,82},{3,83},{4,84},{5,85},{6,86},{7,87},{8,88},{9,... | collective-permute-start | bytes 245768 | tf_op jit(solution)/shard_map/ppermute | solution.py:65
  75.1 4.7 %collective-permute-done.13.refs_3_ = bf16[320,128]{1,0:T(8,128)(2,1)S(1)} collective-permute-done((bf16[320,128]{1,0:T(8,128)(2,1)S(1)}, bf16[320,128]{1,0:T(8,128)(2,1)S(1)}, u32[]{:S(2)}, u32[]{:S(2)}) %collective-permute-start.13) | collective-permute-done | bytes 81952 | tf_op jit(solution)/shard_map/ppermute | solution.py:65
  83.5 4.4 %collective-permute-start.15 = (f32[80,768]{1,0:T(8,128)S(1)}, f32[80,768]{1,0:T(8,128)S(1)}, u32[]{:S(2)}, u32[]{:S(2)}) collective-permute-start(f32[80,768]{1,0:T(8,128)S(1)} %get-tuple-element.29), channel_id=1, source_target_pairs={{0,256},{1,257},{2,258},{3,259},{4,260},{5,261},{6,262},{7,263},{8... | collective-permute-start | bytes 737288 | tf_op jit(solution)/shard_map/ppermute | solution.py:65
  87.9 2.1 %collective-permute-start.16 = (f32[80,768]{1,0:T(8,128)S(1)}, f32[80,768]{1,0:T(8,128)S(1)}, u32[]{:S(2)}, u32[]{:S(2)}) collective-permute-start(f32[80,768]{1,0:T(8,128)S(1)} %get-tuple-element.28), channel_id=1, source_target_pairs={{0,384},{1,385},{2,386},{3,387},{4,388},{5,389},{6,390},{7,391},{8... | collective-permute-start | bytes 737288 | tf_op jit(solution)/shard_map/ppermute | solution.py:65
  90.2 2.5 %collective-permute-done.14 = f32[80,768]{1,0:T(8,128)S(1)} collective-permute-done((f32[80,768]{1,0:T(8,128)S(1)}, f32[80,768]{1,0:T(8,128)S(1)}, u32[]{:S(2)}, u32[]{:S(2)}) %collective-permute-start.14) | collective-permute-done | bytes 245792 | tf_op jit(solution)/shard_map/ppermute | solution.py:65
  92.7 2.5 %collective-permute-done.16 = f32[80,768]{1,0:T(8,128)S(1)} collective-permute-done((f32[80,768]{1,0:T(8,128)S(1)}, f32[80,768]{1,0:T(8,128)S(1)}, u32[]{:S(2)}, u32[]{:S(2)}) %collective-permute-start.16) | collective-permute-done | bytes 245792 | tf_op jit(solution)/shard_map/ppermute | solution.py:65
  95.3 5.1 %collective-permute-start.17 = (f32[88,384]{1,0:T(8,128)S(1)}, f32[88,384]{1,0:T(8,128)S(1)}, u32[]{:S(2)}, u32[]{:S(2)}) collective-permute-start(f32[88,384]{1,0:T(8,128)S(1)} %select_maximum_fusion), channel_id=1, source_target_pairs={{0,32},{1,33},{2,34},{3,35},{4,36},{5,37},{6,38},{7,39},{8,40},{9,... | collective-permute-start | bytes 405512 | tf_op jit(solution)/shard_map/ppermute | solution.py:77
  102.1 12.3 %all-to-all-start = ((f32[16,16,128]{2,1,0:T(8,128)}), f32[16,16,128]{2,1,0:T(8,128)S(1)}, u32[]{:S(2)}, u32[]{:S(2)}) async-start(f32[16,16,128]{2,1,0:T(8,128)} %pad.22), calls=%async_computation | async-start | bytes 262144 | tf_op jit(solution)/shard_map/all_to_all | solution.py:69
  114.5 12.0 %all-to-all-done = f32[16,16,128]{2,1,0:T(8,128)S(1)} async-done(((f32[16,16,128]{2,1,0:T(8,128)}), f32[16,16,128]{2,1,0:T(8,128)S(1)}, u32[]{:S(2)}, u32[]{:S(2)}) %all-to-all-start) | async-done | bytes 131104 | tf_op jit(solution)/shard_map/all_to_all | solution.py:69
  126.7 18.3 %all_to_all.15 = bf16[16,5,384]{2,1,0:T(8,128)(2,1)S(1)} all-to-all(bf16[16,5,384]{2,1,0:T(8,128)(2,1)S(1)} %broadcast_in_dim.8), channel_id=1, replica_groups={{0,1,2,3,4,5,6,7,8,9,10,11,12,13,14,15},{32,33,34,35,36,37,38,39,40,41,..., dimensions={0} | all-to-all | bytes 122880 | tf_op jit(solution)/shard_map/all_to_all | solution.py:69
  146.4 4.9 %all-to-all-start.2 = ((bf16[16,96,384]{2,1,0:T(8,128)(2,1)}), bf16[16,96,384]{2,1,0:T(8,128)(2,1)S(1)}, u32[]{:S(2)}, u32[]{:S(2)}) async-start(bf16[16,96,384]{2,1,0:T(8,128)(2,1)} %broadcast_in_dim.10), calls=%async_computation.2 | async-start | bytes 2359296 | tf_op jit(solution)/shard_map/all_to_all | solution.py:69
  151.3 14.3 %all-to-all-done.2 = bf16[16,96,384]{2,1,0:T(8,128)(2,1)S(1)} async-done(((bf16[16,96,384]{2,1,0:T(8,128)(2,1)}), bf16[16,96,384]{2,1,0:T(8,128)(2,1)S(1)}, u32[]{:S(2)}, u32[]{:S(2)}) %all-to-all-start.2) | async-done | bytes 1179680 | tf_op jit(solution)/shard_map/all_to_all | solution.py:69
  167.5 7.0 %collective-permute-start.18 = (bf16[1272,384]{1,0:T(8,128)(2,1)S(1)}, bf16[1272,384]{1,0:T(8,128)(2,1)S(1)}, u32[]{:S(2)}, u32[]{:S(2)}) collective-permute-start(bf16[1272,384]{1,0:T(8,128)(2,1)S(1)} %pad_maximum_fusion.1), channel_id=1, source_target_pairs={{0,32},{1,33},{2,34},{3,35},{4,36},{5,37},{6,38},{7,39},{8,40},{9,... | collective-permute-start | bytes 2930696 | tf_op jit(solution)/shard_map/ppermute | solution.py:77
  (104 shorter events, 40.6 us)
Async XLA Ops:
  0.6 39.9 %copy-start = (bf16[1152,768]{1,0:T(8,128)(2,1)S(1)}, bf16[1152,768]{1,0:T(8,128)(2,1)}, u32[]{:S(2)}) copy-start(bf16[1152,768]{1,0:T(8,128)(2,1)} %param.11) | copy-start | bytes 5308420
  4.6 20.9 %collective-permute-start.4 = (bf16[128,1920]{1,0:T(8,128)(2,1)S(1)}, bf16[128,1920]{1,0:T(8,128)(2,1)S(1)}, u32[]{:S(2)}, u32[]{:S(2)}) collective-permute-start(bf16[128,1920]{1,0:T(8,128)(2,1)S(1)} %get-tuple-element.13.refs_4_), channel_id=1, source_target_pairs={{0,80},{1,81},{2,82},{3,83},{4,84},{5,85},{6,86},{7,87},{8,88},{9,... | collective-permute-start | bytes 1474568 | tf_op jit(solution)/shard_map/ppermute | solution.py:65
  10.0 15.5 %collective-permute-start.5 = (bf16[128,1920]{1,0:T(8,128)(2,1)S(1)}, bf16[128,1920]{1,0:T(8,128)(2,1)S(1)}, u32[]{:S(2)}, u32[]{:S(2)}) collective-permute-start(bf16[128,1920]{1,0:T(8,128)(2,1)S(1)} %get-tuple-element.13.refs_4_), channel_id=1, source_target_pairs={{0,64},{1,65},{2,66},{3,67},{4,68},{5,69},{6,70},{7,71},{8,72},{9,... | collective-permute-start | bytes 1474568 | tf_op jit(solution)/shard_map/ppermute | solution.py:65
  12.3 17.8 %collective-permute-start.1 = (bf16[128,1920]{1,0:T(8,128)(2,1)S(1)}, bf16[128,1920]{1,0:T(8,128)(2,1)}, u32[]{:S(2)}, u32[]{:S(2)}) collective-permute-start(bf16[128,1920]{1,0:T(8,128)(2,1)S(1)} %get-tuple-element.13.refs_4_), channel_id=1, source_target_pairs={{0,16},{1,17},{2,18},{3,19},{4,20},{5,21},{6,22},{7,23},{8,24},{9,... | collective-permute-start | bytes 1474568 | tf_op jit(solution)/shard_map/ppermute | solution.py:65
  14.9 24.7 %collective-permute-start = (bf16[128,1920]{1,0:T(8,128)(2,1)}, bf16[128,1920]{1,0:T(8,128)(2,1)}, u32[]{:S(2)}, u32[]{:S(2)}) collective-permute-start(bf16[128,1920]{1,0:T(8,128)(2,1)} %get-tuple-element.12), channel_id=1, source_target_pairs={{0,32},{1,33},{2,34},{3,35},{4,36},{5,37},{6,38},{7,39},{8,40},{9,... | collective-permute-start | bytes 1474568 | tf_op jit(solution)/shard_map/ppermute | solution.py:77
  25.6 15.8 %collective-permute-start.6 = (bf16[256,1152]{1,0:T(8,128)(2,1)S(1)}, bf16[256,1152]{1,0:T(8,128)(2,1)S(1)}, u32[]{:S(2)}, u32[]{:S(2)}) collective-permute-start(bf16[256,1152]{1,0:T(8,128)(2,1)S(1)} %pad_maximum_fusion.4.refs_4_), channel_id=1, source_target_pairs={{0,384},{1,385},{2,386},{3,387},{4,388},{5,389},{6,390},{7,391},{8... | collective-permute-start | bytes 1769480 | tf_op jit(solution)/shard_map/ppermute | solution.py:65
  31.1 13.6 %collective-permute-start.2 = (bf16[256,1152]{1,0:T(8,128)(2,1)S(1)}, bf16[256,1152]{1,0:T(8,128)(2,1)S(1)}, u32[]{:S(2)}, u32[]{:S(2)}) collective-permute-start(bf16[256,1152]{1,0:T(8,128)(2,1)S(1)} %pad_maximum_fusion.3.refs_3_), channel_id=1, source_target_pairs={{0,128},{1,129},{2,130},{3,131},{4,132},{5,133},{6,134},{7,135},{8... | collective-permute-start | bytes 1769480 | tf_op jit(solution)/shard_map/ppermute | solution.py:65
  33.1 16.7 %collective-permute-start.9 = (bf16[256,1152]{1,0:T(8,128)(2,1)S(1)}, bf16[256,1152]{1,0:T(8,128)(2,1)S(1)}, u32[]{:S(2)}, u32[]{:S(2)}) collective-permute-start(bf16[256,1152]{1,0:T(8,128)(2,1)S(1)} %pad_maximum_fusion.4.refs_4_), channel_id=1, source_target_pairs={{0,128},{1,129},{2,130},{3,131},{4,132},{5,133},{6,134},{7,135},{8... | collective-permute-start | bytes 1769480 | tf_op jit(solution)/shard_map/ppermute | solution.py:65
  36.1 13.7 %collective-permute-start.8 = (bf16[256,1152]{1,0:T(8,128)(2,1)S(1)}, bf16[256,1152]{1,0:T(8,128)(2,1)S(1)}, u32[]{:S(2)}, u32[]{:S(2)}) collective-permute-start(bf16[256,1152]{1,0:T(8,128)(2,1)S(1)} %pad_maximum_fusion.3.refs_3_), channel_id=1, source_target_pairs={{0,384},{1,385},{2,386},{3,387},{4,388},{5,389},{6,390},{7,391},{8... | collective-permute-start | bytes 1769480 | tf_op jit(solution)/shard_map/ppermute | solution.py:65
  41.4 12.0 %collective-permute-start.7 = (bf16[256,1152]{1,0:T(8,128)(2,1)S(1)}, bf16[256,1152]{1,0:T(8,128)(2,1)S(1)}, u32[]{:S(2)}, u32[]{:S(2)}) collective-permute-start(bf16[256,1152]{1,0:T(8,128)(2,1)S(1)} %collective-permute-done.6.refs_5_), channel_id=1, source_target_pairs={{0,384},{1,385},{2,386},{3,387},{4,388},{5,389},{6,390},{7,391},{8... | collective-permute-start | bytes 1769480 | tf_op jit(solution)/shard_map/ppermute | solution.py:65
  44.8 12.1 %collective-permute-start.3 = (bf16[256,1152]{1,0:T(8,128)(2,1)S(1)}, bf16[256,1152]{1,0:T(8,128)(2,1)S(1)}, u32[]{:S(2)}, u32[]{:S(2)}) collective-permute-start(bf16[256,1152]{1,0:T(8,128)(2,1)S(1)} %collective-permute-done.2.refs_3_), channel_id=1, source_target_pairs={{0,128},{1,129},{2,130},{3,131},{4,132},{5,133},{6,134},{7,135},{8... | collective-permute-start | bytes 1769480 | tf_op jit(solution)/shard_map/ppermute | solution.py:65
  58.8 6.3 %collective-permute-start.10 = (f32[128,1152]{1,0:T(8,128)S(1)}, f32[128,1152]{1,0:T(8,128)S(1)}, u32[]{:S(2)}, u32[]{:S(2)}) collective-permute-start(f32[128,1152]{1,0:T(8,128)S(1)} %slice.179), channel_id=1, source_target_pairs={{0,32},{1,33},{2,34},{3,35},{4,36},{5,37},{6,38},{7,39},{8,40},{9,... | collective-permute-start | bytes 1769480 | tf_op jit(solution)/shard_map/ppermute | solution.py:77
  66.6 8.4 %collective-permute-start.11 = (bf16[320,128]{1,0:T(8,128)(2,1)S(1)}, bf16[320,128]{1,0:T(8,128)(2,1)S(1)}, u32[]{:S(2)}, u32[]{:S(2)}) collective-permute-start(bf16[320,128]{1,0:T(8,128)(2,1)S(1)} %get-tuple-element.38), channel_id=1, source_target_pairs={{0,16},{1,17},{2,18},{3,19},{4,20},{5,21},{6,22},{7,23},{8,24},{9,... | collective-permute-start | bytes 245768 | tf_op jit(solution)/shard_map/ppermute | solution.py:65
  68.6 6.5 %collective-permute-start.12 = (bf16[320,128]{1,0:T(8,128)(2,1)S(1)}, bf16[320,128]{1,0:T(8,128)(2,1)S(1)}, u32[]{:S(2)}, u32[]{:S(2)}) collective-permute-start(bf16[320,128]{1,0:T(8,128)(2,1)S(1)} %get-tuple-element.37), channel_id=1, source_target_pairs={{0,80},{1,81},{2,82},{3,83},{4,84},{5,85},{6,86},{7,87},{8,88},{9,... | collective-permute-start | bytes 245768 | tf_op jit(solution)/shard_map/ppermute | solution.py:65
  73.1 6.7 %collective-permute-start.13 = (bf16[320,128]{1,0:T(8,128)(2,1)S(1)}, bf16[320,128]{1,0:T(8,128)(2,1)S(1)}, u32[]{:S(2)}, u32[]{:S(2)}) collective-permute-start(bf16[320,128]{1,0:T(8,128)(2,1)S(1)} %get-tuple-element.36), channel_id=1, source_target_pairs={{0,64},{1,65},{2,66},{3,67},{4,68},{5,69},{6,70},{7,71},{8,72},{9,... | collective-permute-start | bytes 245768 | tf_op jit(solution)/shard_map/ppermute | solution.py:65
  81.6 11.1 %collective-permute-start.14 = (f32[80,768]{1,0:T(8,128)S(1)}, f32[80,768]{1,0:T(8,128)S(1)}, u32[]{:S(2)}, u32[]{:S(2)}) collective-permute-start(f32[80,768]{1,0:T(8,128)S(1)} %get-tuple-element.30), channel_id=1, source_target_pairs={{0,128},{1,129},{2,130},{3,131},{4,132},{5,133},{6,134},{7,135},{8... | collective-permute-start | bytes 737288 | tf_op jit(solution)/shard_map/ppermute | solution.py:65
  83.5 9.2 %collective-permute-start.15 = (f32[80,768]{1,0:T(8,128)S(1)}, f32[80,768]{1,0:T(8,128)S(1)}, u32[]{:S(2)}, u32[]{:S(2)}) collective-permute-start(f32[80,768]{1,0:T(8,128)S(1)} %get-tuple-element.29), channel_id=1, source_target_pairs={{0,256},{1,257},{2,258},{3,259},{4,260},{5,261},{6,262},{7,263},{8... | collective-permute-start | bytes 737288 | tf_op jit(solution)/shard_map/ppermute | solution.py:65
  87.9 7.2 %collective-permute-start.16 = (f32[80,768]{1,0:T(8,128)S(1)}, f32[80,768]{1,0:T(8,128)S(1)}, u32[]{:S(2)}, u32[]{:S(2)}) collective-permute-start(f32[80,768]{1,0:T(8,128)S(1)} %get-tuple-element.28), channel_id=1, source_target_pairs={{0,384},{1,385},{2,386},{3,387},{4,388},{5,389},{6,390},{7,391},{8... | collective-permute-start | bytes 737288 | tf_op jit(solution)/shard_map/ppermute | solution.py:65
  90.1 36.4 %copy-start.7 = (f32[36,768]{1,0:T(8,128)S(1)}, f32[36,768]{1,0:T(8,128)}, u32[]{:S(2)}) copy-start(f32[36,768]{1,0:T(8,128)} %param.13) | copy-start | bytes 331780
  90.2 36.4 %copy-start.8 = (f32[36,768]{1,0:T(8,128)S(1)}, f32[36,768]{1,0:T(8,128)}, u32[]{:S(2)}) copy-start(f32[36,768]{1,0:T(8,128)} %param.12) | copy-start | bytes 331780
  95.3 6.1 %collective-permute-start.17 = (f32[88,384]{1,0:T(8,128)S(1)}, f32[88,384]{1,0:T(8,128)S(1)}, u32[]{:S(2)}, u32[]{:S(2)}) collective-permute-start(f32[88,384]{1,0:T(8,128)S(1)} %select_maximum_fusion), channel_id=1, source_target_pairs={{0,32},{1,33},{2,34},{3,35},{4,36},{5,37},{6,38},{7,39},{8,40},{9,... | collective-permute-start | bytes 405512 | tf_op jit(solution)/shard_map/ppermute | solution.py:77
  102.1 24.4 %all-to-all-start = ((f32[16,16,128]{2,1,0:T(8,128)}), f32[16,16,128]{2,1,0:T(8,128)S(1)}, u32[]{:S(2)}, u32[]{:S(2)}) async-start(f32[16,16,128]{2,1,0:T(8,128)} %pad.22), calls=%async_computation | async-start | bytes 262144 | tf_op jit(solution)/shard_map/all_to_all | solution.py:69
  146.4 19.2 %all-to-all-start.2 = ((bf16[16,96,384]{2,1,0:T(8,128)(2,1)}), bf16[16,96,384]{2,1,0:T(8,128)(2,1)S(1)}, u32[]{:S(2)}, u32[]{:S(2)}) async-start(bf16[16,96,384]{2,1,0:T(8,128)(2,1)} %broadcast_in_dim.10), calls=%async_computation.2 | async-start | bytes 2359296 | tf_op jit(solution)/shard_map/all_to_all | solution.py:69
  167.5 9.1 %collective-permute-start.18 = (bf16[1272,384]{1,0:T(8,128)(2,1)S(1)}, bf16[1272,384]{1,0:T(8,128)(2,1)S(1)}, u32[]{:S(2)}, u32[]{:S(2)}) collective-permute-start(bf16[1272,384]{1,0:T(8,128)(2,1)S(1)} %pad_maximum_fusion.1), channel_id=1, source_target_pairs={{0,32},{1,33},{2,34},{3,35},{4,36},{5,37},{6,38},{7,39},{8,40},{9,... | collective-permute-start | bytes 2930696 | tf_op jit(solution)/shard_map/ppermute | solution.py:77
  (8 other events, 48.7 us)

commit v3 on v1

--- a/solution.py
+++ b/solution.py
@@ -96,28 +96,81 @@
     return values * lax.rsqrt(jnp.sum(values * values, axis=-1, keepdims=True) + norm_eps)
 
 
-def copies_kernel(values_ref, others_ref, out_ref):
-    width = values_ref.shape[1]
-    rows = unit_rows(values_ref[...]).astype(jnp.bfloat16)
-    for i in range(out_ref.shape[0]):
-        out_ref[i, :, :width] = rows
-        out_ref[i, :, width:] = others_ref[...]
+def copies_kernel(texts_ref, features_ref, out_ref, texts, packed, sems):
+    width = texts_ref.shape[1]
+    take_texts = pltpu.make_async_copy(texts_ref, texts, sems.at[0])
+    take_features = pltpu.make_async_copy(features_ref, packed.at[:, width:], sems.at[1])
+    take_texts.start()
+    take_features.start()
+    take_texts.wait()
+    packed[:, :width] = unit_rows(texts[...]).astype(jnp.bfloat16)
+    take_features.wait()
+    puts = [
+        pltpu.make_async_copy(packed, out_ref.at[i], sems.at[2 + i])
+        for i in range(out_ref.shape[0])
+    ]
+    for put in puts:
+        put.start()
+    for put in puts:
+        put.wait()
 
 
 def unit_copies(values, others, count):
-    width = values.shape[1] + others.shape[1]
+    rows, width = values.shape[0], values.shape[1] + others.shape[1]
     return pl.pallas_call(
         copies_kernel,
-        out_shape=jax.ShapeDtypeStruct((count, values.shape[0], width), jnp.bfloat16),
-        in_specs=[pl.BlockSpec(memory_space=pltpu.VMEM)] * 2,
-        out_specs=pl.BlockSpec(memory_space=pltpu.VMEM),
+        out_shape=jax.ShapeDtypeStruct((count, rows, width), jnp.bfloat16),
+        in_specs=[pl.BlockSpec(memory_space=pl.ANY)] * 2,
+        out_specs=pl.BlockSpec(memory_space=pl.ANY),
+        scratch_shapes=[
+            pltpu.VMEM(values.shape, jnp.bfloat16),
+            pltpu.VMEM((rows, width), jnp.bfloat16),
+            pltpu.SemaphoreType.DMA((2 + count,)),
+        ],
         compiler_params=pltpu.CompilerParams(vmem_limit_bytes=8 << 20),
         cost_estimate=pl.CostEstimate(
-            flops=4 * values.size,
-            bytes_accessed=2 * values.size + 2 * count * values.shape[0] * width,
-            transcendentals=0,
+            flops=4 * values.size, bytes_accessed=2 * (count + 1) * rows * width, transcendentals=0
         ),
     )(values, others)
+
+
+def last_kernel(core_ref, half_ref, twin_ref, first_ref, second_ref, *outs):
+    weights_ref, new_first_ref, new_second_ref = outs
+
+    def put(left, right):
+        weights_ref[:, :384] = left[:1152, :]
+        weights_ref[:, 384:] = right[:1152, :]
+        for side, ref in enumerate((left, right)):
+            columns = slice(side * 384, side * 384 + 384)
+            high, middle, low = (
+                ref[1152 + i * 48 : 1200 + i * 48, :].astype(jnp.float32) for i in range(3)
+            )
+            grad = ((high + middle) + low)[:36]
+            new_first_ref[:, columns] = beta_one * first_ref[:, columns] + (1.0 - beta_one) * grad
+            new_second_ref[:, columns] = (
+                beta_two * second_ref[:, columns] + (1.0 - beta_two) * grad * grad
+            )
+
+    @pl.when(core_ref[0] == 0)
+    def _():
+        put(half_ref, twin_ref)
+
+    @pl.when(core_ref[0] != 0)
+    def _():
+        put(twin_ref, half_ref)
+
+
+def last_outputs(core, half, twin_half, moment_first, moment_second):
+    whole = pl.BlockSpec(memory_space=pltpu.VMEM)
+    moment = jax.ShapeDtypeStruct(moment_first.shape, jnp.float32)
+    return pl.pallas_call(
+        last_kernel,
+        out_shape=(jax.ShapeDtypeStruct((1152, 768), jnp.bfloat16), moment, moment),
+        in_specs=[pl.BlockSpec(memory_space=pltpu.SMEM)] + [whole] * 4,
+        out_specs=(whole,) * 3,
+        compiler_params=pltpu.CompilerParams(vmem_limit_bytes=12 << 20),
+        cost_estimate=pl.CostEstimate(flops=0, bytes_accessed=6 << 20, transcendentals=0),
+    )(core.reshape(1), half, twin_half, moment_first, moment_second)
 
 
 def pair_terms(student_rows, teacher_rows, left_ids, text_rows, right_ids):
@@ -201,9 +254,9 @@
 
 
 def grad_order():
-    part = lax.iota(jnp.int32, 120)
-    q = part % 40
-    return q // 5 * 96 + 80 + part // 40 * 5 + q % 5
+    part = lax.iota(jnp.int32, 144)
+    q = part % 48
+    return jnp.where(q < 40, q // 5 * 96 + 80 + part // 48 * 5 + q % 5, -1)
 
 
 def one_hot(index, width):
@@ -282,10 +335,25 @@
         (after_top, ids_at(1)[:2]),
     ]
     sums = pair_sums(*images, near_chunks, sums)
+    features, sums = lax.optimization_barrier((features, sums))
     pulled, losses = pair_sums(
         *images, [(far_top, ids_at(2)[:2]), (far_bottom, ids_at(2)[2:])], sums
     )
     losses = losses.reshape(-1)
+
+    def piece(values, start):
+        group_rows = lax.dynamic_slice_in_dim(values, start, 36, 0)
+        padded = jnp.pad(group_rows, ((0, 4), (0, 0)))
+        return lax.dynamic_slice(padded, ((xh * 4 + y) * 5, core * 384), (5, 384))
+
+    own_moments = (
+        piece(moment_first, 0),
+        piece(moment_second, 0),
+        piece(head_weights, group_index * 36),
+    )
+    order = row_order(core)
+    own_losses = losses[:rows]
+    other_losses = jnp.pad(losses[rows:].reshape(1, rows), ((0, 7), (0, 256)))
 
     pulled = pulled[:rows] + from_twin(pulled[rows:])
     student, inverse = student[:rows], inverse[:rows]
@@ -295,21 +363,23 @@
     ).astype(jnp.bfloat16)
 
     grad_rows = lax.dot_general(
-        one_hot(row_order(core), 1152),
+        one_hot(order, 1152),
         grad_projected,
         (((1,), (1,)), ((), ())),
         preferred_element_type=jnp.float32,
     ).astype(jnp.bfloat16)
+    grad_rows, own_moments, own_losses, other_losses = lax.optimization_barrier(
+        (grad_rows, own_moments, own_losses, other_losses)
+    )
     grad_rows = exchange(grad_rows.reshape(4, 320, rows), FIRST)
     line_grad = lax.dot_general(
         grad_rows, features, (((0, 2), (0, 1)), ((), ())), preferred_element_type=jnp.float32
     )
     core_grad = jnp.sum(exchange(line_grad.reshape(4, 80, 768), SECOND), axis=0)
     left, right = core_grad[:, :384], core_grad[:, 384:]
-    other_losses = jnp.pad(losses[rows:].reshape(1, rows), ((0, 7), (0, 256)))
     arrived = from_twin(jnp.concatenate([jnp.where(core == 0, right, left), other_losses], axis=0))
     chip_grad = jnp.where(core == 0, left, right) + arrived[:80]
-    row_loss = (losses[:rows] + arrived[80, :rows]) / rows
+    row_loss = (own_losses + arrived[80, :rows]) / rows
 
     column_grad = jnp.pad(chip_grad.reshape(16, 15, 128), ((0, 0), (0, 1), (0, 0)))
     own_grad = jnp.sum(exchange(column_grad, COLUMN), axis=0)[:15].reshape(5, 384)
@@ -325,17 +395,7 @@
         )
         return updated.astype(jnp.bfloat16)
 
-    def piece(values, start):
-        group_rows = lax.dynamic_slice_in_dim(values, start, 36, 0)
-        padded = jnp.pad(group_rows, ((0, 4), (0, 0)))
-        return lax.dynamic_slice(padded, ((xh * 4 + y) * 5, core * 384), (5, 384))
-
-    own_weights = adam(
-        own_grad,
-        piece(moment_first, 0),
-        piece(moment_second, 0),
-        piece(head_weights, group_index * 36),
-    )
+    own_weights = adam(own_grad, *own_moments)
     chip_weights = share(own_weights, COLUMN).reshape(80, 384)
     high = rounded(own_grad)
     middle = rounded(own_grad - high)
@@ -343,25 +403,21 @@
     spare = jnp.zeros((1, 384), jnp.float32)
     grad_parts = jnp.concatenate([high, middle, low, spare], axis=0).astype(jnp.bfloat16)
     plane = share(jnp.concatenate([chip_weights, grad_parts], axis=0), PLANE).reshape(2, 768, 384)
-    select_weights = one_hot(weight_order(), 768)
+    plane, same_xl = lax.optimization_barrier((plane, xl))
+    after = same_xl - xl
+    select_weights = one_hot(weight_order() + after, 768)
     halves = [
         jnp.dot(select_weights, plane[i], preferred_element_type=jnp.float32) for i in range(2)
     ]
     group_parts = jnp.dot(
-        one_hot(grad_order(), 768),
+        one_hot(grad_order() + after, 768),
         lax.dynamic_index_in_dim(plane, xl, 0, keepdims=False),
         preferred_element_type=jnp.float32,
     )
     half = jnp.concatenate([*halves, group_parts], axis=0).astype(jnp.bfloat16)
-    twin_half = from_twin(half)
-    whole = jnp.concatenate(
-        [jnp.where(core == 0, half, twin_half), jnp.where(core == 0, twin_half, half)], axis=1
-    )
-    new_weights = whole[:1152]
-    parts = whole[1152:].reshape(3, 40, 768).astype(jnp.float32)
-    head_grad = ((parts[0] + parts[1]) + parts[2])[:36]
-    new_first = beta_one * moment_first + (1.0 - beta_one) * head_grad
-    new_second = beta_two * moment_second + (1.0 - beta_two) * head_grad * head_grad
+    new_weights, new_first, new_second = last_outputs(
+        core, half, from_twin(half), moment_first, moment_second
+    )
     return (row_loss, new_first, new_second, new_weights)
 
 

time: 179 us -> 180 us (level)
  blocking collectives: 28.5 us -> 60.9 us
  waiting for transfers between devices: 51.2 us -> 29.5 us
  starting transfers between devices: 67.8 us -> 54.8 us
  Pallas kernels: 8.14 us -> 10.7 us
  local copies, waits for them, and re-layouts: 7.82 us -> 10.1 us
    all_to_all x2 -> x4, blocking collectives: 28.5 us -> 60.9 us  [exchange(): lax.all_to_all(pieces, AXES, 0, 0, axis_index_groups=groups, tiled=True)]
    all_to_all x4 -> x2, waiting for transfers between devices: 46.5 us -> 25.3 us  [exchange(): lax.all_to_all(pieces, AXES, 0, 0, axis_index_groups=groups, tiled=True)]
    all_to_all x4 -> x2, starting transfers between devices: 21.4 us -> 8.13 us  [exchange(): lax.all_to_all(pieces, AXES, 0, 0, axis_index_groups=groups, tiled=True)]
    pallas_call x1 -> x2, Pallas kernels: 1.19 us -> 3.8 us  [the longest x1 2.32 us: unit_copies(): pl.pallas_call(copies_kernel, out_shape=jax.ShapeDtypeStruct((count, rows...]
    dot_general x1, matrix products: 2.5 us -> 0.42 us  [per_device(): lax.dot_general(grad_rows, features, (((0, 2), (0, 1)), ((), ())), prefer...]
    slice x2 -> x1, local copies, waits for them, and re-layouts: 0.15 us -> 2.07 us  [per_device(): features = near[:, :, 1152:]]
  transfers between devices with their start and end apart: 15 -> 13, of which waited for: 8 -> 5; matrix products, arithmetic and copies ran while one was open for 5% -> 6% of each run, Pallas kernels for 3% -> 3%
where the time goes in v3:
time: 180 us; the launch traced here: 179 us
  blocking collectives  60.9 us (34%)
  starting transfers between devices  54.8 us (30%)
  waiting for transfers between devices  29.5 us (16%)
  Pallas kernels  10.7 us (6%)
  local copies, waits for them, and re-layouts  10.1 us (6%)
  matrix products  6.29 us (3%)
  other arithmetic  5.78 us (3%)
    all_to_all x4, blocking collectives, exchange(): lax.all_to_all(pieces, AXES, 0, 0, axis_index_groups=groups, tiled=True)  60.9 us
    ppermute x5, starting transfers between devices, from_twin(): return lax.ppermute(shard, AXES, TWIN)  27.2 us
    all_to_all x2, waiting for transfers between devices, exchange(): lax.all_to_all(pieces, AXES, 0, 0, axis_index_groups=groups, tiled=True)  25.3 us
    all_to_all x2, starting transfers between devices, exchange(): lax.all_to_all(pieces, AXES, 0, 0, axis_index_groups=groups, tiled=True)  8.13 us
    pallas_call x3, Pallas kernels, pair_sums(): pl.pallas_call(functools.partial(pair_kernel, len(texts), bool(carried)),...  6.94 us
    ppermute x1, starting transfers between devices, per_device(): after_bottom = lax.ppermute(bottom, AXES, BACK)  4.57 us
    ppermute x1, starting transfers between devices, per_device(): after_top = lax.ppermute(top, AXES, BACK)  4.57 us
    ppermute x1, starting transfers between devices, per_device(): far_bottom = lax.ppermute(after_bottom, AXES, BACK)  4.57 us
  transfers between devices with their start and end apart: 13, of which 5 were waited for; matrix products, arithmetic and copies ran while one was open for 6% of the time, Pallas kernels for 3%

profile of v3, /device:TPU:1, one launch (start us, length us, event | category | flops | bytes accessed | tf_op | source)
XLA Modules:
  0.0 179.3 jit_solution(13791413318485908030)
XLA Ops:
  1.7 2.3 %shard_map.102 = bf16[4,128,1920]{2,1,0:T(8,128)(2,1)S(1)} custom-call(bf16[128,1152]{1,0:T(8,128)(2,1)S(1)} %copy-done.4, bf16[128,768]{1,0:T(8,128)(2,1)} %features_ref.1), custom_call_target="tpu_custom_call" | custom-call | flops 589824 | bytes 2457600 | tf_op jit(solution)/shard_map/pallas_call | solution.py:120
  5.3 8.7 %collective-permute-start.1 = (bf16[128,1152]{1,0:T(8,128)(2,1)S(1)}, bf16[128,1152]{1,0:T(8,128)(2,1)}, u32[]{:S(2)}, u32[]{:S(2)}) collective-permute-start(bf16[128,1152]{1,0:T(8,128)(2,1)S(1)} %copy-done.7), channel_id=1, source_target_pairs={{0,32},{1,33},{2,34},{3,35},{4,36},{5,37},{6,38},{7,39},{8,40},{9,... | collective-permute-start | bytes 884744 | tf_op jit(solution)/shard_map/ppermute | solution.py:91
  14.1 1.9 %collective-permute-start = (bf16[128,768]{1,0:T(8,128)(2,1)}, bf16[128,768]{1,0:T(8,128)(2,1)}, u32[]{:S(2)}, u32[]{:S(2)}) collective-permute-start(bf16[128,768]{1,0:T(8,128)(2,1)} %features_ref.1), channel_id=1, source_target_pairs={{0,32},{1,33},{2,34},{3,35},{4,36},{5,37},{6,38},{7,39},{8,40},{9,... | collective-permute-start | bytes 589832 | tf_op jit(solution)/shard_map/ppermute | solution.py:91
  16.0 4.4 %all-to-all-start = ((bf16[4,128,1920]{2,1,0:T(8,128)(2,1)}), bf16[4,128,1920]{2,1,0:T(8,128)(2,1)}, u32[]{:S(2)}, u32[]{:S(2)}) async-start(bf16[4,128,1920]{2,1,0:T(8,128)(2,1)} %copy-done.1), calls=%async_computation | async-start | bytes 3932160 | tf_op jit(solution)/shard_map/all_to_all | solution.py:83
  24.2 11.0 %all-to-all-done = bf16[4,128,1920]{2,1,0:T(8,128)(2,1)} async-done(((bf16[4,128,1920]{2,1,0:T(8,128)(2,1)}), bf16[4,128,1920]{2,1,0:T(8,128)(2,1)}, u32[]{:S(2)}, u32[]{:S(2)}) %all-to-all-start) | async-done | bytes 1966112 | tf_op jit(solution)/shard_map/all_to_all | solution.py:83
  36.5 1.9 %collective-permute-start.2 = (bf16[256,1152]{1,0:T(8,128)(2,1)S(1)}, bf16[256,1152]{1,0:T(8,128)(2,1)S(1)}, u32[]{:S(2)}, u32[]{:S(2)}) collective-permute-start(bf16[256,1152]{1,0:T(8,128)(2,1)S(1)} %bitcast.51), channel_id=1, source_target_pairs={{0,128},{1,129},{2,130},{3,131},{4,132},{5,133},{6,134},{7,135},{8... | collective-permute-start | bytes 1769480 | tf_op jit(solution)/shard_map/ppermute | solution.py:292
  38.4 4.6 %collective-permute-start.4 = (bf16[256,1152]{1,0:T(8,128)(2,1)S(1)}, bf16[256,1152]{1,0:T(8,128)(2,1)S(1)}, u32[]{:S(2)}, u32[]{:S(2)}) collective-permute-start(bf16[256,1152]{1,0:T(8,128)(2,1)S(1)} %bitcast.54), channel_id=1, source_target_pairs={{0,384},{1,385},{2,386},{3,387},{4,388},{5,389},{6,390},{7,391},{8... | collective-permute-start | bytes 1769480 | tf_op jit(solution)/shard_map/ppermute | solution.py:293
  45.4 1.9 %collective-permute-start.6 = (bf16[256,1152]{1,0:T(8,128)(2,1)S(1)}, bf16[256,1152]{1,0:T(8,128)(2,1)S(1)}, u32[]{:S(2)}, u32[]{:S(2)}) collective-permute-start(bf16[256,1152]{1,0:T(8,128)(2,1)S(1)} %bitcast.55), channel_id=1, source_target_pairs={{0,128},{1,129},{2,130},{3,131},{4,132},{5,133},{6,134},{7,135},{8... | collective-permute-start | bytes 1769480 | tf_op jit(solution)/shard_map/ppermute | solution.py:294
  47.3 4.6 %collective-permute-start.7 = (bf16[256,1152]{1,0:T(8,128)(2,1)S(1)}, bf16[256,1152]{1,0:T(8,128)(2,1)S(1)}, u32[]{:S(2)}, u32[]{:S(2)}) collective-permute-start(bf16[256,1152]{1,0:T(8,128)(2,1)S(1)} %bitcast.52), channel_id=1, source_target_pairs={{0,384},{1,385},{2,386},{3,387},{4,388},{5,389},{6,390},{7,391},{8... | collective-permute-start | bytes 1769480 | tf_op jit(solution)/shard_map/ppermute | solution.py:295
  51.9 1.9 %collective-permute-start.3 = (bf16[256,1152]{1,0:T(8,128)(2,1)S(1)}, bf16[256,1152]{1,0:T(8,128)(2,1)S(1)}, u32[]{:S(2)}, u32[]{:S(2)}) collective-permute-start(bf16[256,1152]{1,0:T(8,128)(2,1)S(1)} %collective-permute-done.2.refs_3_), channel_id=1, source_target_pairs={{0,128},{1,129},{2,130},{3,131},{4,132},{5,133},{6,134},{7,135},{8... | collective-permute-start | bytes 1769480 | tf_op jit(solution)/shard_map/ppermute | solution.py:296
  53.8 4.6 %collective-permute-start.5 = (bf16[256,1152]{1,0:T(8,128)(2,1)S(1)}, bf16[256,1152]{1,0:T(8,128)(2,1)S(1)}, u32[]{:S(2)}, u32[]{:S(2)}) collective-permute-start(bf16[256,1152]{1,0:T(8,128)(2,1)S(1)} %collective-permute-done.4.refs_4_), channel_id=1, source_target_pairs={{0,384},{1,385},{2,386},{3,387},{4,388},{5,389},{6,390},{7,391},{8... | collective-permute-start | bytes 1769480 | tf_op jit(solution)/shard_map/ppermute | solution.py:297
  59.6 2.1 %slice.112 = bf16[4,128,768]{2,1,0:T(8,128)(2,1)} slice(bf16[4,128,1920]{2,1,0:T(8,128)(2,1)} %all-to-all-done), slice={[0:4], [0:128], [1152:1920]} | slice | bytes 1572864 | tf_op jit(solution)/shard_map/slice | solution.py:291
  63.4 3.3 %shard_map.104 = (f32[256,1152]{1,0:T(8,128)S(1)}, f32[256,1]{1,0:T(8,128)S(1)}) custom-call(bf16[256,1152]{1,0:T(8,128)(2,1)S(1)} %get-tuple-element.52.refs_0_, bf16[256,1152]{1,0:T(8,128)(2,1)S(1)} %fusion.8.refs_1_, s32[256,1]{1,0:T(8,128)S(1)} %copy.24.refs_2_, bf16[256,1152]{1,0:T(8,128)(2,1)S(1)} %collective-permute-done.2.refs_3_, ...), custom_call_target="tpu_custom_call" | custom-call | flops 1811939328 | bytes 2359296 | tf_op jit(solution)/shard_map/pallas_call | solution.py:224
  66.8 1.8 %shard_map.105 = (f32[256,1152]{1,0:T(8,128)S(1)}, f32[256,1]{1,0:T(8,128)S(1)}) custom-call(bf16[256,1152]{1,0:T(8,128)(2,1)S(1)} %get-tuple-element.52.refs_0_, bf16[256,1152]{1,0:T(8,128)(2,1)S(1)} %fusion.8.refs_1_, s32[256,1]{1,0:T(8,128)S(1)} %copy.24.refs_2_, bf16[256,1152]{1,0:T(8,128)(2,1)S(1)} %collective-permute-done.3.refs_3_, ...), custom_call_target="tpu_custom_call" | custom-call | flops 905969664 | bytes 1179648 | tf_op jit(solution)/shard_map/pallas_call | solution.py:224
  69.5 4.9 %collective-permute-start.8 = (f32[128,1152]{1,0:T(8,128)}, f32[128,1152]{1,0:T(8,128)}, u32[]{:S(2)}, u32[]{:S(2)}) collective-permute-start(f32[128,1152]{1,0:T(8,128)} %slice.98), channel_id=1, source_target_pairs={{0,32},{1,33},{2,34},{3,35},{4,36},{5,37},{6,38},{7,39},{8,40},{9,... | collective-permute-start | bytes 1769480 | tf_op jit(solution)/shard_map/ppermute | solution.py:91
  77.8 2.4 %fusion.2 = bf16[1280,128]{1,0:T(8,128)(2,1)S(1)} fusion(s32[1280]{0:T(1024)S(1)} %fusion.42, f32[256,1152]{1,0:T(8,128)S(1)} %copy-done.6, f32[128]{0:T(128)S(1)} %multiply_reduce_fusion.1, f32[128]{0:T(128)S(1)} %slice-done, f32[128,1152]{1,0:T(8,128)} %collective-permute-done.8, f32[256,1152]{1,0:T(8,128)S(1)} %get-tuple-element.36), kind=kOutput, calls=%fused_computation.3 | convolution fusion | flops 380010496 | bytes 2106368 | tf_op jit(solution)/shard_map/dot_general | solution.py:365
  80.2 9.4 %all_to_all.30 = bf16[4,320,128]{2,1,0:T(8,128)(2,1)S(1)} all-to-all(bf16[4,320,128]{2,1,0:T(8,128)(2,1)S(1)} %bitcast.69), channel_id=1, replica_groups={{0,64,16,80},{128,192,144,208},{256,320,272,336},{384,448,400,464},{1,6..., dimensions={0} | all-to-all | bytes 655360 | tf_op jit(solution)/shard_map/all_to_all | solution.py:83
  90.1 11.8 %all_to_all.31 = f32[4,80,768]{2,1,0:T(8,128)S(1)} all-to-all(f32[4,80,768]{2,1,0:T(8,128)S(1)} %bitcast.65), channel_id=1, replica_groups={{0,128,256,384},{64,192,320,448},{16,144,272,400},{80,208,336,464},{1,1..., dimensions={0} | all-to-all | bytes 1966080 | tf_op jit(solution)/shard_map/all_to_all | solution.py:83
  102.0 4.8 %collective-permute-start.9 = (f32[88,384]{1,0:T(8,128)S(1)}, f32[88,384]{1,0:T(8,128)S(1)}, u32[]{:S(2)}, u32[]{:S(2)}) collective-permute-start(f32[88,384]{1,0:T(8,128)S(1)} %pad_maximum_fusion.2), channel_id=1, source_target_pairs={{0,32},{1,33},{2,34},{3,35},{4,36},{5,37},{6,38},{7,39},{8,40},{9,... | collective-permute-start | bytes 405512 | tf_op jit(solution)/shard_map/ppermute | solution.py:91
  107.8 21.5 %all_to_all.32 = f32[16,16,128]{2,1,0:T(8,128)S(1)} all-to-all(f32[16,16,128]{2,1,0:T(8,128)S(1)} %pad.23), channel_id=1, replica_groups={{0,1,2,3,4,5,6,7,8,9,10,11,12,13,14,15},{32,33,34,35,36,37,38,39,40,41,..., dimensions={0} | all-to-all | bytes 262144 | tf_op jit(solution)/shard_map/all_to_all | solution.py:83
  129.4 18.2 %all_to_all.33 = bf16[16,5,384]{2,1,0:T(8,128)(2,1)S(1)} all-to-all(bf16[16,5,384]{2,1,0:T(8,128)(2,1)S(1)} %broadcast_in_dim.9), channel_id=1, replica_groups={{0,1,2,3,4,5,6,7,8,9,10,11,12,13,14,15},{32,33,34,35,36,37,38,39,40,41,..., dimensions={0} | all-to-all | bytes 122880 | tf_op jit(solution)/shard_map/all_to_all | solution.py:83
  148.9 3.7 %all-to-all-start.5 = ((bf16[16,96,384]{2,1,0:T(8,128)(2,1)}), bf16[16,96,384]{2,1,0:T(8,128)(2,1)S(1)}, u32[]{:S(2)}, u32[]{:S(2)}) async-start(bf16[16,96,384]{2,1,0:T(8,128)(2,1)} %broadcast_in_dim.11), calls=%async_computation.5 | async-start | bytes 2359296 | tf_op jit(solution)/shard_map/all_to_all | solution.py:83
  152.6 14.3 %all-to-all-done.5 = bf16[16,96,384]{2,1,0:T(8,128)(2,1)S(1)} async-done(((bf16[16,96,384]{2,1,0:T(8,128)(2,1)}), bf16[16,96,384]{2,1,0:T(8,128)(2,1)S(1)}, u32[]{:S(2)}, u32[]{:S(2)}) %all-to-all-start.5) | async-done | bytes 1179680 | tf_op jit(solution)/shard_map/all_to_all | solution.py:83
  168.8 6.8 %collective-permute-start.10 = (bf16[1296,384]{1,0:T(8,128)(2,1)S(1)}, bf16[1296,384]{1,0:T(8,128)(2,1)S(1)}, u32[]{:S(2)}, u32[]{:S(2)}) collective-permute-start(bf16[1296,384]{1,0:T(8,128)(2,1)S(1)} %pad_maximum_fusion.half_ref), channel_id=1, source_target_pairs={{0,32},{1,33},{2,34},{3,35},{4,36},{5,37},{6,38},{7,39},{8,40},{9,... | collective-permute-start | bytes 2985992 | tf_op jit(solution)/shard_map/ppermute | solution.py:91
  (79 shorter events, 25.1 us)
Async XLA Ops:
  0.6 21.7 %copy-start = (bf16[1152,768]{1,0:T(8,128)(2,1)S(1)}, bf16[1152,768]{1,0:T(8,128)(2,1)}, u32[]{:S(2)}) copy-start(bf16[1152,768]{1,0:T(8,128)(2,1)} %param.11) | copy-start | bytes 5308420
  0.6 1.1 copy-start.4
  1.7 3.6 %copy-start.7 = (bf16[128,1152]{1,0:T(8,128)(2,1)S(1)}, bf16[128,1152]{1,0:T(8,128)(2,1)}, u32[]{:S(2)}) copy-start(bf16[128,1152]{1,0:T(8,128)(2,1)} %param.8) | copy-start | bytes 884740
  4.1 1.3 copy-start.1
  5.3 38.9 %collective-permute-start.1 = (bf16[128,1152]{1,0:T(8,128)(2,1)S(1)}, bf16[128,1152]{1,0:T(8,128)(2,1)}, u32[]{:S(2)}, u32[]{:S(2)}) collective-permute-start(bf16[128,1152]{1,0:T(8,128)(2,1)S(1)} %copy-done.7), channel_id=1, source_target_pairs={{0,32},{1,33},{2,34},{3,35},{4,36},{5,37},{6,38},{7,39},{8,40},{9,... | collective-permute-start | bytes 884744 | tf_op jit(solution)/shard_map/ppermute | solution.py:91
  14.1 8.2 %collective-permute-start = (bf16[128,768]{1,0:T(8,128)(2,1)}, bf16[128,768]{1,0:T(8,128)(2,1)}, u32[]{:S(2)}, u32[]{:S(2)}) collective-permute-start(bf16[128,768]{1,0:T(8,128)(2,1)} %features_ref.1), channel_id=1, source_target_pairs={{0,32},{1,33},{2,34},{3,35},{4,36},{5,37},{6,38},{7,39},{8,40},{9,... | collective-permute-start | bytes 589832 | tf_op jit(solution)/shard_map/ppermute | solution.py:91
  16.0 19.2 %all-to-all-start = ((bf16[4,128,1920]{2,1,0:T(8,128)(2,1)}), bf16[4,128,1920]{2,1,0:T(8,128)(2,1)}, u32[]{:S(2)}, u32[]{:S(2)}) async-start(bf16[4,128,1920]{2,1,0:T(8,128)(2,1)} %copy-done.1), calls=%async_computation | async-start | bytes 3932160 | tf_op jit(solution)/shard_map/all_to_all | solution.py:83
  24.2 50.6 %copy-start.8 = (f32[256]{0:T(256)}, f32[256]{0:T(256)S(1)}, u32[]{:S(2)}) copy-start(f32[256]{0:T(256)S(1)} %add_rsqrt_fusion.1) | copy-start | bytes 3076
  36.5 15.4 %collective-permute-start.2 = (bf16[256,1152]{1,0:T(8,128)(2,1)S(1)}, bf16[256,1152]{1,0:T(8,128)(2,1)S(1)}, u32[]{:S(2)}, u32[]{:S(2)}) collective-permute-start(bf16[256,1152]{1,0:T(8,128)(2,1)S(1)} %bitcast.51), channel_id=1, source_target_pairs={{0,128},{1,129},{2,130},{3,131},{4,132},{5,133},{6,134},{7,135},{8... | collective-permute-start | bytes 1769480 | tf_op jit(solution)/shard_map/ppermute | solution.py:292
  38.4 15.4 %collective-permute-start.4 = (bf16[256,1152]{1,0:T(8,128)(2,1)S(1)}, bf16[256,1152]{1,0:T(8,128)(2,1)S(1)}, u32[]{:S(2)}, u32[]{:S(2)}) collective-permute-start(bf16[256,1152]{1,0:T(8,128)(2,1)S(1)} %bitcast.54), channel_id=1, source_target_pairs={{0,384},{1,385},{2,386},{3,387},{4,388},{5,389},{6,390},{7,391},{8... | collective-permute-start | bytes 1769480 | tf_op jit(solution)/shard_map/ppermute | solution.py:293
  45.4 18.1 %collective-permute-start.6 = (bf16[256,1152]{1,0:T(8,128)(2,1)S(1)}, bf16[256,1152]{1,0:T(8,128)(2,1)S(1)}, u32[]{:S(2)}, u32[]{:S(2)}) collective-permute-start(bf16[256,1152]{1,0:T(8,128)(2,1)S(1)} %bitcast.55), channel_id=1, source_target_pairs={{0,128},{1,129},{2,130},{3,131},{4,132},{5,133},{6,134},{7,135},{8... | collective-permute-start | bytes 1769480 | tf_op jit(solution)/shard_map/ppermute | solution.py:294
  47.3 16.1 %collective-permute-start.7 = (bf16[256,1152]{1,0:T(8,128)(2,1)S(1)}, bf16[256,1152]{1,0:T(8,128)(2,1)S(1)}, u32[]{:S(2)}, u32[]{:S(2)}) collective-permute-start(bf16[256,1152]{1,0:T(8,128)(2,1)S(1)} %bitcast.52), channel_id=1, source_target_pairs={{0,384},{1,385},{2,386},{3,387},{4,388},{5,389},{6,390},{7,391},{8... | collective-permute-start | bytes 1769480 | tf_op jit(solution)/shard_map/ppermute | solution.py:295
  51.9 14.9 %collective-permute-start.3 = (bf16[256,1152]{1,0:T(8,128)(2,1)S(1)}, bf16[256,1152]{1,0:T(8,128)(2,1)S(1)}, u32[]{:S(2)}, u32[]{:S(2)}) collective-permute-start(bf16[256,1152]{1,0:T(8,128)(2,1)S(1)} %collective-permute-done.2.refs_3_), channel_id=1, source_target_pairs={{0,128},{1,129},{2,130},{3,131},{4,132},{5,133},{6,134},{7,135},{8... | collective-permute-start | bytes 1769480 | tf_op jit(solution)/shard_map/ppermute | solution.py:296
  53.8 12.9 %collective-permute-start.5 = (bf16[256,1152]{1,0:T(8,128)(2,1)S(1)}, bf16[256,1152]{1,0:T(8,128)(2,1)S(1)}, u32[]{:S(2)}, u32[]{:S(2)}) collective-permute-start(bf16[256,1152]{1,0:T(8,128)(2,1)S(1)} %collective-permute-done.4.refs_4_), channel_id=1, source_target_pairs={{0,384},{1,385},{2,386},{3,387},{4,388},{5,389},{6,390},{7,391},{8... | collective-permute-start | bytes 1769480 | tf_op jit(solution)/shard_map/ppermute | solution.py:297
  68.6 6.0 %copy-start.2 = (f32[36,768]{1,0:T(8,128)S(1)}, f32[36,768]{1,0:T(8,128)}, u32[]{:S(2)}) copy-start(f32[36,768]{1,0:T(8,128)} %second_ref.1) | copy-start | bytes 331780
  68.6 6.0 %copy-start.3 = (f32[36,768]{1,0:T(8,128)S(1)}, f32[36,768]{1,0:T(8,128)}, u32[]{:S(2)}) copy-start(f32[36,768]{1,0:T(8,128)} %first_ref.1) | copy-start | bytes 331780
  69.5 6.9 %collective-permute-start.8 = (f32[128,1152]{1,0:T(8,128)}, f32[128,1152]{1,0:T(8,128)}, u32[]{:S(2)}, u32[]{:S(2)}) collective-permute-start(f32[128,1152]{1,0:T(8,128)} %slice.98), channel_id=1, source_target_pairs={{0,32},{1,33},{2,34},{3,35},{4,36},{5,37},{6,38},{7,39},{8,40},{9,... | collective-permute-start | bytes 1769480 | tf_op jit(solution)/shard_map/ppermute | solution.py:91
  74.5 3.3 %copy-start.6 = (f32[256,1152]{1,0:T(8,128)S(1)}, f32[256,1152]{1,0:T(8,128)}, u32[]{:S(2)}) copy-start(f32[256,1152]{1,0:T(8,128)} %get-tuple-element.53) | copy-start | bytes 3538948
  74.8 3.0 %slice-start = ((f32[256]{0:T(256)}), f32[128]{0:T(128)S(1)}, s32[]{:S(2)}) async-start(f32[256]{0:T(256)} %copy-done.8), calls=%async_computation.6 | async-start | bytes 1024 | tf_op jit(solution)/shard_map/slice | solution.py:359
  77.8 11.8 %copy-start.5 = (bf16[4,128,768]{2,1,0:T(8,128)(2,1)S(1)}, bf16[4,128,768]{2,1,0:T(8,128)(2,1)}, u32[]{:S(2)}) copy-start(bf16[4,128,768]{2,1,0:T(8,128)(2,1)} %slice.112) | copy-start | bytes 2359300
  102.0 5.7 %collective-permute-start.9 = (f32[88,384]{1,0:T(8,128)S(1)}, f32[88,384]{1,0:T(8,128)S(1)}, u32[]{:S(2)}, u32[]{:S(2)}) collective-permute-start(f32[88,384]{1,0:T(8,128)S(1)} %pad_maximum_fusion.2), channel_id=1, source_target_pairs={{0,32},{1,33},{2,34},{3,35},{4,36},{5,37},{6,38},{7,39},{8,40},{9,... | collective-permute-start | bytes 405512 | tf_op jit(solution)/shard_map/ppermute | solution.py:91
  148.9 18.0 %all-to-all-start.5 = ((bf16[16,96,384]{2,1,0:T(8,128)(2,1)}), bf16[16,96,384]{2,1,0:T(8,128)(2,1)S(1)}, u32[]{:S(2)}, u32[]{:S(2)}) async-start(bf16[16,96,384]{2,1,0:T(8,128)(2,1)} %broadcast_in_dim.11), calls=%async_computation.5 | async-start | bytes 2359296 | tf_op jit(solution)/shard_map/all_to_all | solution.py:83
  168.8 9.0 %collective-permute-start.10 = (bf16[1296,384]{1,0:T(8,128)(2,1)S(1)}, bf16[1296,384]{1,0:T(8,128)(2,1)S(1)}, u32[]{:S(2)}, u32[]{:S(2)}) collective-permute-start(bf16[1296,384]{1,0:T(8,128)(2,1)S(1)} %pad_maximum_fusion.half_ref), channel_id=1, source_target_pairs={{0,32},{1,33},{2,34},{3,35},{4,36},{5,37},{6,38},{7,39},{8,40},{9,... | collective-permute-start | bytes 2985992 | tf_op jit(solution)/shard_map/ppermute | solution.py:91

commit v4 on v3

--- a/solution.py
+++ b/solution.py
@@ -120,14 +120,14 @@
     return pl.pallas_call(
         copies_kernel,
         out_shape=jax.ShapeDtypeStruct((count, rows, width), jnp.bfloat16),
-        in_specs=[pl.BlockSpec(memory_space=pl.ANY)] * 2,
-        out_specs=pl.BlockSpec(memory_space=pl.ANY),
+        in_specs=[pl.BlockSpec(memory_space=pltpu.HBM)] * 2,
+        out_specs=pl.BlockSpec(memory_space=pltpu.HBM),
         scratch_shapes=[
             pltpu.VMEM(values.shape, jnp.bfloat16),
             pltpu.VMEM((rows, width), jnp.bfloat16),
             pltpu.SemaphoreType.DMA((2 + count,)),
         ],
-        compiler_params=pltpu.CompilerParams(vmem_limit_bytes=8 << 20),
+        compiler_params=pltpu.CompilerParams(vmem_limit_bytes=60 << 20),
         cost_estimate=pl.CostEstimate(
             flops=4 * values.size, bytes_accessed=2 * (count + 1) * rows * width, transcendentals=0
         ),
@@ -194,11 +194,13 @@
     return losses, (chance - target).astype(jnp.bfloat16)
 
 
-def pair_kernel(parts, carried, *refs):
+def pair_kernel(parts, carried, last, *refs):
     student_ref, teacher_ref, left_ref = refs[:3]
     chunks, ids = refs[3 : 3 + parts], refs[3 + parts : 3 + 2 * parts]
     rest = refs[3 + 2 * parts :]
     pulled_ref, losses_ref = rest[-2:]
+    if last:
+        own_ref, twin_ref, losses_ref, pulled_ref = rest[-4:]
     if carried:
         pulled_ref[...] = rest[0][...]
         losses_ref[...] = rest[1][...]
@@ -212,23 +214,27 @@
         )
         losses_ref[...] += losses
         pulled_ref[...] += jnp.dot(coeff, texts, preferred_element_type=jnp.float32)
-
-
-def pair_sums(student_rows, teacher_rows, left_ids, chunks, carried=()):
+    if last:
+        half = pulled_ref.shape[0] // 2
+        own_ref[...] = pulled_ref[:half]
+        twin_ref[...] = pulled_ref[half:]
+
+
+def pair_sums(student_rows, teacher_rows, left_ids, chunks, carried=(), last=False):
     rows, width = student_rows.shape
     texts = [chunk for chunk, _ in chunks]
     ids = [ids.reshape(1, -1) for _, ids in chunks]
     count = sum(chunk.shape[0] for chunk in texts)
     operands = (student_rows, teacher_rows, left_ids, *texts, *ids, *carried)
     whole = pl.BlockSpec(memory_space=pltpu.VMEM)
+    parts = 1 + last
+    sums = (jax.ShapeDtypeStruct((rows // parts, width), jnp.float32),) * parts
     return pl.pallas_call(
-        functools.partial(pair_kernel, len(texts), bool(carried)),
-        out_shape=(
-            jax.ShapeDtypeStruct((rows, width), jnp.float32),
-            jax.ShapeDtypeStruct((rows, 1), jnp.float32),
-        ),
+        functools.partial(pair_kernel, len(texts), bool(carried), last),
+        out_shape=(*sums, jax.ShapeDtypeStruct((rows, 1), jnp.float32)),
         in_specs=[whole] * len(operands),
-        out_specs=(whole, whole),
+        out_specs=(whole,) * (len(sums) + 1),
+        scratch_shapes=[pltpu.VMEM((rows, width), jnp.float32)] * last,
         compiler_params=pltpu.CompilerParams(vmem_limit_bytes=20 << 20),
         cost_estimate=pl.CostEstimate(
             flops=6 * rows * count * width,
@@ -336,26 +342,11 @@
     ]
     sums = pair_sums(*images, near_chunks, sums)
     features, sums = lax.optimization_barrier((features, sums))
-    pulled, losses = pair_sums(
-        *images, [(far_top, ids_at(2)[:2]), (far_bottom, ids_at(2)[2:])], sums
-    )
+    far_chunks = [(far_top, ids_at(2)[:2]), (far_bottom, ids_at(2)[2:])]
+    pulled, twin_pulled, losses = pair_sums(*images, far_chunks, sums, last=True)
     losses = losses.reshape(-1)
 
-    def piece(values, start):
-        group_rows = lax.dynamic_slice_in_dim(values, start, 36, 0)
-        padded = jnp.pad(group_rows, ((0, 4), (0, 0)))
-        return lax.dynamic_slice(padded, ((xh * 4 + y) * 5, core * 384), (5, 384))
-
-    own_moments = (
-        piece(moment_first, 0),
-        piece(moment_second, 0),
-        piece(head_weights, group_index * 36),
-    )
-    order = row_order(core)
-    own_losses = losses[:rows]
-    other_losses = jnp.pad(losses[rows:].reshape(1, rows), ((0, 7), (0, 256)))
-
-    pulled = pulled[:rows] + from_twin(pulled[rows:])
+    pulled = pulled + from_twin(twin_pulled)
     student, inverse = student[:rows], inverse[:rows]
     grad_student = student_scale / rows * pulled
     grad_projected = (
@@ -363,23 +354,21 @@
     ).astype(jnp.bfloat16)
 
     grad_rows = lax.dot_general(
-        one_hot(order, 1152),
+        one_hot(row_order(core), 1152),
         grad_projected,
         (((1,), (1,)), ((), ())),
         preferred_element_type=jnp.float32,
     ).astype(jnp.bfloat16)
-    grad_rows, own_moments, own_losses, other_losses = lax.optimization_barrier(
-        (grad_rows, own_moments, own_losses, other_losses)
-    )
     grad_rows = exchange(grad_rows.reshape(4, 320, rows), FIRST)
     line_grad = lax.dot_general(
         grad_rows, features, (((0, 2), (0, 1)), ((), ())), preferred_element_type=jnp.float32
     )
     core_grad = jnp.sum(exchange(line_grad.reshape(4, 80, 768), SECOND), axis=0)
     left, right = core_grad[:, :384], core_grad[:, 384:]
+    other_losses = jnp.pad(losses[rows:].reshape(1, rows), ((0, 7), (0, 256)))
     arrived = from_twin(jnp.concatenate([jnp.where(core == 0, right, left), other_losses], axis=0))
     chip_grad = jnp.where(core == 0, left, right) + arrived[:80]
-    row_loss = (own_losses + arrived[80, :rows]) / rows
+    row_loss = (losses[:rows] + arrived[80, :rows]) / rows
 
     column_grad = jnp.pad(chip_grad.reshape(16, 15, 128), ((0, 0), (0, 1), (0, 0)))
     own_grad = jnp.sum(exchange(column_grad, COLUMN), axis=0)[:15].reshape(5, 384)
@@ -395,7 +384,17 @@
         )
         return updated.astype(jnp.bfloat16)
 
-    own_weights = adam(own_grad, *own_moments)
+    def piece(values, start):
+        group_rows = lax.dynamic_slice_in_dim(values, start, 36, 0)
+        padded = jnp.pad(group_rows, ((0, 4), (0, 0)))
+        return lax.dynamic_slice(padded, ((xh * 4 + y) * 5, core * 384), (5, 384))
+
+    own_weights = adam(
+        own_grad,
+        piece(moment_first, 0),
+        piece(moment_second, 0),
+        piece(head_weights, group_index * 36),
+    )
     chip_weights = share(own_weights, COLUMN).reshape(80, 384)
     high = rounded(own_grad)
     middle = rounded(own_grad - high)
@@ -403,14 +402,12 @@
     spare = jnp.zeros((1, 384), jnp.float32)
     grad_parts = jnp.concatenate([high, middle, low, spare], axis=0).astype(jnp.bfloat16)
     plane = share(jnp.concatenate([chip_weights, grad_parts], axis=0), PLANE).reshape(2, 768, 384)
-    plane, same_xl = lax.optimization_barrier((plane, xl))
-    after = same_xl - xl
-    select_weights = one_hot(weight_order() + after, 768)
+    select_weights = one_hot(weight_order(), 768)
     halves = [
         jnp.dot(select_weights, plane[i], preferred_element_type=jnp.float32) for i in range(2)
     ]
     group_parts = jnp.dot(
-        one_hot(grad_order() + after, 768),
+        one_hot(grad_order(), 768),
         lax.dynamic_index_in_dim(plane, xl, 0, keepdims=False),
         preferred_element_type=jnp.float32,
     )

time: 180 us -> 176 us (0.978)
  blocking collectives: 60.9 us -> 28.4 us
  waiting for transfers between devices: 29.5 us -> 50.6 us
  starting transfers between devices: 54.8 us -> 67.4 us
  local copies, waits for them, and re-layouts: 10.1 us -> 6.58 us
  other arithmetic: 5.78 us -> 3.6 us
    all_to_all x4 -> x2, blocking collectives: 60.9 us -> 28.4 us  [exchange(): lax.all_to_all(pieces, AXES, 0, 0, axis_index_groups=groups, tiled=True)]
    all_to_all x2 -> x4, waiting for transfers between devices: 25.3 us -> 46.4 us  [exchange(): lax.all_to_all(pieces, AXES, 0, 0, axis_index_groups=groups, tiled=True)]
    all_to_all x2 -> x4, starting transfers between devices: 8.13 us -> 21.4 us  [exchange(): lax.all_to_all(pieces, AXES, 0, 0, axis_index_groups=groups, tiled=True)]
    unnamed x18 -> x12, local copies, waits for them, and re-layouts: 2.38 us -> 0.04 us
  transfers between devices with their start and end apart: 13 -> 15, of which waited for: 5 -> 7; matrix products, arithmetic and copies ran while one was open for 6% -> 5% of each run, Pallas kernels for 3% -> 3%
where the time goes in v4:
time: 176 us; the launch traced here: 175 us
  starting transfers between devices  67.4 us (38%)
  waiting for transfers between devices  50.6 us (29%)
  blocking collectives  28.4 us (16%)
  Pallas kernels  11 us (6%)
  local copies, waits for them, and re-layouts  6.58 us (4%)
  matrix products  6.11 us (3%)
  other arithmetic  3.6 us (2%)
    all_to_all x4, waiting for transfers between devices, exchange(): lax.all_to_all(pieces, AXES, 0, 0, axis_index_groups=groups, tiled=True)  46.4 us
    all_to_all x2, blocking collectives, exchange(): lax.all_to_all(pieces, AXES, 0, 0, axis_index_groups=groups, tiled=True)  28.4 us
    ppermute x5, starting transfers between devices, from_twin(): return lax.ppermute(shard, AXES, TWIN)  26.6 us
    all_to_all x4, starting transfers between devices, exchange(): lax.all_to_all(pieces, AXES, 0, 0, axis_index_groups=groups, tiled=True)  21.4 us
    pallas_call x3, Pallas kernels, pair_sums(): pl.pallas_call(functools.partial(pair_kernel, len(texts), bool(carried),...  6.95 us
    ppermute x1, starting transfers between devices, per_device(): after_top = lax.ppermute(top, AXES, BACK)  4.57 us
    ppermute x1, starting transfers between devices, per_device(): far_bottom = lax.ppermute(after_bottom, AXES, BACK)  4.57 us
    ppermute x1, starting transfers between devices, per_device(): after_bottom = lax.ppermute(bottom, AXES, BACK)  4.57 us
  transfers between devices with their start and end apart: 15, of which 7 were waited for; matrix products, arithmetic and copies ran while one was open for 5% of the time, Pallas kernels for 3%

profile of v4, /device:TPU:1, one launch (start us, length us, event | category | flops | bytes accessed | tf_op | source)
XLA Modules:
  0.0 175.1 jit_solution(875754879447547299)
XLA Ops:
  0.7 2.6 %shard_map.102 = bf16[4,128,1920]{2,1,0:T(8,128)(2,1)} custom-call(bf16[128,1152]{1,0:T(8,128)(2,1)} %texts_ref.1, bf16[128,768]{1,0:T(8,128)(2,1)} %features_ref.1), custom_call_target="tpu_custom_call" | custom-call | flops 589824 | bytes 2457600 | tf_op jit(solution)/shard_map/pallas_call | solution.py:120
  3.3 8.7 %collective-permute-start = (bf16[128,768]{1,0:T(8,128)(2,1)S(1)}, bf16[128,768]{1,0:T(8,128)(2,1)}, u32[]{:S(2)}, u32[]{:S(2)}) collective-permute-start(bf16[128,768]{1,0:T(8,128)(2,1)S(1)} %copy-done.4), channel_id=1, source_target_pairs={{0,32},{1,33},{2,34},{3,35},{4,36},{5,37},{6,38},{7,39},{8,40},{9,... | collective-permute-start | bytes 589832 | tf_op jit(solution)/shard_map/ppermute | solution.py:91
  12.1 1.9 %collective-permute-start.1 = (bf16[128,1152]{1,0:T(8,128)(2,1)S(1)}, bf16[128,1152]{1,0:T(8,128)(2,1)}, u32[]{:S(2)}, u32[]{:S(2)}) collective-permute-start(bf16[128,1152]{1,0:T(8,128)(2,1)S(1)} %copy-done.3), channel_id=1, source_target_pairs={{0,32},{1,33},{2,34},{3,35},{4,36},{5,37},{6,38},{7,39},{8,40},{9,... | collective-permute-start | bytes 884744 | tf_op jit(solution)/shard_map/ppermute | solution.py:91
  14.0 4.4 %all-to-all-start = ((bf16[4,128,1920]{2,1,0:T(8,128)(2,1)}), bf16[4,128,1920]{2,1,0:T(8,128)(2,1)}, u32[]{:S(2)}, u32[]{:S(2)}) async-start(bf16[4,128,1920]{2,1,0:T(8,128)(2,1)} %shard_map.102), calls=%async_computation | async-start | bytes 3932160 | tf_op jit(solution)/shard_map/all_to_all | solution.py:83
  22.3 10.9 %all-to-all-done = bf16[4,128,1920]{2,1,0:T(8,128)(2,1)} async-done(((bf16[4,128,1920]{2,1,0:T(8,128)(2,1)}), bf16[4,128,1920]{2,1,0:T(8,128)(2,1)}, u32[]{:S(2)}, u32[]{:S(2)}) %all-to-all-start) | async-done | bytes 1966112 | tf_op jit(solution)/shard_map/all_to_all | solution.py:83
  34.5 1.9 %collective-permute-start.2 = (bf16[256,1152]{1,0:T(8,128)(2,1)S(1)}, bf16[256,1152]{1,0:T(8,128)(2,1)S(1)}, u32[]{:S(2)}, u32[]{:S(2)}) collective-permute-start(bf16[256,1152]{1,0:T(8,128)(2,1)S(1)} %bitcast.49), channel_id=1, source_target_pairs={{0,128},{1,129},{2,130},{3,131},{4,132},{5,133},{6,134},{7,135},{8... | collective-permute-start | bytes 1769480 | tf_op jit(solution)/shard_map/ppermute | solution.py:298
  36.4 4.6 %collective-permute-start.4 = (bf16[256,1152]{1,0:T(8,128)(2,1)S(1)}, bf16[256,1152]{1,0:T(8,128)(2,1)S(1)}, u32[]{:S(2)}, u32[]{:S(2)}) collective-permute-start(bf16[256,1152]{1,0:T(8,128)(2,1)S(1)} %bitcast.52), channel_id=1, source_target_pairs={{0,384},{1,385},{2,386},{3,387},{4,388},{5,389},{6,390},{7,391},{8... | collective-permute-start | bytes 1769480 | tf_op jit(solution)/shard_map/ppermute | solution.py:299
  42.4 1.9 %collective-permute-start.6 = (bf16[256,1152]{1,0:T(8,128)(2,1)S(1)}, bf16[256,1152]{1,0:T(8,128)(2,1)S(1)}, u32[]{:S(2)}, u32[]{:S(2)}) collective-permute-start(bf16[256,1152]{1,0:T(8,128)(2,1)S(1)} %bitcast.53), channel_id=1, source_target_pairs={{0,128},{1,129},{2,130},{3,131},{4,132},{5,133},{6,134},{7,135},{8... | collective-permute-start | bytes 1769480 | tf_op jit(solution)/shard_map/ppermute | solution.py:300
  44.3 4.6 %collective-permute-start.7 = (bf16[256,1152]{1,0:T(8,128)(2,1)S(1)}, bf16[256,1152]{1,0:T(8,128)(2,1)S(1)}, u32[]{:S(2)}, u32[]{:S(2)}) collective-permute-start(bf16[256,1152]{1,0:T(8,128)(2,1)S(1)} %bitcast.50), channel_id=1, source_target_pairs={{0,384},{1,385},{2,386},{3,387},{4,388},{5,389},{6,390},{7,391},{8... | collective-permute-start | bytes 1769480 | tf_op jit(solution)/shard_map/ppermute | solution.py:301
  48.9 1.9 %collective-permute-start.3 = (bf16[256,1152]{1,0:T(8,128)(2,1)S(1)}, bf16[256,1152]{1,0:T(8,128)(2,1)S(1)}, u32[]{:S(2)}, u32[]{:S(2)}) collective-permute-start(bf16[256,1152]{1,0:T(8,128)(2,1)S(1)} %collective-permute-done.2.refs_3_), channel_id=1, source_target_pairs={{0,128},{1,129},{2,130},{3,131},{4,132},{5,133},{6,134},{7,135},{8... | collective-permute-start | bytes 1769480 | tf_op jit(solution)/shard_map/ppermute | solution.py:302
  50.8 4.6 %collective-permute-start.5 = (bf16[256,1152]{1,0:T(8,128)(2,1)S(1)}, bf16[256,1152]{1,0:T(8,128)(2,1)S(1)}, u32[]{:S(2)}, u32[]{:S(2)}) collective-permute-start(bf16[256,1152]{1,0:T(8,128)(2,1)S(1)} %collective-permute-done.4.refs_4_), channel_id=1, source_target_pairs={{0,384},{1,385},{2,386},{3,387},{4,388},{5,389},{6,390},{7,391},{8... | collective-permute-start | bytes 1769480 | tf_op jit(solution)/shard_map/ppermute | solution.py:303
  59.5 3.3 %shard_map.104 = (f32[256,1152]{1,0:T(8,128)S(1)}, f32[256,1]{1,0:T(8,128)S(1)}) custom-call(bf16[256,1152]{1,0:T(8,128)(2,1)S(1)} %get-tuple-element.38.refs_0_, bf16[256,1152]{1,0:T(8,128)(2,1)S(1)} %fusion.8.refs_1_, s32[256,1]{1,0:T(8,128)S(1)} %copy.24.refs_2_, bf16[256,1152]{1,0:T(8,128)(2,1)S(1)} %collective-permute-done.2.refs_3_, ...), custom_call_target="tpu_custom_call" | custom-call | flops 1811939328 | bytes 2359296 | tf_op jit(solution)/shard_map/pallas_call | solution.py:232
  62.9 1.8 %shard_map.105 = (f32[128,1152]{1,0:T(8,128)S(1)}, f32[128,1152]{1,0:T(8,128)S(1)}, f32[256,1]{1,0:T(8,128)S(1)}) custom-call(bf16[256,1152]{1,0:T(8,128)(2,1)S(1)} %get-tuple-element.38.refs_0_, bf16[256,1152]{1,0:T(8,128)(2,1)S(1)} %fusion.8.refs_1_, s32[256,1]{1,0:T(8,128)S(1)} %copy.24.refs_2_, bf16[256,1152]{1,0:T(8,128)(2,1)S(1)} %collective-permute-done.3.refs_3_, ...), custom_call_target="tpu_custom_call" | custom-call | flops 905969664 | bytes 1179648 | tf_op jit(solution)/shard_map/pallas_call | solution.py:232
  64.7 4.9 %collective-permute-start.8 = (f32[128,1152]{1,0:T(8,128)S(1)}, f32[128,1152]{1,0:T(8,128)S(1)}, u32[]{:S(2)}, u32[]{:S(2)}) collective-permute-start(f32[128,1152]{1,0:T(8,128)S(1)} %get-tuple-element.31), channel_id=1, source_target_pairs={{0,32},{1,33},{2,34},{3,35},{4,36},{5,37},{6,38},{7,39},{8,40},{9,... | collective-permute-start | bytes 1769480 | tf_op jit(solution)/shard_map/ppermute | solution.py:91
  72.7 10.2 %all_to_all.30 = bf16[4,320,128]{2,1,0:T(8,128)(2,1)S(1)} all-to-all(bf16[4,320,128]{2,1,0:T(8,128)(2,1)S(1)} %bitcast.67), channel_id=1, replica_groups={{0,64,16,80},{128,192,144,208},{256,320,272,336},{384,448,400,464},{1,6..., dimensions={0} | all-to-all | bytes 655360 | tf_op jit(solution)/shard_map/all_to_all | solution.py:83
  84.3 3.5 %all-to-all-start.2 = ((f32[4,80,768]{2,1,0:T(8,128)}), f32[4,80,768]{2,1,0:T(8,128)S(1)}, u32[]{:S(2)}, u32[]{:S(2)}) async-start(f32[4,80,768]{2,1,0:T(8,128)} %bitcast.64), calls=%async_computation.2 | async-start | bytes 1966080 | tf_op jit(solution)/shard_map/all_to_all | solution.py:83
  88.0 9.3 %all-to-all-done.2 = f32[4,80,768]{2,1,0:T(8,128)S(1)} async-done(((f32[4,80,768]{2,1,0:T(8,128)}), f32[4,80,768]{2,1,0:T(8,128)S(1)}, u32[]{:S(2)}, u32[]{:S(2)}) %all-to-all-start.2) | async-done | bytes 983072 | tf_op jit(solution)/shard_map/all_to_all | solution.py:83
  97.3 4.1 %collective-permute-start.9 = (f32[88,384]{1,0:T(8,128)S(1)}, f32[88,384]{1,0:T(8,128)S(1)}, u32[]{:S(2)}, u32[]{:S(2)}) collective-permute-start(f32[88,384]{1,0:T(8,128)S(1)} %select_maximum_fusion), channel_id=1, source_target_pairs={{0,32},{1,33},{2,34},{3,35},{4,36},{5,37},{6,38},{7,39},{8,40},{9,... | collective-permute-start | bytes 405512 | tf_op jit(solution)/shard_map/ppermute | solution.py:91
  103.2 9.6 %all-to-all-start.3 = ((f32[16,16,128]{2,1,0:T(8,128)}), f32[16,16,128]{2,1,0:T(8,128)S(1)}, u32[]{:S(2)}, u32[]{:S(2)}) async-start(f32[16,16,128]{2,1,0:T(8,128)} %pad.22), calls=%async_computation.3 | async-start | bytes 262144 | tf_op jit(solution)/shard_map/all_to_all | solution.py:83
  112.8 12.0 %all-to-all-done.3 = f32[16,16,128]{2,1,0:T(8,128)S(1)} async-done(((f32[16,16,128]{2,1,0:T(8,128)}), f32[16,16,128]{2,1,0:T(8,128)S(1)}, u32[]{:S(2)}, u32[]{:S(2)}) %all-to-all-start.3) | async-done | bytes 131104 | tf_op jit(solution)/shard_map/all_to_all | solution.py:83
  125.0 18.2 %all_to_all.31 = bf16[16,5,384]{2,1,0:T(8,128)(2,1)S(1)} all-to-all(bf16[16,5,384]{2,1,0:T(8,128)(2,1)S(1)} %broadcast_in_dim.9), channel_id=1, replica_groups={{0,1,2,3,4,5,6,7,8,9,10,11,12,13,14,15},{32,33,34,35,36,37,38,39,40,41,..., dimensions={0} | all-to-all | bytes 122880 | tf_op jit(solution)/shard_map/all_to_all | solution.py:83
  144.5 3.9 %all-to-all-start.5 = ((bf16[16,96,384]{2,1,0:T(8,128)(2,1)}), bf16[16,96,384]{2,1,0:T(8,128)(2,1)S(1)}, u32[]{:S(2)}, u32[]{:S(2)}) async-start(bf16[16,96,384]{2,1,0:T(8,128)(2,1)} %broadcast_in_dim.11), calls=%async_computation.5 | async-start | bytes 2359296 | tf_op jit(solution)/shard_map/all_to_all | solution.py:83
  148.5 14.3 %all-to-all-done.5 = bf16[16,96,384]{2,1,0:T(8,128)(2,1)S(1)} async-done(((bf16[16,96,384]{2,1,0:T(8,128)(2,1)}), bf16[16,96,384]{2,1,0:T(8,128)(2,1)S(1)}, u32[]{:S(2)}, u32[]{:S(2)}) %all-to-all-start.5) | async-done | bytes 1179680 | tf_op jit(solution)/shard_map/all_to_all | solution.py:83
  164.6 6.8 %collective-permute-start.10 = (bf16[1296,384]{1,0:T(8,128)(2,1)S(1)}, bf16[1296,384]{1,0:T(8,128)(2,1)S(1)}, u32[]{:S(2)}, u32[]{:S(2)}) collective-permute-start(bf16[1296,384]{1,0:T(8,128)(2,1)S(1)} %pad_maximum_fusion.half_ref), channel_id=1, source_target_pairs={{0,32},{1,33},{2,34},{3,35},{4,36},{5,37},{6,38},{7,39},{8,40},{9,... | collective-permute-start | bytes 2985992 | tf_op jit(solution)/shard_map/ppermute | solution.py:91
  (72 shorter events, 23.8 us)
Async XLA Ops:
  0.6 19.8 %copy-start = (bf16[1152,768]{1,0:T(8,128)(2,1)S(1)}, bf16[1152,768]{1,0:T(8,128)(2,1)}, u32[]{:S(2)}) copy-start(bf16[1152,768]{1,0:T(8,128)(2,1)} %param.11) | copy-start | bytes 5308420
  0.6 2.6 %copy-start.4 = (bf16[128,768]{1,0:T(8,128)(2,1)S(1)}, bf16[128,768]{1,0:T(8,128)(2,1)}, u32[]{:S(2)}) copy-start(bf16[128,768]{1,0:T(8,128)(2,1)} %features_ref.1) | copy-start | bytes 589828
  0.7 11.4 %copy-start.3 = (bf16[128,1152]{1,0:T(8,128)(2,1)S(1)}, bf16[128,1152]{1,0:T(8,128)(2,1)}, u32[]{:S(2)}) copy-start(bf16[128,1152]{1,0:T(8,128)(2,1)} %param.8) | copy-start | bytes 884740
  3.3 17.1 %collective-permute-start = (bf16[128,768]{1,0:T(8,128)(2,1)S(1)}, bf16[128,768]{1,0:T(8,128)(2,1)}, u32[]{:S(2)}, u32[]{:S(2)}) collective-permute-start(bf16[128,768]{1,0:T(8,128)(2,1)S(1)} %copy-done.4), channel_id=1, source_target_pairs={{0,32},{1,33},{2,34},{3,35},{4,36},{5,37},{6,38},{7,39},{8,40},{9,... | collective-permute-start | bytes 589832 | tf_op jit(solution)/shard_map/ppermute | solution.py:91
  12.1 29.1 %collective-permute-start.1 = (bf16[128,1152]{1,0:T(8,128)(2,1)S(1)}, bf16[128,1152]{1,0:T(8,128)(2,1)}, u32[]{:S(2)}, u32[]{:S(2)}) collective-permute-start(bf16[128,1152]{1,0:T(8,128)(2,1)S(1)} %copy-done.3), channel_id=1, source_target_pairs={{0,32},{1,33},{2,34},{3,35},{4,36},{5,37},{6,38},{7,39},{8,40},{9,... | collective-permute-start | bytes 884744 | tf_op jit(solution)/shard_map/ppermute | solution.py:91
  14.0 19.2 %all-to-all-start = ((bf16[4,128,1920]{2,1,0:T(8,128)(2,1)}), bf16[4,128,1920]{2,1,0:T(8,128)(2,1)}, u32[]{:S(2)}, u32[]{:S(2)}) async-start(bf16[4,128,1920]{2,1,0:T(8,128)(2,1)} %shard_map.102), calls=%async_computation | async-start | bytes 3932160 | tf_op jit(solution)/shard_map/all_to_all | solution.py:83
  22.3 47.4 %copy-start.5 = (f32[256]{0:T(256)}, f32[256]{0:T(256)S(1)}, u32[]{:S(2)}) copy-start(f32[256]{0:T(256)S(1)} %add_rsqrt_fusion.1) | copy-start | bytes 3076
  34.5 14.4 %collective-permute-start.2 = (bf16[256,1152]{1,0:T(8,128)(2,1)S(1)}, bf16[256,1152]{1,0:T(8,128)(2,1)S(1)}, u32[]{:S(2)}, u32[]{:S(2)}) collective-permute-start(bf16[256,1152]{1,0:T(8,128)(2,1)S(1)} %bitcast.49), channel_id=1, source_target_pairs={{0,128},{1,129},{2,130},{3,131},{4,132},{5,133},{6,134},{7,135},{8... | collective-permute-start | bytes 1769480 | tf_op jit(solution)/shard_map/ppermute | solution.py:298
  36.4 14.4 %collective-permute-start.4 = (bf16[256,1152]{1,0:T(8,128)(2,1)S(1)}, bf16[256,1152]{1,0:T(8,128)(2,1)S(1)}, u32[]{:S(2)}, u32[]{:S(2)}) collective-permute-start(bf16[256,1152]{1,0:T(8,128)(2,1)S(1)} %bitcast.52), channel_id=1, source_target_pairs={{0,384},{1,385},{2,386},{3,387},{4,388},{5,389},{6,390},{7,391},{8... | collective-permute-start | bytes 1769480 | tf_op jit(solution)/shard_map/ppermute | solution.py:299
  42.4 17.2 %collective-permute-start.6 = (bf16[256,1152]{1,0:T(8,128)(2,1)S(1)}, bf16[256,1152]{1,0:T(8,128)(2,1)S(1)}, u32[]{:S(2)}, u32[]{:S(2)}) collective-permute-start(bf16[256,1152]{1,0:T(8,128)(2,1)S(1)} %bitcast.53), channel_id=1, source_target_pairs={{0,128},{1,129},{2,130},{3,131},{4,132},{5,133},{6,134},{7,135},{8... | collective-permute-start | bytes 1769480 | tf_op jit(solution)/shard_map/ppermute | solution.py:300
  44.3 15.3 %collective-permute-start.7 = (bf16[256,1152]{1,0:T(8,128)(2,1)S(1)}, bf16[256,1152]{1,0:T(8,128)(2,1)S(1)}, u32[]{:S(2)}, u32[]{:S(2)}) collective-permute-start(bf16[256,1152]{1,0:T(8,128)(2,1)S(1)} %bitcast.50), channel_id=1, source_target_pairs={{0,384},{1,385},{2,386},{3,387},{4,388},{5,389},{6,390},{7,391},{8... | collective-permute-start | bytes 1769480 | tf_op jit(solution)/shard_map/ppermute | solution.py:301
  48.9 14.0 %collective-permute-start.3 = (bf16[256,1152]{1,0:T(8,128)(2,1)S(1)}, bf16[256,1152]{1,0:T(8,128)(2,1)S(1)}, u32[]{:S(2)}, u32[]{:S(2)}) collective-permute-start(bf16[256,1152]{1,0:T(8,128)(2,1)S(1)} %collective-permute-done.2.refs_3_), channel_id=1, source_target_pairs={{0,128},{1,129},{2,130},{3,131},{4,132},{5,133},{6,134},{7,135},{8... | collective-permute-start | bytes 1769480 | tf_op jit(solution)/shard_map/ppermute | solution.py:302
  50.8 12.1 %collective-permute-start.5 = (bf16[256,1152]{1,0:T(8,128)(2,1)S(1)}, bf16[256,1152]{1,0:T(8,128)(2,1)S(1)}, u32[]{:S(2)}, u32[]{:S(2)}) collective-permute-start(bf16[256,1152]{1,0:T(8,128)(2,1)S(1)} %collective-permute-done.4.refs_4_), channel_id=1, source_target_pairs={{0,384},{1,385},{2,386},{3,387},{4,388},{5,389},{6,390},{7,391},{8... | collective-permute-start | bytes 1769480 | tf_op jit(solution)/shard_map/ppermute | solution.py:303
  64.7 6.6 %collective-permute-start.8 = (f32[128,1152]{1,0:T(8,128)S(1)}, f32[128,1152]{1,0:T(8,128)S(1)}, u32[]{:S(2)}, u32[]{:S(2)}) collective-permute-start(f32[128,1152]{1,0:T(8,128)S(1)} %get-tuple-element.31), channel_id=1, source_target_pairs={{0,32},{1,33},{2,34},{3,35},{4,36},{5,37},{6,38},{7,39},{8,40},{9,... | collective-permute-start | bytes 1769480 | tf_op jit(solution)/shard_map/ppermute | solution.py:91
  69.7 1.7 slice-start
  84.3 12.9 %all-to-all-start.2 = ((f32[4,80,768]{2,1,0:T(8,128)}), f32[4,80,768]{2,1,0:T(8,128)S(1)}, u32[]{:S(2)}, u32[]{:S(2)}) async-start(f32[4,80,768]{2,1,0:T(8,128)} %bitcast.64), calls=%async_computation.2 | async-start | bytes 1966080 | tf_op jit(solution)/shard_map/all_to_all | solution.py:83
  97.3 27.6 %copy-start.1 = (f32[36,768]{1,0:T(8,128)S(1)}, f32[36,768]{1,0:T(8,128)}, u32[]{:S(2)}) copy-start(f32[36,768]{1,0:T(8,128)} %second_ref.1) | copy-start | bytes 331780
  97.3 27.6 %copy-start.2 = (f32[36,768]{1,0:T(8,128)S(1)}, f32[36,768]{1,0:T(8,128)}, u32[]{:S(2)}) copy-start(f32[36,768]{1,0:T(8,128)} %first_ref.1) | copy-start | bytes 331780
  97.3 5.1 %collective-permute-start.9 = (f32[88,384]{1,0:T(8,128)S(1)}, f32[88,384]{1,0:T(8,128)S(1)}, u32[]{:S(2)}, u32[]{:S(2)}) collective-permute-start(f32[88,384]{1,0:T(8,128)S(1)} %select_maximum_fusion), channel_id=1, source_target_pairs={{0,32},{1,33},{2,34},{3,35},{4,36},{5,37},{6,38},{7,39},{8,40},{9,... | collective-permute-start | bytes 405512 | tf_op jit(solution)/shard_map/ppermute | solution.py:91
  103.2 21.7 %all-to-all-start.3 = ((f32[16,16,128]{2,1,0:T(8,128)}), f32[16,16,128]{2,1,0:T(8,128)S(1)}, u32[]{:S(2)}, u32[]{:S(2)}) async-start(f32[16,16,128]{2,1,0:T(8,128)} %pad.22), calls=%async_computation.3 | async-start | bytes 262144 | tf_op jit(solution)/shard_map/all_to_all | solution.py:83
  144.5 18.2 %all-to-all-start.5 = ((bf16[16,96,384]{2,1,0:T(8,128)(2,1)}), bf16[16,96,384]{2,1,0:T(8,128)(2,1)S(1)}, u32[]{:S(2)}, u32[]{:S(2)}) async-start(bf16[16,96,384]{2,1,0:T(8,128)(2,1)} %broadcast_in_dim.11), calls=%async_computation.5 | async-start | bytes 2359296 | tf_op jit(solution)/shard_map/all_to_all | solution.py:83
  164.6 9.0 %collective-permute-start.10 = (bf16[1296,384]{1,0:T(8,128)(2,1)S(1)}, bf16[1296,384]{1,0:T(8,128)(2,1)S(1)}, u32[]{:S(2)}, u32[]{:S(2)}) collective-permute-start(bf16[1296,384]{1,0:T(8,128)(2,1)S(1)} %pad_maximum_fusion.half_ref), channel_id=1, source_target_pairs={{0,32},{1,33},{2,34},{3,35},{4,36},{5,37},{6,38},{7,39},{8,40},{9,... | collective-permute-start | bytes 2985992 | tf_op jit(solution)/shard_map/ppermute | solution.py:91

commit v5 on v4

--- a/solution.py
+++ b/solution.py
@@ -96,42 +96,54 @@
     return values * lax.rsqrt(jnp.sum(values * values, axis=-1, keepdims=True) + norm_eps)
 
 
-def copies_kernel(texts_ref, features_ref, out_ref, texts, packed, sems):
+def head_kernel(texts_ref, features_ref, teacher_ref, out_ref, unit_ref, texts, teacher, packed, unit, sems):
     width = texts_ref.shape[1]
     take_texts = pltpu.make_async_copy(texts_ref, texts, sems.at[0])
     take_features = pltpu.make_async_copy(features_ref, packed.at[:, width:], sems.at[1])
+    take_teacher = pltpu.make_async_copy(teacher_ref, teacher, sems.at[2])
     take_texts.start()
     take_features.start()
+    take_teacher.start()
     take_texts.wait()
     packed[:, :width] = unit_rows(texts[...]).astype(jnp.bfloat16)
     take_features.wait()
     puts = [
-        pltpu.make_async_copy(packed, out_ref.at[i], sems.at[2 + i])
+        pltpu.make_async_copy(packed, out_ref.at[i], sems.at[3 + i])
         for i in range(out_ref.shape[0])
     ]
     for put in puts:
         put.start()
+    take_teacher.wait()
+    unit[...] = unit_rows(teacher[...]).astype(jnp.bfloat16)
+    put_unit = pltpu.make_async_copy(unit, unit_ref, sems.at[3 + len(puts)])
+    put_unit.start()
     for put in puts:
         put.wait()
-
-
-def unit_copies(values, others, count):
-    rows, width = values.shape[0], values.shape[1] + others.shape[1]
+    put_unit.wait()
+
+
+def head(texts, features, teacher, count):
+    rows, width = texts.shape[0], texts.shape[1] + features.shape[1]
     return pl.pallas_call(
-        copies_kernel,
-        out_shape=jax.ShapeDtypeStruct((count, rows, width), jnp.bfloat16),
-        in_specs=[pl.BlockSpec(memory_space=pltpu.HBM)] * 2,
-        out_specs=pl.BlockSpec(memory_space=pltpu.HBM),
+        head_kernel,
+        out_shape=(
+            jax.ShapeDtypeStruct((count, rows, width), jnp.bfloat16),
+            jax.ShapeDtypeStruct(teacher.shape, jnp.bfloat16),
+        ),
+        in_specs=[pl.BlockSpec(memory_space=pltpu.HBM)] * 3,
+        out_specs=(pl.BlockSpec(memory_space=pltpu.HBM),) * 2,
         scratch_shapes=[
-            pltpu.VMEM(values.shape, jnp.bfloat16),
+            pltpu.VMEM(texts.shape, jnp.bfloat16),
+            pltpu.VMEM(teacher.shape, jnp.bfloat16),
             pltpu.VMEM((rows, width), jnp.bfloat16),
-            pltpu.SemaphoreType.DMA((2 + count,)),
+            pltpu.VMEM(teacher.shape, jnp.bfloat16),
+            pltpu.SemaphoreType.DMA((4 + count,)),
         ],
         compiler_params=pltpu.CompilerParams(vmem_limit_bytes=60 << 20),
         cost_estimate=pl.CostEstimate(
-            flops=4 * values.size, bytes_accessed=2 * (count + 1) * rows * width, transcendentals=0
+            flops=8 * texts.size, bytes_accessed=2 * (count + 2) * rows * width, transcendentals=0
         ),
-    )(values, others)
+    )(texts, features, teacher)
 
 
 def last_kernel(core_ref, half_ref, twin_ref, first_ref, second_ref, *outs):
@@ -194,10 +206,9 @@
     return losses, (chance - target).astype(jnp.bfloat16)
 
 
-def pair_kernel(parts, carried, last, *refs):
-    student_ref, teacher_ref, left_ref = refs[:3]
-    chunks, ids = refs[3 : 3 + parts], refs[3 + parts : 3 + 2 * parts]
-    rest = refs[3 + 2 * parts :]
+def pair_kernel(places, carried, last, *refs):
+    student_ref, own_teacher_ref, twin_teacher_ref, left_ref, ids_ref = refs[:5]
+    chunks, rest = refs[5 : 5 + len(places)], refs[5 + len(places) :]
     pulled_ref, losses_ref = rest[-2:]
     if last:
         own_ref, twin_ref, losses_ref, pulled_ref = rest[-4:]
@@ -207,10 +218,14 @@
     else:
         pulled_ref[...] = jnp.zeros_like(pulled_ref)
         losses_ref[...] = jnp.zeros_like(losses_ref)
-    for chunk_ref, ids_ref in zip(chunks, ids):
+    teacher = jnp.concatenate([own_teacher_ref[...], twin_teacher_ref[...]], axis=0)
+    left_ids = jnp.concatenate(
+        [jnp.transpose(jnp.broadcast_to(left_ref[i : i + 1, :], (128, 128))) for i in range(2)], axis=0
+    )[:, :1]
+    for place, chunk_ref in zip(places, chunks):
         texts = chunk_ref[...]
         losses, coeff = pair_terms(
-            student_ref[...], teacher_ref[...], left_ref[...], texts, ids_ref[...]
+            student_ref[...], teacher, left_ids, texts, ids_ref[place : place + 1, :]
         )
         losses_ref[...] += losses
         pulled_ref[...] += jnp.dot(coeff, texts, preferred_element_type=jnp.float32)
@@ -220,17 +235,16 @@
         twin_ref[...] = pulled_ref[half:]
 
 
-def pair_sums(student_rows, teacher_rows, left_ids, chunks, carried=(), last=False):
+def pair_sums(student_rows, own_teacher, twin_teacher, left_ids, text_ids, chunks, carried=(), last=False):
     rows, width = student_rows.shape
-    texts = [chunk for chunk, _ in chunks]
-    ids = [ids.reshape(1, -1) for _, ids in chunks]
+    texts, places = zip(*chunks)
     count = sum(chunk.shape[0] for chunk in texts)
-    operands = (student_rows, teacher_rows, left_ids, *texts, *ids, *carried)
+    operands = (student_rows, own_teacher, twin_teacher, left_ids, text_ids, *texts, *carried)
     whole = pl.BlockSpec(memory_space=pltpu.VMEM)
     parts = 1 + last
     sums = (jax.ShapeDtypeStruct((rows // parts, width), jnp.float32),) * parts
     return pl.pallas_call(
-        functools.partial(pair_kernel, len(texts), bool(carried), last),
+        functools.partial(pair_kernel, places, bool(carried), last),
         out_shape=(*sums, jax.ShapeDtypeStruct((rows, 1), jnp.float32)),
         in_specs=[whole] * len(operands),
         out_specs=(whole,) * (len(sums) + 1),
@@ -288,65 +302,59 @@
     y, xh, core = blk_index // 4, blk_index // 2 % 2, blk_index % 2
     xl, z = group_index // 16, group_index % 16
 
-    copies, teacher_image, twin_features = lax.optimization_barrier(
-        (unit_copies(text_embeds, student_features, 4), teacher_image, student_features)
-    )
+    copies, unit_teacher = head(text_embeds, student_features, teacher_image, 4)
+    copies, twin_features = lax.optimization_barrier((copies, student_features))
     near = exchange(copies, FIRST)
+
+    far_features, far_teacher = from_twin(twin_features), from_twin(unit_teacher)
+    both_features = jnp.concatenate([student_features, far_features], axis=0)
+    projected = lax.dot_general(
+        both_features,
+        head_weights,
+        (((1,), (1,)), ((), ())),
+        preferred_element_type=jnp.float32,
+    )
+    inverse = lax.rsqrt(jnp.sum(projected * projected, axis=-1, keepdims=True) + norm_eps)
+    student = projected * inverse
+    student_b = student.astype(jnp.bfloat16)
+
+    ids_grid = pair_ids.reshape(4, 2, 2, 2, 16, rows)
+    ids_plane = lax.dynamic_index_in_dim(ids_grid, z, 4, keepdims=False)
+    ids_core = lax.dynamic_index_in_dim(ids_plane, core, 2, keepdims=False)
+    ids_yx = ids_core.transpose(0, 2, 1, 3).reshape(4, 4, rows)
+    ids_xy = ids_core.transpose(1, 2, 0, 3).reshape(4, 4, rows)
+    text_ids = jnp.where(core == 0, ids_yx, ids_xy)
+    text_ids = jnp.concatenate([text_ids, text_ids[:3]], axis=0)
+    text_ids = lax.dynamic_slice_in_dim(text_ids, jnp.where(core == 0, y, xh * 2 + xl), 4, 0)
+    text_ids = text_ids.reshape(8, 2 * rows)
+    ids_rows = pair_ids.reshape(512, rows)
+    left_ids = jnp.stack(
+        [
+            lax.dynamic_index_in_dim(ids_rows, blk_index * 32 + group_index, 0, keepdims=False),
+            lax.dynamic_index_in_dim(ids_rows, (blk_index ^ 1) * 32 + group_index, 0, keepdims=False),
+        ]
+    )
+    near, *images = lax.optimization_barrier(
+        (near, student_b, unit_teacher, far_teacher, left_ids, text_ids)
+    )
+
     top = near[:2, :, :1152].reshape(2 * rows, 1152)
     bottom = near[2:, :, :1152].reshape(2 * rows, 1152)
-    features = near[:, :, 1152:]
     before_top = lax.ppermute(top, AXES, FORTH)
     after_bottom = lax.ppermute(bottom, AXES, BACK)
     before_bottom = lax.ppermute(bottom, AXES, FORTH)
     after_top = lax.ppermute(top, AXES, BACK)
     far_top = lax.ppermute(before_top, AXES, FORTH)
     far_bottom = lax.ppermute(after_bottom, AXES, BACK)
-
-    far_features, far_teacher = from_twin(twin_features), from_twin(teacher_image)
-    both_features = jnp.concatenate([student_features, far_features], axis=0)
-    both_teacher = jnp.concatenate([teacher_image, far_teacher], axis=0)
-    projected = lax.dot_general(
-        both_features, head_weights, (((1,), (1,)), ((), ())), preferred_element_type=jnp.float32
-    )
-    inverse = lax.rsqrt(jnp.sum(projected * projected, axis=-1, keepdims=True) + norm_eps)
-    student = projected * inverse
-    student_b = student.astype(jnp.bfloat16)
-    teacher_b = unit_rows(both_teacher).astype(jnp.bfloat16)
-
-    ids_grid = pair_ids.reshape(4, 2, 2, 2, 16, rows)
-    ids_plane = lax.dynamic_index_in_dim(ids_grid, z, 4, keepdims=False)
-    ids_core = lax.dynamic_index_in_dim(ids_plane, core, 2, keepdims=False)
-    ids_yx = ids_core.transpose(0, 2, 1, 3).reshape(4, 4, rows)
-    ids_xy = ids_core.transpose(1, 2, 0, 3).reshape(4, 4, rows)
-    text_ids = jnp.where(core == 0, ids_yx, ids_xy)
-    place = jnp.where(core == 0, y, xh * 2 + xl)
-
-    def ids_at(step):
-        return lax.dynamic_index_in_dim(text_ids, (place + step) % 4, 0, keepdims=False)
-
-    ids_rows = pair_ids.reshape(512, rows)
-    left_ids = jnp.concatenate(
-        [
-            lax.dynamic_index_in_dim(ids_rows, blk_index * 32 + group_index, 0, keepdims=False),
-            lax.dynamic_index_in_dim(ids_rows, (blk_index ^ 1) * 32 + group_index, 0, keepdims=False),
-        ]
-    )
-    images = (student_b, teacher_b, left_ids.reshape(-1, 1))
-    own_chunks = [(top, ids_at(0)[:2]), (bottom, ids_at(0)[2:])]
-    sums = pair_sums(*images, own_chunks)
-    near_chunks = [
-        (before_top, ids_at(3)[:2]),
-        (after_bottom, ids_at(1)[2:]),
-        (before_bottom, ids_at(3)[2:]),
-        (after_top, ids_at(1)[:2]),
-    ]
+    sums = pair_sums(*images, [(top, 0), (bottom, 1)])
+    near_chunks = [(before_top, 6), (after_bottom, 3), (before_bottom, 7), (after_top, 2)]
     sums = pair_sums(*images, near_chunks, sums)
-    features, sums = lax.optimization_barrier((features, sums))
-    far_chunks = [(far_top, ids_at(2)[:2]), (far_bottom, ids_at(2)[2:])]
+    far_chunks = [(far_top, 4), (far_bottom, 5)]
     pulled, twin_pulled, losses = pair_sums(*images, far_chunks, sums, last=True)
     losses = losses.reshape(-1)
 
     pulled = pulled + from_twin(twin_pulled)
+    features = lax.optimization_barrier(near[:, :, 1152:])
     student, inverse = student[:rows], inverse[:rows]
     grad_student = student_scale / rows * pulled
     grad_projected = (

time: 176 us -> 177 us (level)
  blocking collectives: 28.4 us -> 18.2 us
  waiting for transfers between devices: 50.6 us -> 57 us
  starting transfers between devices: 67.4 us -> 73 us
    all_to_all x2 -> x1, blocking collectives: 28.4 us -> 18.2 us  [exchange(): lax.all_to_all(pieces, AXES, 0, 0, axis_index_groups=groups, tiled=True)]
    all_to_all x4 -> x5, starting transfers between devices: 21.4 us -> 26.6 us  [exchange(): lax.all_to_all(pieces, AXES, 0, 0, axis_index_groups=groups, tiled=True)]
    all_to_all x4 -> x5, waiting for transfers between devices: 46.4 us -> 51.2 us  [exchange(): lax.all_to_all(pieces, AXES, 0, 0, axis_index_groups=groups, tiled=True)]
  transfers between devices with their start and end apart: 15 -> 16, of which waited for: 7 -> 10; matrix products, arithmetic and copies ran while one was open for 5% -> 3% of each run, Pallas kernels for 3% -> 3%
where the time goes in v5:
time: 177 us; the launch traced here: 176 us
  starting transfers between devices  73 us (41%)
  waiting for transfers between devices  57 us (32%)
  blocking collectives  18.2 us (10%)
  Pallas kernels  11.1 us (6%)
  local copies, waits for them, and re-layouts  6.44 us (4%)
  matrix products  5.8 us (3%)
  other arithmetic  3.56 us (2%)
    all_to_all x5, waiting for transfers between devices, exchange(): lax.all_to_all(pieces, AXES, 0, 0, axis_index_groups=groups, tiled=True)  51.2 us
    ppermute x5, starting transfers between devices, from_twin(): return lax.ppermute(shard, AXES, TWIN)  26.9 us
    all_to_all x5, starting transfers between devices, exchange(): lax.all_to_all(pieces, AXES, 0, 0, axis_index_groups=groups, tiled=True)  26.6 us
    all_to_all x1, blocking collectives, exchange(): lax.all_to_all(pieces, AXES, 0, 0, axis_index_groups=groups, tiled=True)  18.2 us
    pallas_call x3, Pallas kernels, pair_sums(): pl.pallas_call(functools.partial(pair_kernel, places, bool(carried), last...  7 us
    ppermute x1, starting transfers between devices, per_device(): after_bottom = lax.ppermute(bottom, AXES, BACK)  4.57 us
    ppermute x1, starting transfers between devices, per_device(): after_top = lax.ppermute(top, AXES, BACK)  4.57 us
    ppermute x1, starting transfers between devices, per_device(): far_bottom = lax.ppermute(after_bottom, AXES, BACK)  4.57 us
  transfers between devices with their start and end apart: 16, of which 10 were waited for; matrix products, arithmetic and copies ran while one was open for 3% of the time, Pallas kernels for 3%

profile of v5, /device:TPU:1, one launch (start us, length us, event | category | flops | bytes accessed | tf_op | source)
XLA Modules:
  0.0 176.4 jit_solution(16275217889968460985)
XLA Ops:
  0.6 2.7 %shard_map.102 = (bf16[4,128,1920]{2,1,0:T(8,128)(2,1)}, bf16[128,1152]{1,0:T(8,128)(2,1)}) custom-call(bf16[128,1152]{1,0:T(8,128)(2,1)} %texts_ref.1, bf16[128,768]{1,0:T(8,128)(2,1)} %features_ref.1, bf16[128,1152]{1,0:T(8,128)(2,1)} %teacher_ref.1), custom_call_target="tpu_custom_call" | custom-call | flops 1179648 | bytes 2949120 | tf_op jit(solution)/shard_map/pallas_call | solution.py:127
  3.3 8.7 %collective-permute-start = (bf16[128,768]{1,0:T(8,128)(2,1)}, bf16[128,768]{1,0:T(8,128)(2,1)S(1)}, u32[]{:S(2)}, u32[]{:S(2)}) collective-permute-start(bf16[128,768]{1,0:T(8,128)(2,1)} %features_ref.1), channel_id=1, source_target_pairs={{0,32},{1,33},{2,34},{3,35},{4,36},{5,37},{6,38},{7,39},{8,40},{9,... | collective-permute-start | bytes 589832 | tf_op jit(solution)/shard_map/ppermute | solution.py:91
  12.1 2.1 %collective-permute-start.1 = (bf16[128,1152]{1,0:T(8,128)(2,1)}, bf16[128,1152]{1,0:T(8,128)(2,1)S(1)}, u32[]{:S(2)}, u32[]{:S(2)}) collective-permute-start(bf16[128,1152]{1,0:T(8,128)(2,1)} %get-tuple-element.29.refs_1_), channel_id=1, source_target_pairs={{0,32},{1,33},{2,34},{3,35},{4,36},{5,37},{6,38},{7,39},{8,40},{9,... | collective-permute-start | bytes 884744 | tf_op jit(solution)/shard_map/ppermute | solution.py:91
  14.1 4.4 %all-to-all-start = ((bf16[4,128,1920]{2,1,0:T(8,128)(2,1)}), bf16[4,128,1920]{2,1,0:T(8,128)(2,1)}, u32[]{:S(2)}, u32[]{:S(2)}) async-start(bf16[4,128,1920]{2,1,0:T(8,128)(2,1)} %get-tuple-element.25), calls=%async_computation | async-start | bytes 3932160 | tf_op jit(solution)/shard_map/all_to_all | solution.py:83
  22.4 10.9 %all-to-all-done = bf16[4,128,1920]{2,1,0:T(8,128)(2,1)} async-done(((bf16[4,128,1920]{2,1,0:T(8,128)(2,1)}), bf16[4,128,1920]{2,1,0:T(8,128)(2,1)}, u32[]{:S(2)}, u32[]{:S(2)}) %all-to-all-start) | async-done | bytes 1966112 | tf_op jit(solution)/shard_map/all_to_all | solution.py:83
  34.6 1.9 %collective-permute-start.2 = (bf16[256,1152]{1,0:T(8,128)(2,1)S(1)}, bf16[256,1152]{1,0:T(8,128)(2,1)S(1)}, u32[]{:S(2)}, u32[]{:S(2)}) collective-permute-start(bf16[256,1152]{1,0:T(8,128)(2,1)S(1)} %bitcast.36), channel_id=1, source_target_pairs={{0,128},{1,129},{2,130},{3,131},{4,132},{5,133},{6,134},{7,135},{8... | collective-permute-start | bytes 1769480 | tf_op jit(solution)/shard_map/ppermute | solution.py:343
  36.6 4.6 %collective-permute-start.4 = (bf16[256,1152]{1,0:T(8,128)(2,1)S(1)}, bf16[256,1152]{1,0:T(8,128)(2,1)S(1)}, u32[]{:S(2)}, u32[]{:S(2)}) collective-permute-start(bf16[256,1152]{1,0:T(8,128)(2,1)S(1)} %bitcast.39), channel_id=1, source_target_pairs={{0,384},{1,385},{2,386},{3,387},{4,388},{5,389},{6,390},{7,391},{8... | collective-permute-start | bytes 1769480 | tf_op jit(solution)/shard_map/ppermute | solution.py:344
  41.2 1.9 %collective-permute-start.6 = (bf16[256,1152]{1,0:T(8,128)(2,1)S(1)}, bf16[256,1152]{1,0:T(8,128)(2,1)S(1)}, u32[]{:S(2)}, u32[]{:S(2)}) collective-permute-start(bf16[256,1152]{1,0:T(8,128)(2,1)S(1)} %bitcast.40), channel_id=1, source_target_pairs={{0,128},{1,129},{2,130},{3,131},{4,132},{5,133},{6,134},{7,135},{8... | collective-permute-start | bytes 1769480 | tf_op jit(solution)/shard_map/ppermute | solution.py:345
  43.1 4.6 %collective-permute-start.7 = (bf16[256,1152]{1,0:T(8,128)(2,1)S(1)}, bf16[256,1152]{1,0:T(8,128)(2,1)S(1)}, u32[]{:S(2)}, u32[]{:S(2)}) collective-permute-start(bf16[256,1152]{1,0:T(8,128)(2,1)S(1)} %bitcast.37), channel_id=1, source_target_pairs={{0,384},{1,385},{2,386},{3,387},{4,388},{5,389},{6,390},{7,391},{8... | collective-permute-start | bytes 1769480 | tf_op jit(solution)/shard_map/ppermute | solution.py:346
  49.6 4.6 %collective-permute-start.5 = (bf16[256,1152]{1,0:T(8,128)(2,1)S(1)}, bf16[256,1152]{1,0:T(8,128)(2,1)S(1)}, u32[]{:S(2)}, u32[]{:S(2)}) collective-permute-start(bf16[256,1152]{1,0:T(8,128)(2,1)S(1)} %collective-permute-done.4.refs_6_), channel_id=1, source_target_pairs={{0,384},{1,385},{2,386},{3,387},{4,388},{5,389},{6,390},{7,391},{8... | collective-permute-start | bytes 1769480 | tf_op jit(solution)/shard_map/ppermute | solution.py:348
  56.0 3.4 %shard_map.104 = (f32[256,1152]{1,0:T(8,128)S(1)}, f32[256,1]{1,0:T(8,128)S(1)}) custom-call(bf16[256,1152]{1,0:T(8,128)(2,1)S(1)} %get-tuple-element.28.refs_0_, bf16[128,1152]{1,0:T(8,128)(2,1)S(1)} %copy-done.3, bf16[128,1152]{1,0:T(8,128)(2,1)S(1)} %collective-permute-done.1.refs_2_, s32[2,128]{1,0:T(2,128)S(1)} %pad_add_fusion.refs_3_, ...), custom_call_target="tpu_custom_call" | custom-call | flops 1811939328 | bytes 2359296 | tf_op jit(solution)/shard_map/pallas_call | solution.py:246
  62.8 5.5 %collective-permute-start.8 = (f32[128,1152]{1,0:T(8,128)S(1)}, f32[128,1152]{1,0:T(8,128)S(1)}, u32[]{:S(2)}, u32[]{:S(2)}) collective-permute-start(f32[128,1152]{1,0:T(8,128)S(1)} %get-tuple-element.40), channel_id=1, source_target_pairs={{0,32},{1,33},{2,34},{3,35},{4,36},{5,37},{6,38},{7,39},{8,40},{9,... | collective-permute-start | bytes 1769480 | tf_op jit(solution)/shard_map/ppermute | solution.py:91
  70.1 2.0 %fusion.2 = bf16[1280,128]{1,0:T(8,128)(2,1)} fusion(s32[1280]{0:T(1024)S(1)} %fusion.40, f32[256,1152]{1,0:T(8,128)S(1)} %copy-done.4, f32[128]{0:T(128)S(1)} %multiply_reduce_fusion.1, f32[128]{0:T(128)S(1)} %slice-done, f32[128,1152]{1,0:T(8,128)S(1)} %get-tuple-element.39, f32[128,1152]{1,0:T(8,128)S(1)} %collective-permute-done.8), kind=kOutput, calls=%fused_computation.3 | convolution fusion | flops 380010496 | bytes 2106368 | tf_op jit(solution)/shard_map/dot_general | solution.py:364
  72.1 4.7 %all-to-all-start.1 = ((bf16[4,320,128]{2,1,0:T(8,128)(2,1)}), bf16[4,320,128]{2,1,0:T(8,128)(2,1)S(1)}, u32[]{:S(2)}, u32[]{:S(2)}) async-start(bf16[4,320,128]{2,1,0:T(8,128)(2,1)} %bitcast.9), calls=%async_computation.1 | async-start | bytes 655360 | tf_op jit(solution)/shard_map/all_to_all | solution.py:83
  78.0 4.7 %all-to-all-done.1 = bf16[4,320,128]{2,1,0:T(8,128)(2,1)S(1)} async-done(((bf16[4,320,128]{2,1,0:T(8,128)(2,1)}), bf16[4,320,128]{2,1,0:T(8,128)(2,1)S(1)}, u32[]{:S(2)}, u32[]{:S(2)}) %all-to-all-start.1) | async-done | bytes 327712 | tf_op jit(solution)/shard_map/all_to_all | solution.py:83
  84.0 4.2 %all-to-all-start.2 = ((f32[4,80,768]{2,1,0:T(8,128)}), f32[4,80,768]{2,1,0:T(8,128)}, u32[]{:S(2)}, u32[]{:S(2)}) async-start(f32[4,80,768]{2,1,0:T(8,128)} %bitcast.43), calls=%async_computation.2 | async-start | bytes 1966080 | tf_op jit(solution)/shard_map/all_to_all | solution.py:83
  88.4 9.3 %all-to-all-done.2 = f32[4,80,768]{2,1,0:T(8,128)} async-done(((f32[4,80,768]{2,1,0:T(8,128)}), f32[4,80,768]{2,1,0:T(8,128)}, u32[]{:S(2)}, u32[]{:S(2)}) %all-to-all-start.2) | async-done | bytes 983072 | tf_op jit(solution)/shard_map/all_to_all | solution.py:83
  99.1 3.8 %collective-permute-start.9 = (f32[88,384]{1,0:T(8,128)S(1)}, f32[88,384]{1,0:T(8,128)S(1)}, u32[]{:S(2)}, u32[]{:S(2)}) collective-permute-start(f32[88,384]{1,0:T(8,128)S(1)} %select_maximum_fusion), channel_id=1, source_target_pairs={{0,32},{1,33},{2,34},{3,35},{4,36},{5,37},{6,38},{7,39},{8,40},{9,... | collective-permute-start | bytes 405512 | tf_op jit(solution)/shard_map/ppermute | solution.py:91
  104.6 9.6 %all-to-all-start.3 = ((f32[16,16,128]{2,1,0:T(8,128)}), f32[16,16,128]{2,1,0:T(8,128)S(1)}, u32[]{:S(2)}, u32[]{:S(2)}) async-start(f32[16,16,128]{2,1,0:T(8,128)} %pad.22), calls=%async_computation.3 | async-start | bytes 262144 | tf_op jit(solution)/shard_map/all_to_all | solution.py:83
  114.2 12.0 %all-to-all-done.3 = f32[16,16,128]{2,1,0:T(8,128)S(1)} async-done(((f32[16,16,128]{2,1,0:T(8,128)}), f32[16,16,128]{2,1,0:T(8,128)S(1)}, u32[]{:S(2)}, u32[]{:S(2)}) %all-to-all-start.3) | async-done | bytes 131104 | tf_op jit(solution)/shard_map/all_to_all | solution.py:83
  126.4 18.2 %all_to_all.30 = bf16[16,5,384]{2,1,0:T(8,128)(2,1)S(1)} all-to-all(bf16[16,5,384]{2,1,0:T(8,128)(2,1)S(1)} %broadcast_in_dim.9), channel_id=1, replica_groups={{0,1,2,3,4,5,6,7,8,9,10,11,12,13,14,15},{32,33,34,35,36,37,38,39,40,41,..., dimensions={0} | all-to-all | bytes 122880 | tf_op jit(solution)/shard_map/all_to_all | solution.py:83
  145.9 3.7 %all-to-all-start.5 = ((bf16[16,96,384]{2,1,0:T(8,128)(2,1)}), bf16[16,96,384]{2,1,0:T(8,128)(2,1)S(1)}, u32[]{:S(2)}, u32[]{:S(2)}) async-start(bf16[16,96,384]{2,1,0:T(8,128)(2,1)} %broadcast_in_dim.11), calls=%async_computation.5 | async-start | bytes 2359296 | tf_op jit(solution)/shard_map/all_to_all | solution.py:83
  149.7 14.3 %all-to-all-done.5 = bf16[16,96,384]{2,1,0:T(8,128)(2,1)S(1)} async-done(((bf16[16,96,384]{2,1,0:T(8,128)(2,1)}), bf16[16,96,384]{2,1,0:T(8,128)(2,1)S(1)}, u32[]{:S(2)}, u32[]{:S(2)}) %all-to-all-start.5) | async-done | bytes 1179680 | tf_op jit(solution)/shard_map/all_to_all | solution.py:83
  165.9 6.8 %collective-permute-start.10 = (bf16[1296,384]{1,0:T(8,128)(2,1)S(1)}, bf16[1296,384]{1,0:T(8,128)(2,1)S(1)}, u32[]{:S(2)}, u32[]{:S(2)}) collective-permute-start(bf16[1296,384]{1,0:T(8,128)(2,1)S(1)} %pad_maximum_fusion.half_ref), channel_id=1, source_target_pairs={{0,32},{1,33},{2,34},{3,35},{4,36},{5,37},{6,38},{7,39},{8,40},{9,... | collective-permute-start | bytes 2985992 | tf_op jit(solution)/shard_map/ppermute | solution.py:91
  (71 shorter events, 26.7 us)
Async XLA Ops:
  0.6 19.8 %copy-start = (bf16[1152,768]{1,0:T(8,128)(2,1)S(1)}, bf16[1152,768]{1,0:T(8,128)(2,1)}, u32[]{:S(2)}) copy-start(bf16[1152,768]{1,0:T(8,128)(2,1)} %param.11) | copy-start | bytes 5308420
  3.3 17.1 %collective-permute-start = (bf16[128,768]{1,0:T(8,128)(2,1)}, bf16[128,768]{1,0:T(8,128)(2,1)S(1)}, u32[]{:S(2)}, u32[]{:S(2)}) collective-permute-start(bf16[128,768]{1,0:T(8,128)(2,1)} %features_ref.1), channel_id=1, source_target_pairs={{0,32},{1,33},{2,34},{3,35},{4,36},{5,37},{6,38},{7,39},{8,40},{9,... | collective-permute-start | bytes 589832 | tf_op jit(solution)/shard_map/ppermute | solution.py:91
  12.1 8.3 %copy-start.5 = (bf16[128,768]{1,0:T(8,128)(2,1)S(1)}, bf16[128,768]{1,0:T(8,128)(2,1)}, u32[]{:S(2)}) copy-start(bf16[128,768]{1,0:T(8,128)(2,1)} %features_ref.1) | copy-start | bytes 589828
  12.1 10.3 %collective-permute-start.1 = (bf16[128,1152]{1,0:T(8,128)(2,1)}, bf16[128,1152]{1,0:T(8,128)(2,1)S(1)}, u32[]{:S(2)}, u32[]{:S(2)}) collective-permute-start(bf16[128,1152]{1,0:T(8,128)(2,1)} %get-tuple-element.29.refs_1_), channel_id=1, source_target_pairs={{0,32},{1,33},{2,34},{3,35},{4,36},{5,37},{6,38},{7,39},{8,40},{9,... | collective-permute-start | bytes 884744 | tf_op jit(solution)/shard_map/ppermute | solution.py:91
  14.1 19.2 %all-to-all-start = ((bf16[4,128,1920]{2,1,0:T(8,128)(2,1)}), bf16[4,128,1920]{2,1,0:T(8,128)(2,1)}, u32[]{:S(2)}, u32[]{:S(2)}) async-start(bf16[4,128,1920]{2,1,0:T(8,128)(2,1)} %get-tuple-element.25), calls=%async_computation | async-start | bytes 3932160 | tf_op jit(solution)/shard_map/all_to_all | solution.py:83
  21.2 47.2 %copy-start.6 = (f32[256]{0:T(256)}, f32[256]{0:T(256)S(1)}, u32[]{:S(2)}) copy-start(f32[256]{0:T(256)S(1)} %add_rsqrt_fusion) | copy-start | bytes 3076
  22.4 31.8 %copy-start.3 = (bf16[128,1152]{1,0:T(8,128)(2,1)S(1)}, bf16[128,1152]{1,0:T(8,128)(2,1)}, u32[]{:S(2)}) copy-start(bf16[128,1152]{1,0:T(8,128)(2,1)} %get-tuple-element.29.refs_1_) | copy-start | bytes 884740
  34.6 13.0 %collective-permute-start.2 = (bf16[256,1152]{1,0:T(8,128)(2,1)S(1)}, bf16[256,1152]{1,0:T(8,128)(2,1)S(1)}, u32[]{:S(2)}, u32[]{:S(2)}) collective-permute-start(bf16[256,1152]{1,0:T(8,128)(2,1)S(1)} %bitcast.36), channel_id=1, source_target_pairs={{0,128},{1,129},{2,130},{3,131},{4,132},{5,133},{6,134},{7,135},{8... | collective-permute-start | bytes 1769480 | tf_op jit(solution)/shard_map/ppermute | solution.py:343
  36.6 13.0 %collective-permute-start.4 = (bf16[256,1152]{1,0:T(8,128)(2,1)S(1)}, bf16[256,1152]{1,0:T(8,128)(2,1)S(1)}, u32[]{:S(2)}, u32[]{:S(2)}) collective-permute-start(bf16[256,1152]{1,0:T(8,128)(2,1)S(1)} %bitcast.39), channel_id=1, source_target_pairs={{0,384},{1,385},{2,386},{3,387},{4,388},{5,389},{6,390},{7,391},{8... | collective-permute-start | bytes 1769480 | tf_op jit(solution)/shard_map/ppermute | solution.py:344
  41.2 14.9 %collective-permute-start.6 = (bf16[256,1152]{1,0:T(8,128)(2,1)S(1)}, bf16[256,1152]{1,0:T(8,128)(2,1)S(1)}, u32[]{:S(2)}, u32[]{:S(2)}) collective-permute-start(bf16[256,1152]{1,0:T(8,128)(2,1)S(1)} %bitcast.40), channel_id=1, source_target_pairs={{0,128},{1,129},{2,130},{3,131},{4,132},{5,133},{6,134},{7,135},{8... | collective-permute-start | bytes 1769480 | tf_op jit(solution)/shard_map/ppermute | solution.py:345
  43.1 12.9 %collective-permute-start.7 = (bf16[256,1152]{1,0:T(8,128)(2,1)S(1)}, bf16[256,1152]{1,0:T(8,128)(2,1)S(1)}, u32[]{:S(2)}, u32[]{:S(2)}) collective-permute-start(bf16[256,1152]{1,0:T(8,128)(2,1)S(1)} %bitcast.37), channel_id=1, source_target_pairs={{0,384},{1,385},{2,386},{3,387},{4,388},{5,389},{6,390},{7,391},{8... | collective-permute-start | bytes 1769480 | tf_op jit(solution)/shard_map/ppermute | solution.py:346
  47.7 12.1 %collective-permute-start.3 = (bf16[256,1152]{1,0:T(8,128)(2,1)S(1)}, bf16[256,1152]{1,0:T(8,128)(2,1)S(1)}, u32[]{:S(2)}, u32[]{:S(2)}) collective-permute-start(bf16[256,1152]{1,0:T(8,128)(2,1)S(1)} %collective-permute-done.2.refs_5_), channel_id=1, source_target_pairs={{0,128},{1,129},{2,130},{3,131},{4,132},{5,133},{6,134},{7,135},{8... | collective-permute-start | bytes 1769480 | tf_op jit(solution)/shard_map/ppermute | solution.py:347
  49.6 11.4 %collective-permute-start.5 = (bf16[256,1152]{1,0:T(8,128)(2,1)S(1)}, bf16[256,1152]{1,0:T(8,128)(2,1)S(1)}, u32[]{:S(2)}, u32[]{:S(2)}) collective-permute-start(bf16[256,1152]{1,0:T(8,128)(2,1)S(1)} %collective-permute-done.4.refs_6_), channel_id=1, source_target_pairs={{0,384},{1,385},{2,386},{3,387},{4,388},{5,389},{6,390},{7,391},{8... | collective-permute-start | bytes 1769480 | tf_op jit(solution)/shard_map/ppermute | solution.py:348
  61.0 9.0 %copy-start.4 = (f32[256,1152]{1,0:T(8,128)S(1)}, f32[256,1152]{1,0:T(8,128)}, u32[]{:S(2)}) copy-start(f32[256,1152]{1,0:T(8,128)} %get-tuple-element.47) | copy-start | bytes 3538948
  62.8 7.1 %collective-permute-start.8 = (f32[128,1152]{1,0:T(8,128)S(1)}, f32[128,1152]{1,0:T(8,128)S(1)}, u32[]{:S(2)}, u32[]{:S(2)}) collective-permute-start(f32[128,1152]{1,0:T(8,128)S(1)} %get-tuple-element.40), channel_id=1, source_target_pairs={{0,32},{1,33},{2,34},{3,35},{4,36},{5,37},{6,38},{7,39},{8,40},{9,... | collective-permute-start | bytes 1769480 | tf_op jit(solution)/shard_map/ppermute | solution.py:91
  68.4 1.7 slice-start
  72.1 10.6 %all-to-all-start.1 = ((bf16[4,320,128]{2,1,0:T(8,128)(2,1)}), bf16[4,320,128]{2,1,0:T(8,128)(2,1)S(1)}, u32[]{:S(2)}, u32[]{:S(2)}) async-start(bf16[4,320,128]{2,1,0:T(8,128)(2,1)} %bitcast.9), calls=%async_computation.1 | async-start | bytes 655360 | tf_op jit(solution)/shard_map/all_to_all | solution.py:83
  84.0 13.7 %all-to-all-start.2 = ((f32[4,80,768]{2,1,0:T(8,128)}), f32[4,80,768]{2,1,0:T(8,128)}, u32[]{:S(2)}, u32[]{:S(2)}) async-start(f32[4,80,768]{2,1,0:T(8,128)} %bitcast.43), calls=%async_computation.2 | async-start | bytes 1966080 | tf_op jit(solution)/shard_map/all_to_all | solution.py:83
  88.3 38.0 %copy-start.1 = (f32[36,768]{1,0:T(8,128)S(1)}, f32[36,768]{1,0:T(8,128)}, u32[]{:S(2)}) copy-start(f32[36,768]{1,0:T(8,128)} %second_ref.1) | copy-start | bytes 331780
  88.3 38.0 %copy-start.2 = (f32[36,768]{1,0:T(8,128)S(1)}, f32[36,768]{1,0:T(8,128)}, u32[]{:S(2)}) copy-start(f32[36,768]{1,0:T(8,128)} %first_ref.1) | copy-start | bytes 331780
  99.1 4.8 %collective-permute-start.9 = (f32[88,384]{1,0:T(8,128)S(1)}, f32[88,384]{1,0:T(8,128)S(1)}, u32[]{:S(2)}, u32[]{:S(2)}) collective-permute-start(f32[88,384]{1,0:T(8,128)S(1)} %select_maximum_fusion), channel_id=1, source_target_pairs={{0,32},{1,33},{2,34},{3,35},{4,36},{5,37},{6,38},{7,39},{8,40},{9,... | collective-permute-start | bytes 405512 | tf_op jit(solution)/shard_map/ppermute | solution.py:91
  104.6 21.7 %all-to-all-start.3 = ((f32[16,16,128]{2,1,0:T(8,128)}), f32[16,16,128]{2,1,0:T(8,128)S(1)}, u32[]{:S(2)}, u32[]{:S(2)}) async-start(f32[16,16,128]{2,1,0:T(8,128)} %pad.22), calls=%async_computation.3 | async-start | bytes 262144 | tf_op jit(solution)/shard_map/all_to_all | solution.py:83
  145.9 18.0 %all-to-all-start.5 = ((bf16[16,96,384]{2,1,0:T(8,128)(2,1)}), bf16[16,96,384]{2,1,0:T(8,128)(2,1)S(1)}, u32[]{:S(2)}, u32[]{:S(2)}) async-start(bf16[16,96,384]{2,1,0:T(8,128)(2,1)} %broadcast_in_dim.11), calls=%async_computation.5 | async-start | bytes 2359296 | tf_op jit(solution)/shard_map/all_to_all | solution.py:83
  165.9 9.0 %collective-permute-start.10 = (bf16[1296,384]{1,0:T(8,128)(2,1)S(1)}, bf16[1296,384]{1,0:T(8,128)(2,1)S(1)}, u32[]{:S(2)}, u32[]{:S(2)}) collective-permute-start(bf16[1296,384]{1,0:T(8,128)(2,1)S(1)} %pad_maximum_fusion.half_ref), channel_id=1, source_target_pairs={{0,32},{1,33},{2,34},{3,35},{4,36},{5,37},{6,38},{7,39},{8,40},{9,... | collective-permute-start | bytes 2985992 | tf_op jit(solution)/shard_map/ppermute | solution.py:91

commit v6 on v5

--- a/solution.py
+++ b/solution.py
@@ -214,10 +214,10 @@
         own_ref, twin_ref, losses_ref, pulled_ref = rest[-4:]
     if carried:
         pulled_ref[...] = rest[0][...]
-        losses_ref[...] = rest[1][...]
+        total = rest[1][...]
     else:
         pulled_ref[...] = jnp.zeros_like(pulled_ref)
-        losses_ref[...] = jnp.zeros_like(losses_ref)
+        total = jnp.zeros(losses_ref.shape, jnp.float32)
     teacher = jnp.concatenate([own_teacher_ref[...], twin_teacher_ref[...]], axis=0)
     left_ids = jnp.concatenate(
         [jnp.transpose(jnp.broadcast_to(left_ref[i : i + 1, :], (128, 128))) for i in range(2)], axis=0
@@ -227,12 +227,16 @@
         losses, coeff = pair_terms(
             student_ref[...], teacher, left_ids, texts, ids_ref[place : place + 1, :]
         )
-        losses_ref[...] += losses
+        total += losses
         pulled_ref[...] += jnp.dot(coeff, texts, preferred_element_type=jnp.float32)
-    if last:
-        half = pulled_ref.shape[0] // 2
-        own_ref[...] = pulled_ref[:half]
-        twin_ref[...] = pulled_ref[half:]
+    if not last:
+        losses_ref[...] = total
+        return
+    own_ref[...] = pulled_ref[:128]
+    twin_ref[...] = pulled_ref[128:]
+    for i in range(2):
+        column = jnp.broadcast_to(total[i * 128 : i * 128 + 128], (128, 128))
+        losses_ref[i : i + 1, :] = jnp.transpose(column)[:1]
 
 
 def pair_sums(student_rows, own_teacher, twin_teacher, left_ids, text_ids, chunks, carried=(), last=False):
@@ -245,7 +249,7 @@
     sums = (jax.ShapeDtypeStruct((rows // parts, width), jnp.float32),) * parts
     return pl.pallas_call(
         functools.partial(pair_kernel, places, bool(carried), last),
-        out_shape=(*sums, jax.ShapeDtypeStruct((rows, 1), jnp.float32)),
+        out_shape=(*sums, jax.ShapeDtypeStruct((2, 128) if last else (rows, 1), jnp.float32)),
         in_specs=[whole] * len(operands),
         out_specs=(whole,) * (len(sums) + 1),
         scratch_shapes=[pltpu.VMEM((rows, width), jnp.float32)] * last,
@@ -349,12 +353,12 @@
     sums = pair_sums(*images, [(top, 0), (bottom, 1)])
     near_chunks = [(before_top, 6), (after_bottom, 3), (before_bottom, 7), (after_top, 2)]
     sums = pair_sums(*images, near_chunks, sums)
+    features = near[:, :, 1152:]
+    features, sums = lax.optimization_barrier((features, sums))
     far_chunks = [(far_top, 4), (far_bottom, 5)]
     pulled, twin_pulled, losses = pair_sums(*images, far_chunks, sums, last=True)
-    losses = losses.reshape(-1)
 
     pulled = pulled + from_twin(twin_pulled)
-    features = lax.optimization_barrier(near[:, :, 1152:])
     student, inverse = student[:rows], inverse[:rows]
     grad_student = student_scale / rows * pulled
     grad_projected = (
@@ -373,10 +377,10 @@
     )
     core_grad = jnp.sum(exchange(line_grad.reshape(4, 80, 768), SECOND), axis=0)
     left, right = core_grad[:, :384], core_grad[:, 384:]
-    other_losses = jnp.pad(losses[rows:].reshape(1, rows), ((0, 7), (0, 256)))
+    other_losses = jnp.pad(losses[1:], ((0, 7), (0, 256)))
     arrived = from_twin(jnp.concatenate([jnp.where(core == 0, right, left), other_losses], axis=0))
     chip_grad = jnp.where(core == 0, left, right) + arrived[:80]
-    row_loss = (losses[:rows] + arrived[80, :rows]) / rows
+    row_loss = (losses[0] + arrived[80, :rows]) / rows
 
     column_grad = jnp.pad(chip_grad.reshape(16, 15, 128), ((0, 0), (0, 1), (0, 0)))
     own_grad = jnp.sum(exchange(column_grad, COLUMN), axis=0)[:15].reshape(5, 384)

time: 177 us -> 178 us (level)
  blocking collectives: 18.2 us -> 28.5 us
  waiting for transfers between devices: 57 us -> 51.2 us
  starting transfers between devices: 73 us -> 68.5 us
    all_to_all x1 -> x2, blocking collectives: 18.2 us -> 28.5 us  [exchange(): lax.all_to_all(pieces, AXES, 0, 0, axis_index_groups=groups, tiled=True)]
    all_to_all x5 -> x4, starting transfers between devices: 26.6 us -> 21.9 us  [exchange(): lax.all_to_all(pieces, AXES, 0, 0, axis_index_groups=groups, tiled=True)]
    all_to_all x5 -> x4, waiting for transfers between devices: 51.2 us -> 46.6 us  [exchange(): lax.all_to_all(pieces, AXES, 0, 0, axis_index_groups=groups, tiled=True)]
  transfers between devices with their start and end apart: 16 -> 15, of which waited for: 10 -> 8; matrix products, arithmetic and copies ran while one was open for 3% -> 3% of each run, Pallas kernels for 3% -> 3%
where the time goes in v6:
time: 178 us; the launch traced here: 177 us
  starting transfers between devices  68.5 us (38%)
  waiting for transfers between devices  51.2 us (29%)
  blocking collectives  28.5 us (16%)
  Pallas kernels  11.1 us (6%)
  local copies, waits for them, and re-layouts  7.63 us (4%)
  matrix products  6.16 us (3%)
  other arithmetic  2.37 us (1%)
    all_to_all x4, waiting for transfers between devices, exchange(): lax.all_to_all(pieces, AXES, 0, 0, axis_index_groups=groups, tiled=True)  46.6 us
    all_to_all x2, blocking collectives, exchange(): lax.all_to_all(pieces, AXES, 0, 0, axis_index_groups=groups, tiled=True)  28.5 us
    ppermute x5, starting transfers between devices, from_twin(): return lax.ppermute(shard, AXES, TWIN)  27.1 us
    all_to_all x4, starting transfers between devices, exchange(): lax.all_to_all(pieces, AXES, 0, 0, axis_index_groups=groups, tiled=True)  21.9 us
    pallas_call x3, Pallas kernels, pair_sums(): pl.pallas_call(functools.partial(pair_kernel, places, bool(carried), last...  6.92 us
    ppermute x1, starting transfers between devices, per_device(): after_bottom = lax.ppermute(bottom, AXES, BACK)  4.57 us
    ppermute x1, starting transfers between devices, per_device(): after_top = lax.ppermute(top, AXES, BACK)  4.57 us
    ppermute x1, starting transfers between devices, per_device(): far_bottom = lax.ppermute(after_bottom, AXES, BACK)  4.57 us
  transfers between devices with their start and end apart: 15, of which 8 were waited for; matrix products, arithmetic and copies ran while one was open for 3% of the time, Pallas kernels for 3%

profile of v6, /device:TPU:1, one launch (start us, length us, event | category | flops | bytes accessed | tf_op | source)
XLA Modules:
  0.0 176.7 jit_solution(11213503368389514682)
XLA Ops:
  0.6 2.7 %shard_map.102 = (bf16[4,128,1920]{2,1,0:T(8,128)(2,1)}, bf16[128,1152]{1,0:T(8,128)(2,1)}) custom-call(bf16[128,1152]{1,0:T(8,128)(2,1)} %texts_ref.1, bf16[128,768]{1,0:T(8,128)(2,1)} %features_ref.1, bf16[128,1152]{1,0:T(8,128)(2,1)} %teacher_ref.1), custom_call_target="tpu_custom_call" | custom-call | flops 1179648 | bytes 2949120 | tf_op jit(solution)/shard_map/pallas_call | solution.py:127
  3.4 8.7 %collective-permute-start = (bf16[128,768]{1,0:T(8,128)(2,1)}, bf16[128,768]{1,0:T(8,128)(2,1)S(1)}, u32[]{:S(2)}, u32[]{:S(2)}) collective-permute-start(bf16[128,768]{1,0:T(8,128)(2,1)} %features_ref.1), channel_id=1, source_target_pairs={{0,32},{1,33},{2,34},{3,35},{4,36},{5,37},{6,38},{7,39},{8,40},{9,... | collective-permute-start | bytes 589832 | tf_op jit(solution)/shard_map/ppermute | solution.py:91
  12.1 2.1 %collective-permute-start.1 = (bf16[128,1152]{1,0:T(8,128)(2,1)}, bf16[128,1152]{1,0:T(8,128)(2,1)S(1)}, u32[]{:S(2)}, u32[]{:S(2)}) collective-permute-start(bf16[128,1152]{1,0:T(8,128)(2,1)} %get-tuple-element.32.refs_1_), channel_id=1, source_target_pairs={{0,32},{1,33},{2,34},{3,35},{4,36},{5,37},{6,38},{7,39},{8,40},{9,... | collective-permute-start | bytes 884744 | tf_op jit(solution)/shard_map/ppermute | solution.py:91
  14.2 4.4 %all-to-all-start = ((bf16[4,128,1920]{2,1,0:T(8,128)(2,1)}), bf16[4,128,1920]{2,1,0:T(8,128)(2,1)}, u32[]{:S(2)}, u32[]{:S(2)}) async-start(bf16[4,128,1920]{2,1,0:T(8,128)(2,1)} %get-tuple-element.28), calls=%async_computation | async-start | bytes 3932160 | tf_op jit(solution)/shard_map/all_to_all | solution.py:83
  22.5 10.9 %all-to-all-done = bf16[4,128,1920]{2,1,0:T(8,128)(2,1)} async-done(((bf16[4,128,1920]{2,1,0:T(8,128)(2,1)}), bf16[4,128,1920]{2,1,0:T(8,128)(2,1)}, u32[]{:S(2)}, u32[]{:S(2)}) %all-to-all-start) | async-done | bytes 1966112 | tf_op jit(solution)/shard_map/all_to_all | solution.py:83
  34.8 1.9 %collective-permute-start.2 = (bf16[256,1152]{1,0:T(8,128)(2,1)S(1)}, bf16[256,1152]{1,0:T(8,128)(2,1)S(1)}, u32[]{:S(2)}, u32[]{:S(2)}) collective-permute-start(bf16[256,1152]{1,0:T(8,128)(2,1)S(1)} %bitcast.31), channel_id=1, source_target_pairs={{0,128},{1,129},{2,130},{3,131},{4,132},{5,133},{6,134},{7,135},{8... | collective-permute-start | bytes 1769480 | tf_op jit(solution)/shard_map/ppermute | solution.py:347
  36.7 4.6 %collective-permute-start.4 = (bf16[256,1152]{1,0:T(8,128)(2,1)S(1)}, bf16[256,1152]{1,0:T(8,128)(2,1)S(1)}, u32[]{:S(2)}, u32[]{:S(2)}) collective-permute-start(bf16[256,1152]{1,0:T(8,128)(2,1)S(1)} %bitcast.34), channel_id=1, source_target_pairs={{0,384},{1,385},{2,386},{3,387},{4,388},{5,389},{6,390},{7,391},{8... | collective-permute-start | bytes 1769480 | tf_op jit(solution)/shard_map/ppermute | solution.py:348
  41.3 1.9 %collective-permute-start.6 = (bf16[256,1152]{1,0:T(8,128)(2,1)S(1)}, bf16[256,1152]{1,0:T(8,128)(2,1)S(1)}, u32[]{:S(2)}, u32[]{:S(2)}) collective-permute-start(bf16[256,1152]{1,0:T(8,128)(2,1)S(1)} %bitcast.35), channel_id=1, source_target_pairs={{0,128},{1,129},{2,130},{3,131},{4,132},{5,133},{6,134},{7,135},{8... | collective-permute-start | bytes 1769480 | tf_op jit(solution)/shard_map/ppermute | solution.py:349
  43.2 4.6 %collective-permute-start.7 = (bf16[256,1152]{1,0:T(8,128)(2,1)S(1)}, bf16[256,1152]{1,0:T(8,128)(2,1)S(1)}, u32[]{:S(2)}, u32[]{:S(2)}) collective-permute-start(bf16[256,1152]{1,0:T(8,128)(2,1)S(1)} %bitcast.32), channel_id=1, source_target_pairs={{0,384},{1,385},{2,386},{3,387},{4,388},{5,389},{6,390},{7,391},{8... | collective-permute-start | bytes 1769480 | tf_op jit(solution)/shard_map/ppermute | solution.py:350
  47.8 1.9 %collective-permute-start.3 = (bf16[256,1152]{1,0:T(8,128)(2,1)S(1)}, bf16[256,1152]{1,0:T(8,128)(2,1)S(1)}, u32[]{:S(2)}, u32[]{:S(2)}) collective-permute-start(bf16[256,1152]{1,0:T(8,128)(2,1)S(1)} %collective-permute-done.2.refs_5_), channel_id=1, source_target_pairs={{0,128},{1,129},{2,130},{3,131},{4,132},{5,133},{6,134},{7,135},{8... | collective-permute-start | bytes 1769480 | tf_op jit(solution)/shard_map/ppermute | solution.py:351
  49.7 4.6 %collective-permute-start.5 = (bf16[256,1152]{1,0:T(8,128)(2,1)S(1)}, bf16[256,1152]{1,0:T(8,128)(2,1)S(1)}, u32[]{:S(2)}, u32[]{:S(2)}) collective-permute-start(bf16[256,1152]{1,0:T(8,128)(2,1)S(1)} %collective-permute-done.4.refs_6_), channel_id=1, source_target_pairs={{0,384},{1,385},{2,386},{3,387},{4,388},{5,389},{6,390},{7,391},{8... | collective-permute-start | bytes 1769480 | tf_op jit(solution)/shard_map/ppermute | solution.py:352
  55.5 1.8 %shard_map.103 = (f32[256,1152]{1,0:T(8,128)S(1)}, f32[256,1]{1,0:T(8,128)S(1)}) custom-call(bf16[256,1152]{1,0:T(8,128)(2,1)S(1)} %get-tuple-element.31.refs_0_, bf16[128,1152]{1,0:T(8,128)(2,1)S(1)} %copy-done.3, bf16[128,1152]{1,0:T(8,128)(2,1)S(1)} %collective-permute-done.1.refs_2_, s32[2,128]{1,0:T(2,128)S(1)} %pad_add_fusion.refs_3_, ...), custom_call_target="tpu_custom_call" | custom-call | flops 905969664 | bytes 1179648 | tf_op jit(solution)/shard_map/pallas_call | solution.py:250
  57.3 3.3 %shard_map.104 = (f32[256,1152]{1,0:T(8,128)S(1)}, f32[256,1]{1,0:T(8,128)S(1)}) custom-call(bf16[256,1152]{1,0:T(8,128)(2,1)S(1)} %get-tuple-element.31.refs_0_, bf16[128,1152]{1,0:T(8,128)(2,1)S(1)} %copy-done.3, bf16[128,1152]{1,0:T(8,128)(2,1)S(1)} %collective-permute-done.1.refs_2_, s32[2,128]{1,0:T(2,128)S(1)} %pad_add_fusion.refs_3_, ...), custom_call_target="tpu_custom_call" | custom-call | flops 1811939328 | bytes 2359296 | tf_op jit(solution)/shard_map/pallas_call | solution.py:250
  62.9 5.5 %collective-permute-start.8 = (f32[128,1152]{1,0:T(8,128)S(1)}, f32[128,1152]{1,0:T(8,128)S(1)}, u32[]{:S(2)}, u32[]{:S(2)}) collective-permute-start(f32[128,1152]{1,0:T(8,128)S(1)} %get-tuple-element.45), channel_id=1, source_target_pairs={{0,32},{1,33},{2,34},{3,35},{4,36},{5,37},{6,38},{7,39},{8,40},{9,... | collective-permute-start | bytes 1769480 | tf_op jit(solution)/shard_map/ppermute | solution.py:91
  71.5 10.4 %all_to_all.30 = bf16[4,320,128]{2,1,0:T(8,128)(2,1)S(1)} all-to-all(bf16[4,320,128]{2,1,0:T(8,128)(2,1)S(1)} %bitcast.40), channel_id=1, replica_groups={{0,64,16,80},{128,192,144,208},{256,320,272,336},{384,448,400,464},{1,6..., dimensions={0} | all-to-all | bytes 655360 | tf_op jit(solution)/shard_map/all_to_all | solution.py:83
  83.2 3.5 %all-to-all-start.2 = ((f32[4,80,768]{2,1,0:T(8,128)}), f32[4,80,768]{2,1,0:T(8,128)S(1)}, u32[]{:S(2)}, u32[]{:S(2)}) async-start(f32[4,80,768]{2,1,0:T(8,128)} %bitcast.37), calls=%async_computation.2 | async-start | bytes 1966080 | tf_op jit(solution)/shard_map/all_to_all | solution.py:83
  86.8 9.3 %all-to-all-done.2 = f32[4,80,768]{2,1,0:T(8,128)S(1)} async-done(((f32[4,80,768]{2,1,0:T(8,128)}), f32[4,80,768]{2,1,0:T(8,128)S(1)}, u32[]{:S(2)}, u32[]{:S(2)}) %all-to-all-start.2) | async-done | bytes 983072 | tf_op jit(solution)/shard_map/all_to_all | solution.py:83
  96.2 4.0 %collective-permute-start.9 = (f32[88,384]{1,0:T(8,128)S(1)}, f32[88,384]{1,0:T(8,128)S(1)}, u32[]{:S(2)}, u32[]{:S(2)}) collective-permute-start(f32[88,384]{1,0:T(8,128)S(1)} %select_maximum_fusion), channel_id=1, source_target_pairs={{0,32},{1,33},{2,34},{3,35},{4,36},{5,37},{6,38},{7,39},{8,40},{9,... | collective-permute-start | bytes 405512 | tf_op jit(solution)/shard_map/ppermute | solution.py:91
  101.9 9.6 %all-to-all-start.3 = ((f32[16,16,128]{2,1,0:T(8,128)}), f32[16,16,128]{2,1,0:T(8,128)S(1)}, u32[]{:S(2)}, u32[]{:S(2)}) async-start(f32[16,16,128]{2,1,0:T(8,128)} %pad.22), calls=%async_computation.3 | async-start | bytes 262144 | tf_op jit(solution)/shard_map/all_to_all | solution.py:83
  111.5 12.0 %all-to-all-done.3 = f32[16,16,128]{2,1,0:T(8,128)S(1)} async-done(((f32[16,16,128]{2,1,0:T(8,128)}), f32[16,16,128]{2,1,0:T(8,128)S(1)}, u32[]{:S(2)}, u32[]{:S(2)}) %all-to-all-start.3) | async-done | bytes 131104 | tf_op jit(solution)/shard_map/all_to_all | solution.py:83
  123.8 18.2 %all_to_all.31 = bf16[16,5,384]{2,1,0:T(8,128)(2,1)S(1)} all-to-all(bf16[16,5,384]{2,1,0:T(8,128)(2,1)S(1)} %broadcast_in_dim.9), channel_id=1, replica_groups={{0,1,2,3,4,5,6,7,8,9,10,11,12,13,14,15},{32,33,34,35,36,37,38,39,40,41,..., dimensions={0} | all-to-all | bytes 122880 | tf_op jit(solution)/shard_map/all_to_all | solution.py:83
  143.3 4.4 %all-to-all-start.5 = ((bf16[16,96,384]{2,1,0:T(8,128)(2,1)}), bf16[16,96,384]{2,1,0:T(8,128)(2,1)}, u32[]{:S(2)}, u32[]{:S(2)}) async-start(bf16[16,96,384]{2,1,0:T(8,128)(2,1)} %broadcast_in_dim.11), calls=%async_computation.5 | async-start | bytes 2359296 | tf_op jit(solution)/shard_map/all_to_all | solution.py:83
  147.7 14.3 %all-to-all-done.5 = bf16[16,96,384]{2,1,0:T(8,128)(2,1)} async-done(((bf16[16,96,384]{2,1,0:T(8,128)(2,1)}), bf16[16,96,384]{2,1,0:T(8,128)(2,1)}, u32[]{:S(2)}, u32[]{:S(2)}) %all-to-all-start.5) | async-done | bytes 1179680 | tf_op jit(solution)/shard_map/all_to_all | solution.py:83
  166.2 6.8 %collective-permute-start.10 = (bf16[1296,384]{1,0:T(8,128)(2,1)S(1)}, bf16[1296,384]{1,0:T(8,128)(2,1)S(1)}, u32[]{:S(2)}, u32[]{:S(2)}) collective-permute-start(bf16[1296,384]{1,0:T(8,128)(2,1)S(1)} %pad_maximum_fusion.half_ref), channel_id=1, source_target_pairs={{0,32},{1,33},{2,34},{3,35},{4,36},{5,37},{6,38},{7,39},{8,40},{9,... | collective-permute-start | bytes 2985992 | tf_op jit(solution)/shard_map/ppermute | solution.py:91
  (70 shorter events, 24.1 us)
Async XLA Ops:
  0.6 19.8 %copy-start = (bf16[1152,768]{1,0:T(8,128)(2,1)S(1)}, bf16[1152,768]{1,0:T(8,128)(2,1)}, u32[]{:S(2)}) copy-start(bf16[1152,768]{1,0:T(8,128)(2,1)} %param.11) | copy-start | bytes 5308420
  3.4 17.1 %collective-permute-start = (bf16[128,768]{1,0:T(8,128)(2,1)}, bf16[128,768]{1,0:T(8,128)(2,1)S(1)}, u32[]{:S(2)}, u32[]{:S(2)}) collective-permute-start(bf16[128,768]{1,0:T(8,128)(2,1)} %features_ref.1), channel_id=1, source_target_pairs={{0,32},{1,33},{2,34},{3,35},{4,36},{5,37},{6,38},{7,39},{8,40},{9,... | collective-permute-start | bytes 589832 | tf_op jit(solution)/shard_map/ppermute | solution.py:91
  12.1 8.3 %copy-start.5 = (bf16[128,768]{1,0:T(8,128)(2,1)S(1)}, bf16[128,768]{1,0:T(8,128)(2,1)}, u32[]{:S(2)}) copy-start(bf16[128,768]{1,0:T(8,128)(2,1)} %features_ref.1) | copy-start | bytes 589828
  12.1 10.3 %collective-permute-start.1 = (bf16[128,1152]{1,0:T(8,128)(2,1)}, bf16[128,1152]{1,0:T(8,128)(2,1)S(1)}, u32[]{:S(2)}, u32[]{:S(2)}) collective-permute-start(bf16[128,1152]{1,0:T(8,128)(2,1)} %get-tuple-element.32.refs_1_), channel_id=1, source_target_pairs={{0,32},{1,33},{2,34},{3,35},{4,36},{5,37},{6,38},{7,39},{8,40},{9,... | collective-permute-start | bytes 884744 | tf_op jit(solution)/shard_map/ppermute | solution.py:91
  14.2 19.2 %all-to-all-start = ((bf16[4,128,1920]{2,1,0:T(8,128)(2,1)}), bf16[4,128,1920]{2,1,0:T(8,128)(2,1)}, u32[]{:S(2)}, u32[]{:S(2)}) async-start(bf16[4,128,1920]{2,1,0:T(8,128)(2,1)} %get-tuple-element.28), calls=%async_computation | async-start | bytes 3932160 | tf_op jit(solution)/shard_map/all_to_all | solution.py:83
  21.3 47.2 %copy-start.6 = (f32[256]{0:T(256)}, f32[256]{0:T(256)S(1)}, u32[]{:S(2)}) copy-start(f32[256]{0:T(256)S(1)} %add_rsqrt_fusion) | copy-start | bytes 3076
  33.4 22.1 %copy-start.3 = (bf16[128,1152]{1,0:T(8,128)(2,1)S(1)}, bf16[128,1152]{1,0:T(8,128)(2,1)}, u32[]{:S(2)}) copy-start(bf16[128,1152]{1,0:T(8,128)(2,1)} %get-tuple-element.32.refs_1_) | copy-start | bytes 884740
  34.8 13.0 %collective-permute-start.2 = (bf16[256,1152]{1,0:T(8,128)(2,1)S(1)}, bf16[256,1152]{1,0:T(8,128)(2,1)S(1)}, u32[]{:S(2)}, u32[]{:S(2)}) collective-permute-start(bf16[256,1152]{1,0:T(8,128)(2,1)S(1)} %bitcast.31), channel_id=1, source_target_pairs={{0,128},{1,129},{2,130},{3,131},{4,132},{5,133},{6,134},{7,135},{8... | collective-permute-start | bytes 1769480 | tf_op jit(solution)/shard_map/ppermute | solution.py:347
  36.7 13.0 %collective-permute-start.4 = (bf16[256,1152]{1,0:T(8,128)(2,1)S(1)}, bf16[256,1152]{1,0:T(8,128)(2,1)S(1)}, u32[]{:S(2)}, u32[]{:S(2)}) collective-permute-start(bf16[256,1152]{1,0:T(8,128)(2,1)S(1)} %bitcast.34), channel_id=1, source_target_pairs={{0,384},{1,385},{2,386},{3,387},{4,388},{5,389},{6,390},{7,391},{8... | collective-permute-start | bytes 1769480 | tf_op jit(solution)/shard_map/ppermute | solution.py:348
  41.3 16.0 %collective-permute-start.6 = (bf16[256,1152]{1,0:T(8,128)(2,1)S(1)}, bf16[256,1152]{1,0:T(8,128)(2,1)S(1)}, u32[]{:S(2)}, u32[]{:S(2)}) collective-permute-start(bf16[256,1152]{1,0:T(8,128)(2,1)S(1)} %bitcast.35), channel_id=1, source_target_pairs={{0,128},{1,129},{2,130},{3,131},{4,132},{5,133},{6,134},{7,135},{8... | collective-permute-start | bytes 1769480 | tf_op jit(solution)/shard_map/ppermute | solution.py:349
  43.2 14.1 %collective-permute-start.7 = (bf16[256,1152]{1,0:T(8,128)(2,1)S(1)}, bf16[256,1152]{1,0:T(8,128)(2,1)S(1)}, u32[]{:S(2)}, u32[]{:S(2)}) collective-permute-start(bf16[256,1152]{1,0:T(8,128)(2,1)S(1)} %bitcast.32), channel_id=1, source_target_pairs={{0,384},{1,385},{2,386},{3,387},{4,388},{5,389},{6,390},{7,391},{8... | collective-permute-start | bytes 1769480 | tf_op jit(solution)/shard_map/ppermute | solution.py:350
  47.8 12.9 %collective-permute-start.3 = (bf16[256,1152]{1,0:T(8,128)(2,1)S(1)}, bf16[256,1152]{1,0:T(8,128)(2,1)S(1)}, u32[]{:S(2)}, u32[]{:S(2)}) collective-permute-start(bf16[256,1152]{1,0:T(8,128)(2,1)S(1)} %collective-permute-done.2.refs_5_), channel_id=1, source_target_pairs={{0,128},{1,129},{2,130},{3,131},{4,132},{5,133},{6,134},{7,135},{8... | collective-permute-start | bytes 1769480 | tf_op jit(solution)/shard_map/ppermute | solution.py:351
  49.7 11.4 %collective-permute-start.5 = (bf16[256,1152]{1,0:T(8,128)(2,1)S(1)}, bf16[256,1152]{1,0:T(8,128)(2,1)S(1)}, u32[]{:S(2)}, u32[]{:S(2)}) collective-permute-start(bf16[256,1152]{1,0:T(8,128)(2,1)S(1)} %collective-permute-done.4.refs_6_), channel_id=1, source_target_pairs={{0,384},{1,385},{2,386},{3,387},{4,388},{5,389},{6,390},{7,391},{8... | collective-permute-start | bytes 1769480 | tf_op jit(solution)/shard_map/ppermute | solution.py:352
  60.7 9.4 %copy-start.4 = (f32[256,1152]{1,0:T(8,128)S(1)}, f32[256,1152]{1,0:T(8,128)}, u32[]{:S(2)}) copy-start(f32[256,1152]{1,0:T(8,128)} %get-tuple-element.51) | copy-start | bytes 3538948
  62.9 7.1 %collective-permute-start.8 = (f32[128,1152]{1,0:T(8,128)S(1)}, f32[128,1152]{1,0:T(8,128)S(1)}, u32[]{:S(2)}, u32[]{:S(2)}) collective-permute-start(f32[128,1152]{1,0:T(8,128)S(1)} %get-tuple-element.45), channel_id=1, source_target_pairs={{0,32},{1,33},{2,34},{3,35},{4,36},{5,37},{6,38},{7,39},{8,40},{9,... | collective-permute-start | bytes 1769480 | tf_op jit(solution)/shard_map/ppermute | solution.py:91
  68.5 1.7 slice-start
  83.2 12.9 %all-to-all-start.2 = ((f32[4,80,768]{2,1,0:T(8,128)}), f32[4,80,768]{2,1,0:T(8,128)S(1)}, u32[]{:S(2)}, u32[]{:S(2)}) async-start(f32[4,80,768]{2,1,0:T(8,128)} %bitcast.37), calls=%async_computation.2 | async-start | bytes 1966080 | tf_op jit(solution)/shard_map/all_to_all | solution.py:83
  86.8 36.9 %copy-start.1 = (f32[36,768]{1,0:T(8,128)S(1)}, f32[36,768]{1,0:T(8,128)}, u32[]{:S(2)}) copy-start(f32[36,768]{1,0:T(8,128)} %second_ref.1) | copy-start | bytes 331780
  86.8 36.9 %copy-start.2 = (f32[36,768]{1,0:T(8,128)S(1)}, f32[36,768]{1,0:T(8,128)}, u32[]{:S(2)}) copy-start(f32[36,768]{1,0:T(8,128)} %first_ref.1) | copy-start | bytes 331780
  96.2 5.0 %collective-permute-start.9 = (f32[88,384]{1,0:T(8,128)S(1)}, f32[88,384]{1,0:T(8,128)S(1)}, u32[]{:S(2)}, u32[]{:S(2)}) collective-permute-start(f32[88,384]{1,0:T(8,128)S(1)} %select_maximum_fusion), channel_id=1, source_target_pairs={{0,32},{1,33},{2,34},{3,35},{4,36},{5,37},{6,38},{7,39},{8,40},{9,... | collective-permute-start | bytes 405512 | tf_op jit(solution)/shard_map/ppermute | solution.py:91
  101.9 21.7 %all-to-all-start.3 = ((f32[16,16,128]{2,1,0:T(8,128)}), f32[16,16,128]{2,1,0:T(8,128)S(1)}, u32[]{:S(2)}, u32[]{:S(2)}) async-start(f32[16,16,128]{2,1,0:T(8,128)} %pad.22), calls=%async_computation.3 | async-start | bytes 262144 | tf_op jit(solution)/shard_map/all_to_all | solution.py:83
  143.3 18.8 %all-to-all-start.5 = ((bf16[16,96,384]{2,1,0:T(8,128)(2,1)}), bf16[16,96,384]{2,1,0:T(8,128)(2,1)}, u32[]{:S(2)}, u32[]{:S(2)}) async-start(bf16[16,96,384]{2,1,0:T(8,128)(2,1)} %broadcast_in_dim.11), calls=%async_computation.5 | async-start | bytes 2359296 | tf_op jit(solution)/shard_map/all_to_all | solution.py:83
  166.2 9.0 %collective-permute-start.10 = (bf16[1296,384]{1,0:T(8,128)(2,1)S(1)}, bf16[1296,384]{1,0:T(8,128)(2,1)S(1)}, u32[]{:S(2)}, u32[]{:S(2)}) collective-permute-start(bf16[1296,384]{1,0:T(8,128)(2,1)S(1)} %pad_maximum_fusion.half_ref), channel_id=1, source_target_pairs={{0,32},{1,33},{2,34},{3,35},{4,36},{5,37},{6,38},{7,39},{8,40},{9,... | collective-permute-start | bytes 2985992 | tf_op jit(solution)/shard_map/ppermute | solution.py:91

commit v7 on v6

--- a/solution.py
+++ b/solution.py
@@ -2,6 +2,7 @@
 
 import jax
 import jax.numpy as jnp
+import numpy as np
 from jax import lax
 from jax.experimental import pallas as pl
 from jax.experimental.pallas import tpu as pltpu
@@ -144,6 +145,35 @@
             flops=8 * texts.size, bytes_accessed=2 * (count + 2) * rows * width, transcendentals=0
         ),
     )(texts, features, teacher)
+
+
+def select_kernel(xl_ref, rows_ref, plane_ref, out_ref):
+    def picked(count, which, part):
+        rows = lax.broadcasted_iota(jnp.int32, (count, rows_ref.shape[1]), 0)
+        chosen = (rows == rows_ref[which : which + 1, :]).astype(jnp.bfloat16)
+        return [
+            jnp.dot(chosen, values, preferred_element_type=jnp.float32).astype(jnp.bfloat16)
+            for values in part
+        ]
+
+    low, high = picked(576, 0, (plane_ref[0], plane_ref[1]))
+    out_ref[:576, :] = low
+    out_ref[576:1152, :] = high
+    (out_ref[1152:, :],) = picked(144, 1, (plane_ref[xl_ref[0]],))
+
+
+def selected(xl, plane):
+    whole = pl.BlockSpec(memory_space=pltpu.VMEM)
+    return pl.pallas_call(
+        select_kernel,
+        out_shape=jax.ShapeDtypeStruct((1296, 384), jnp.bfloat16),
+        in_specs=[pl.BlockSpec(memory_space=pltpu.SMEM), whole, whole],
+        out_specs=whole,
+        compiler_params=pltpu.CompilerParams(vmem_limit_bytes=12 << 20),
+        cost_estimate=pl.CostEstimate(
+            flops=2 * 1296 * 768 * 384, bytes_accessed=2 << 20, transcendentals=0
+        ),
+    )(xl.reshape(1), jnp.asarray(place_rows()), plane)
 
 
 def last_kernel(core_ref, half_ref, twin_ref, first_ref, second_ref, *outs):
@@ -271,16 +301,12 @@
     return jnp.where(row < 36, X // 2 * 576 + place // 5 % 16 * 36 + row, -1)
 
 
-def weight_order():
-    row = lax.iota(jnp.int32, 576)
-    q = row % 36
-    return q // 5 * 96 + row // 36 * 5 + q % 5
-
-
-def grad_order():
-    part = lax.iota(jnp.int32, 144)
-    q = part % 48
-    return jnp.where(q < 40, q // 5 * 96 + 80 + part // 48 * 5 + q % 5, -1)
+def place_rows():
+    chip, row = np.arange(768) // 96, np.arange(768) % 96
+    q = chip * 5 + row % 5
+    weights = np.where((row < 80) & (q < 36), row // 5 * 36 + q, -1)
+    grads = np.where((row >= 80) & (row < 95), (row - 80) // 5 * 48 + q, -1)
+    return np.stack([weights, grads]).astype(np.int32)
 
 
 def one_hot(index, width):
@@ -414,16 +440,7 @@
     spare = jnp.zeros((1, 384), jnp.float32)
     grad_parts = jnp.concatenate([high, middle, low, spare], axis=0).astype(jnp.bfloat16)
     plane = share(jnp.concatenate([chip_weights, grad_parts], axis=0), PLANE).reshape(2, 768, 384)
-    select_weights = one_hot(weight_order(), 768)
-    halves = [
-        jnp.dot(select_weights, plane[i], preferred_element_type=jnp.float32) for i in range(2)
-    ]
-    group_parts = jnp.dot(
-        one_hot(grad_order(), 768),
-        lax.dynamic_index_in_dim(plane, xl, 0, keepdims=False),
-        preferred_element_type=jnp.float32,
-    )
-    half = jnp.concatenate([*halves, group_parts], axis=0).astype(jnp.bfloat16)
+    half = selected(xl, plane)
     new_weights, new_first, new_second = last_outputs(
         core, half, from_twin(half), moment_first, moment_second
     )

time: 178 us -> 174 us (0.978)
  blocking collectives: 28.5 us -> 46.5 us
  waiting for transfers between devices: 51.2 us -> 37 us
  starting transfers between devices: 68.5 us -> 63.8 us
  matrix products: 6.16 us -> 3.42 us
  local copies, waits for them, and re-layouts: 7.63 us -> 5.22 us
    all_to_all x2 -> x3, blocking collectives: 28.5 us -> 46.5 us  [exchange(): lax.all_to_all(pieces, AXES, 0, 0, axis_index_groups=groups, tiled=True)]
    all_to_all x4 -> x3, waiting for transfers between devices: 46.6 us -> 32.4 us  [exchange(): lax.all_to_all(pieces, AXES, 0, 0, axis_index_groups=groups, tiled=True)]
    all_to_all x4 -> x3, starting transfers between devices: 21.9 us -> 18.3 us  [exchange(): lax.all_to_all(pieces, AXES, 0, 0, axis_index_groups=groups, tiled=True)]
    dot_general x3 -> x0, matrix products: 2.73 us -> none  [the longest x1 1.39 us: per_device(): jnp.dot(one_hot(grad_order(), 768), lax.dynamic_index_in_dim(plane, xl, 0...]
  transfers between devices with their start and end apart: 15 -> 14, of which waited for: 8 -> 7; matrix products, arithmetic and copies ran while one was open for 3% -> 3% of each run, Pallas kernels for 3% -> 3%
where the time goes in v7:
time: 174 us; the launch traced here: 173 us
  starting transfers between devices  63.8 us (37%)
  blocking collectives  46.5 us (27%)
  waiting for transfers between devices  37 us (21%)
  Pallas kernels  12.3 us (7%)
  local copies, waits for them, and re-layouts  5.22 us (3%)
  other arithmetic  3.42 us (2%)
  matrix products  3.42 us (2%)
    all_to_all x3, blocking collectives, exchange(): lax.all_to_all(pieces, AXES, 0, 0, axis_index_groups=groups, tiled=True)  46.5 us
    all_to_all x3, waiting for transfers between devices, exchange(): lax.all_to_all(pieces, AXES, 0, 0, axis_index_groups=groups, tiled=True)  32.4 us
    ppermute x5, starting transfers between devices, from_twin(): return lax.ppermute(shard, AXES, TWIN)  25.9 us
    all_to_all x3, starting transfers between devices, exchange(): lax.all_to_all(pieces, AXES, 0, 0, axis_index_groups=groups, tiled=True)  18.3 us
    pallas_call x3, Pallas kernels, pair_sums(): pl.pallas_call(functools.partial(pair_kernel, places, bool(carried), last...  6.92 us
    ppermute x1, starting transfers between devices, per_device(): after_bottom = lax.ppermute(bottom, AXES, BACK)  4.57 us
    ppermute x1, starting transfers between devices, per_device(): after_top = lax.ppermute(top, AXES, BACK)  4.57 us
    ppermute x1, starting transfers between devices, per_device(): far_bottom = lax.ppermute(after_bottom, AXES, BACK)  4.57 us
  transfers between devices with their start and end apart: 14, of which 7 were waited for; matrix products, arithmetic and copies ran while one was open for 3% of the time, Pallas kernels for 3%

profile of v7, /device:TPU:1, one launch (start us, length us, event | category | flops | bytes accessed | tf_op | source)
XLA Modules:
  0.0 172.8 jit_solution(11551426846232563677)
XLA Ops:
  0.6 2.7 %shard_map.111 = (bf16[4,128,1920]{2,1,0:T(8,128)(2,1)}, bf16[128,1152]{1,0:T(8,128)(2,1)}) custom-call(bf16[128,1152]{1,0:T(8,128)(2,1)} %texts_ref.1, bf16[128,768]{1,0:T(8,128)(2,1)} %features_ref.1, bf16[128,1152]{1,0:T(8,128)(2,1)} %teacher_ref.1), custom_call_target="tpu_custom_call" | custom-call | flops 1179648 | bytes 2949120 | tf_op jit(solution)/shard_map/pallas_call | solution.py:128
  3.4 8.7 %collective-permute-start = (bf16[128,768]{1,0:T(8,128)(2,1)}, bf16[128,768]{1,0:T(8,128)(2,1)S(1)}, u32[]{:S(2)}, u32[]{:S(2)}) collective-permute-start(bf16[128,768]{1,0:T(8,128)(2,1)} %features_ref.1), channel_id=1, source_target_pairs={{0,32},{1,33},{2,34},{3,35},{4,36},{5,37},{6,38},{7,39},{8,40},{9,... | collective-permute-start | bytes 589832 | tf_op jit(solution)/shard_map/ppermute | solution.py:92
  12.1 2.1 %collective-permute-start.1 = (bf16[128,1152]{1,0:T(8,128)(2,1)}, bf16[128,1152]{1,0:T(8,128)(2,1)S(1)}, u32[]{:S(2)}, u32[]{:S(2)}) collective-permute-start(bf16[128,1152]{1,0:T(8,128)(2,1)} %get-tuple-element.32.refs_1_), channel_id=1, source_target_pairs={{0,32},{1,33},{2,34},{3,35},{4,36},{5,37},{6,38},{7,39},{8,40},{9,... | collective-permute-start | bytes 884744 | tf_op jit(solution)/shard_map/ppermute | solution.py:92
  14.2 4.4 %all-to-all-start = ((bf16[4,128,1920]{2,1,0:T(8,128)(2,1)}), bf16[4,128,1920]{2,1,0:T(8,128)(2,1)}, u32[]{:S(2)}, u32[]{:S(2)}) async-start(bf16[4,128,1920]{2,1,0:T(8,128)(2,1)} %get-tuple-element.28), calls=%async_computation | async-start | bytes 3932160 | tf_op jit(solution)/shard_map/all_to_all | solution.py:84
  22.5 10.9 %all-to-all-done = bf16[4,128,1920]{2,1,0:T(8,128)(2,1)} async-done(((bf16[4,128,1920]{2,1,0:T(8,128)(2,1)}), bf16[4,128,1920]{2,1,0:T(8,128)(2,1)}, u32[]{:S(2)}, u32[]{:S(2)}) %all-to-all-start) | async-done | bytes 1966112 | tf_op jit(solution)/shard_map/all_to_all | solution.py:84
  34.7 2.1 %collective-permute-start.2 = (bf16[256,1152]{1,0:T(8,128)(2,1)S(1)}, bf16[256,1152]{1,0:T(8,128)(2,1)S(1)}, u32[]{:S(2)}, u32[]{:S(2)}) collective-permute-start(bf16[256,1152]{1,0:T(8,128)(2,1)S(1)} %bitcast.26), channel_id=1, source_target_pairs={{0,128},{1,129},{2,130},{3,131},{4,132},{5,133},{6,134},{7,135},{8... | collective-permute-start | bytes 1769480 | tf_op jit(solution)/shard_map/ppermute | solution.py:373
  36.8 4.6 %collective-permute-start.4 = (bf16[256,1152]{1,0:T(8,128)(2,1)S(1)}, bf16[256,1152]{1,0:T(8,128)(2,1)S(1)}, u32[]{:S(2)}, u32[]{:S(2)}) collective-permute-start(bf16[256,1152]{1,0:T(8,128)(2,1)S(1)} %bitcast.29), channel_id=1, source_target_pairs={{0,384},{1,385},{2,386},{3,387},{4,388},{5,389},{6,390},{7,391},{8... | collective-permute-start | bytes 1769480 | tf_op jit(solution)/shard_map/ppermute | solution.py:374
  41.3 1.9 %collective-permute-start.6 = (bf16[256,1152]{1,0:T(8,128)(2,1)S(1)}, bf16[256,1152]{1,0:T(8,128)(2,1)S(1)}, u32[]{:S(2)}, u32[]{:S(2)}) collective-permute-start(bf16[256,1152]{1,0:T(8,128)(2,1)S(1)} %bitcast.30), channel_id=1, source_target_pairs={{0,128},{1,129},{2,130},{3,131},{4,132},{5,133},{6,134},{7,135},{8... | collective-permute-start | bytes 1769480 | tf_op jit(solution)/shard_map/ppermute | solution.py:375
  43.3 4.6 %collective-permute-start.7 = (bf16[256,1152]{1,0:T(8,128)(2,1)S(1)}, bf16[256,1152]{1,0:T(8,128)(2,1)S(1)}, u32[]{:S(2)}, u32[]{:S(2)}) collective-permute-start(bf16[256,1152]{1,0:T(8,128)(2,1)S(1)} %bitcast.27), channel_id=1, source_target_pairs={{0,384},{1,385},{2,386},{3,387},{4,388},{5,389},{6,390},{7,391},{8... | collective-permute-start | bytes 1769480 | tf_op jit(solution)/shard_map/ppermute | solution.py:376
  47.9 1.9 %collective-permute-start.3 = (bf16[256,1152]{1,0:T(8,128)(2,1)S(1)}, bf16[256,1152]{1,0:T(8,128)(2,1)S(1)}, u32[]{:S(2)}, u32[]{:S(2)}) collective-permute-start(bf16[256,1152]{1,0:T(8,128)(2,1)S(1)} %collective-permute-done.2.refs_5_), channel_id=1, source_target_pairs={{0,128},{1,129},{2,130},{3,131},{4,132},{5,133},{6,134},{7,135},{8... | collective-permute-start | bytes 1769480 | tf_op jit(solution)/shard_map/ppermute | solution.py:377
  49.8 4.6 %collective-permute-start.5 = (bf16[256,1152]{1,0:T(8,128)(2,1)S(1)}, bf16[256,1152]{1,0:T(8,128)(2,1)S(1)}, u32[]{:S(2)}, u32[]{:S(2)}) collective-permute-start(bf16[256,1152]{1,0:T(8,128)(2,1)S(1)} %collective-permute-done.4.refs_6_), channel_id=1, source_target_pairs={{0,384},{1,385},{2,386},{3,387},{4,388},{5,389},{6,390},{7,391},{8... | collective-permute-start | bytes 1769480 | tf_op jit(solution)/shard_map/ppermute | solution.py:378
  55.6 1.8 %shard_map.112 = (f32[256,1152]{1,0:T(8,128)S(1)}, f32[256,1]{1,0:T(8,128)S(1)}) custom-call(bf16[256,1152]{1,0:T(8,128)(2,1)S(1)} %get-tuple-element.31.refs_0_, bf16[128,1152]{1,0:T(8,128)(2,1)S(1)} %copy-done.3, bf16[128,1152]{1,0:T(8,128)(2,1)S(1)} %collective-permute-done.1.refs_2_, s32[2,128]{1,0:T(2,128)S(1)} %pad_add_fusion.refs_3_, ...), custom_call_target="tpu_custom_call" | custom-call | flops 905969664 | bytes 1179648 | tf_op jit(solution)/shard_map/pallas_call | solution.py:280
  57.4 3.3 %shard_map.113 = (f32[256,1152]{1,0:T(8,128)S(1)}, f32[256,1]{1,0:T(8,128)S(1)}) custom-call(bf16[256,1152]{1,0:T(8,128)(2,1)S(1)} %get-tuple-element.31.refs_0_, bf16[128,1152]{1,0:T(8,128)(2,1)S(1)} %copy-done.3, bf16[128,1152]{1,0:T(8,128)(2,1)S(1)} %collective-permute-done.1.refs_2_, s32[2,128]{1,0:T(2,128)S(1)} %pad_add_fusion.refs_3_, ...), custom_call_target="tpu_custom_call" | custom-call | flops 1811939328 | bytes 2359296 | tf_op jit(solution)/shard_map/pallas_call | solution.py:280
  61.2 1.8 %shard_map.114 = (f32[128,1152]{1,0:T(8,128)S(1)}, f32[128,1152]{1,0:T(8,128)S(1)}, f32[2,128]{1,0:T(2,128)S(1)}) custom-call(bf16[256,1152]{1,0:T(8,128)(2,1)S(1)} %get-tuple-element.31.refs_0_, bf16[128,1152]{1,0:T(8,128)(2,1)S(1)} %copy-done.3, bf16[128,1152]{1,0:T(8,128)(2,1)S(1)} %collective-permute-done.1.refs_2_, s32[2,128]{1,0:T(2,128)S(1)} %pad_add_fusion.refs_3_, ...), custom_call_target="tpu_custom_call" | custom-call | flops 905969664 | bytes 1179648 | tf_op jit(solution)/shard_map/pallas_call | solution.py:280
  63.0 5.5 %collective-permute-start.8 = (f32[128,1152]{1,0:T(8,128)S(1)}, f32[128,1152]{1,0:T(8,128)S(1)}, u32[]{:S(2)}, u32[]{:S(2)}) collective-permute-start(f32[128,1152]{1,0:T(8,128)S(1)} %get-tuple-element.45), channel_id=1, source_target_pairs={{0,32},{1,33},{2,34},{3,35},{4,36},{5,37},{6,38},{7,39},{8,40},{9,... | collective-permute-start | bytes 1769480 | tf_op jit(solution)/shard_map/ppermute | solution.py:92
  71.6 10.4 %all_to_all.30 = bf16[4,320,128]{2,1,0:T(8,128)(2,1)S(1)} all-to-all(bf16[4,320,128]{2,1,0:T(8,128)(2,1)S(1)} %bitcast.32), channel_id=1, replica_groups={{0,64,16,80},{128,192,144,208},{256,320,272,336},{384,448,400,464},{1,6..., dimensions={0} | all-to-all | bytes 655360 | tf_op jit(solution)/shard_map/all_to_all | solution.py:84
  83.3 4.2 %all-to-all-start.2 = ((f32[4,80,768]{2,1,0:T(8,128)}), f32[4,80,768]{2,1,0:T(8,128)}, u32[]{:S(2)}, u32[]{:S(2)}) async-start(f32[4,80,768]{2,1,0:T(8,128)} %bitcast.11), calls=%async_computation.2 | async-start | bytes 1966080 | tf_op jit(solution)/shard_map/all_to_all | solution.py:84
  87.5 9.4 %all-to-all-done.2 = f32[4,80,768]{2,1,0:T(8,128)} async-done(((f32[4,80,768]{2,1,0:T(8,128)}), f32[4,80,768]{2,1,0:T(8,128)}, u32[]{:S(2)}, u32[]{:S(2)}) %all-to-all-start.2) | async-done | bytes 983072 | tf_op jit(solution)/shard_map/all_to_all | solution.py:84
  98.3 3.4 %collective-permute-start.9 = (f32[88,384]{1,0:T(8,128)S(1)}, f32[88,384]{1,0:T(8,128)S(1)}, u32[]{:S(2)}, u32[]{:S(2)}) collective-permute-start(f32[88,384]{1,0:T(8,128)S(1)} %select_maximum_fusion), channel_id=1, source_target_pairs={{0,32},{1,33},{2,34},{3,35},{4,36},{5,37},{6,38},{7,39},{8,40},{9,... | collective-permute-start | bytes 405512 | tf_op jit(solution)/shard_map/ppermute | solution.py:92
  103.4 9.6 %all-to-all-start.3 = ((f32[16,16,128]{2,1,0:T(8,128)}), f32[16,16,128]{2,1,0:T(8,128)S(1)}, u32[]{:S(2)}, u32[]{:S(2)}) async-start(f32[16,16,128]{2,1,0:T(8,128)} %pad.22), calls=%async_computation.3 | async-start | bytes 262144 | tf_op jit(solution)/shard_map/all_to_all | solution.py:84
  113.1 12.0 %all-to-all-done.3 = f32[16,16,128]{2,1,0:T(8,128)S(1)} async-done(((f32[16,16,128]{2,1,0:T(8,128)}), f32[16,16,128]{2,1,0:T(8,128)S(1)}, u32[]{:S(2)}, u32[]{:S(2)}) %all-to-all-start.3) | async-done | bytes 131104 | tf_op jit(solution)/shard_map/all_to_all | solution.py:84
  125.3 18.2 %all_to_all.31 = bf16[16,5,384]{2,1,0:T(8,128)(2,1)S(1)} all-to-all(bf16[16,5,384]{2,1,0:T(8,128)(2,1)S(1)} %broadcast_in_dim.8), channel_id=1, replica_groups={{0,1,2,3,4,5,6,7,8,9,10,11,12,13,14,15},{32,33,34,35,36,37,38,39,40,41,..., dimensions={0} | all-to-all | bytes 122880 | tf_op jit(solution)/shard_map/all_to_all | solution.py:84
  143.8 18.0 %all_to_all.32 = bf16[16,96,384]{2,1,0:T(8,128)(2,1)S(1)} all-to-all(bf16[16,96,384]{2,1,0:T(8,128)(2,1)S(1)} %broadcast_in_dim.10), channel_id=1, replica_groups={{0,128,256,384,64,192,320,448,16,144,272,400,80,208,336,464},{1,129,257..., dimensions={0} | all-to-all | bytes 2359296 | tf_op jit(solution)/shard_map/all_to_all | solution.py:84
  163.0 6.2 %collective-permute-start.10 = (bf16[1296,384]{1,0:T(8,128)(2,1)S(1)}, bf16[1296,384]{1,0:T(8,128)(2,1)S(1)}, u32[]{:S(2)}, u32[]{:S(2)}) collective-permute-start(bf16[1296,384]{1,0:T(8,128)(2,1)S(1)} %shard_map.115.half_ref), channel_id=1, source_target_pairs={{0,32},{1,33},{2,34},{3,35},{4,36},{5,37},{6,38},{7,39},{8,40},{9,... | collective-permute-start | bytes 2985992 | tf_op jit(solution)/shard_map/ppermute | solution.py:92
  (65 shorter events, 19.4 us)
Async XLA Ops:
  0.6 19.8 %copy-start = (bf16[1152,768]{1,0:T(8,128)(2,1)S(1)}, bf16[1152,768]{1,0:T(8,128)(2,1)}, u32[]{:S(2)}) copy-start(bf16[1152,768]{1,0:T(8,128)(2,1)} %param.12) | copy-start | bytes 5308420
  3.4 17.1 %collective-permute-start = (bf16[128,768]{1,0:T(8,128)(2,1)}, bf16[128,768]{1,0:T(8,128)(2,1)S(1)}, u32[]{:S(2)}, u32[]{:S(2)}) collective-permute-start(bf16[128,768]{1,0:T(8,128)(2,1)} %features_ref.1), channel_id=1, source_target_pairs={{0,32},{1,33},{2,34},{3,35},{4,36},{5,37},{6,38},{7,39},{8,40},{9,... | collective-permute-start | bytes 589832 | tf_op jit(solution)/shard_map/ppermute | solution.py:92
  12.1 8.3 %copy-start.6 = (bf16[128,768]{1,0:T(8,128)(2,1)S(1)}, bf16[128,768]{1,0:T(8,128)(2,1)}, u32[]{:S(2)}) copy-start(bf16[128,768]{1,0:T(8,128)(2,1)} %features_ref.1) | copy-start | bytes 589828
  12.1 10.3 %collective-permute-start.1 = (bf16[128,1152]{1,0:T(8,128)(2,1)}, bf16[128,1152]{1,0:T(8,128)(2,1)S(1)}, u32[]{:S(2)}, u32[]{:S(2)}) collective-permute-start(bf16[128,1152]{1,0:T(8,128)(2,1)} %get-tuple-element.32.refs_1_), channel_id=1, source_target_pairs={{0,32},{1,33},{2,34},{3,35},{4,36},{5,37},{6,38},{7,39},{8,40},{9,... | collective-permute-start | bytes 884744 | tf_op jit(solution)/shard_map/ppermute | solution.py:92
  14.2 19.2 %all-to-all-start = ((bf16[4,128,1920]{2,1,0:T(8,128)(2,1)}), bf16[4,128,1920]{2,1,0:T(8,128)(2,1)}, u32[]{:S(2)}, u32[]{:S(2)}) async-start(bf16[4,128,1920]{2,1,0:T(8,128)(2,1)} %get-tuple-element.28), calls=%async_computation | async-start | bytes 3932160 | tf_op jit(solution)/shard_map/all_to_all | solution.py:84
  21.3 47.3 %copy-start.7 = (f32[256]{0:T(256)}, f32[256]{0:T(256)S(1)}, u32[]{:S(2)}) copy-start(f32[256]{0:T(256)S(1)} %add_rsqrt_fusion) | copy-start | bytes 3076
  34.7 20.9 %copy-start.3 = (bf16[128,1152]{1,0:T(8,128)(2,1)S(1)}, bf16[128,1152]{1,0:T(8,128)(2,1)}, u32[]{:S(2)}) copy-start(bf16[128,1152]{1,0:T(8,128)(2,1)} %get-tuple-element.32.refs_1_) | copy-start | bytes 884740
  34.7 13.2 %collective-permute-start.2 = (bf16[256,1152]{1,0:T(8,128)(2,1)S(1)}, bf16[256,1152]{1,0:T(8,128)(2,1)S(1)}, u32[]{:S(2)}, u32[]{:S(2)}) collective-permute-start(bf16[256,1152]{1,0:T(8,128)(2,1)S(1)} %bitcast.26), channel_id=1, source_target_pairs={{0,128},{1,129},{2,130},{3,131},{4,132},{5,133},{6,134},{7,135},{8... | collective-permute-start | bytes 1769480 | tf_op jit(solution)/shard_map/ppermute | solution.py:373
  36.8 13.0 %collective-permute-start.4 = (bf16[256,1152]{1,0:T(8,128)(2,1)S(1)}, bf16[256,1152]{1,0:T(8,128)(2,1)S(1)}, u32[]{:S(2)}, u32[]{:S(2)}) collective-permute-start(bf16[256,1152]{1,0:T(8,128)(2,1)S(1)} %bitcast.29), channel_id=1, source_target_pairs={{0,384},{1,385},{2,386},{3,387},{4,388},{5,389},{6,390},{7,391},{8... | collective-permute-start | bytes 1769480 | tf_op jit(solution)/shard_map/ppermute | solution.py:374
  41.3 16.0 %collective-permute-start.6 = (bf16[256,1152]{1,0:T(8,128)(2,1)S(1)}, bf16[256,1152]{1,0:T(8,128)(2,1)S(1)}, u32[]{:S(2)}, u32[]{:S(2)}) collective-permute-start(bf16[256,1152]{1,0:T(8,128)(2,1)S(1)} %bitcast.30), channel_id=1, source_target_pairs={{0,128},{1,129},{2,130},{3,131},{4,132},{5,133},{6,134},{7,135},{8... | collective-permute-start | bytes 1769480 | tf_op jit(solution)/shard_map/ppermute | solution.py:375
  43.3 14.1 %collective-permute-start.7 = (bf16[256,1152]{1,0:T(8,128)(2,1)S(1)}, bf16[256,1152]{1,0:T(8,128)(2,1)S(1)}, u32[]{:S(2)}, u32[]{:S(2)}) collective-permute-start(bf16[256,1152]{1,0:T(8,128)(2,1)S(1)} %bitcast.27), channel_id=1, source_target_pairs={{0,384},{1,385},{2,386},{3,387},{4,388},{5,389},{6,390},{7,391},{8... | collective-permute-start | bytes 1769480 | tf_op jit(solution)/shard_map/ppermute | solution.py:376
  47.9 12.9 %collective-permute-start.3 = (bf16[256,1152]{1,0:T(8,128)(2,1)S(1)}, bf16[256,1152]{1,0:T(8,128)(2,1)S(1)}, u32[]{:S(2)}, u32[]{:S(2)}) collective-permute-start(bf16[256,1152]{1,0:T(8,128)(2,1)S(1)} %collective-permute-done.2.refs_5_), channel_id=1, source_target_pairs={{0,128},{1,129},{2,130},{3,131},{4,132},{5,133},{6,134},{7,135},{8... | collective-permute-start | bytes 1769480 | tf_op jit(solution)/shard_map/ppermute | solution.py:377
  49.8 11.4 %collective-permute-start.5 = (bf16[256,1152]{1,0:T(8,128)(2,1)S(1)}, bf16[256,1152]{1,0:T(8,128)(2,1)S(1)}, u32[]{:S(2)}, u32[]{:S(2)}) collective-permute-start(bf16[256,1152]{1,0:T(8,128)(2,1)S(1)} %collective-permute-done.4.refs_6_), channel_id=1, source_target_pairs={{0,384},{1,385},{2,386},{3,387},{4,388},{5,389},{6,390},{7,391},{8... | collective-permute-start | bytes 1769480 | tf_op jit(solution)/shard_map/ppermute | solution.py:378
  60.7 9.4 %copy-start.5 = (f32[256,1152]{1,0:T(8,128)S(1)}, f32[256,1152]{1,0:T(8,128)}, u32[]{:S(2)}) copy-start(f32[256,1152]{1,0:T(8,128)} %get-tuple-element.51) | copy-start | bytes 3538948
  63.0 7.1 %collective-permute-start.8 = (f32[128,1152]{1,0:T(8,128)S(1)}, f32[128,1152]{1,0:T(8,128)S(1)}, u32[]{:S(2)}, u32[]{:S(2)}) collective-permute-start(f32[128,1152]{1,0:T(8,128)S(1)} %get-tuple-element.45), channel_id=1, source_target_pairs={{0,32},{1,33},{2,34},{3,35},{4,36},{5,37},{6,38},{7,39},{8,40},{9,... | collective-permute-start | bytes 1769480 | tf_op jit(solution)/shard_map/ppermute | solution.py:92
  68.6 1.7 %slice-start = ((f32[256]{0:T(256)}), f32[128]{0:T(128)S(1)}, s32[]{:S(2)}) async-start(f32[256]{0:T(256)} %copy-done.7), calls=%async_computation.6 | async-start | bytes 1024 | tf_op jit(solution)/shard_map/slice | solution.py:388
  83.3 13.7 %all-to-all-start.2 = ((f32[4,80,768]{2,1,0:T(8,128)}), f32[4,80,768]{2,1,0:T(8,128)}, u32[]{:S(2)}, u32[]{:S(2)}) async-start(f32[4,80,768]{2,1,0:T(8,128)} %bitcast.11), calls=%async_computation.2 | async-start | bytes 1966080 | tf_op jit(solution)/shard_map/all_to_all | solution.py:84
  98.3 26.9 %copy-start.1 = (f32[36,768]{1,0:T(8,128)S(1)}, f32[36,768]{1,0:T(8,128)}, u32[]{:S(2)}) copy-start(f32[36,768]{1,0:T(8,128)} %second_ref.1) | copy-start | bytes 331780
  98.3 26.9 %copy-start.2 = (f32[36,768]{1,0:T(8,128)S(1)}, f32[36,768]{1,0:T(8,128)}, u32[]{:S(2)}) copy-start(f32[36,768]{1,0:T(8,128)} %first_ref.1) | copy-start | bytes 331780
  98.3 4.4 %collective-permute-start.9 = (f32[88,384]{1,0:T(8,128)S(1)}, f32[88,384]{1,0:T(8,128)S(1)}, u32[]{:S(2)}, u32[]{:S(2)}) collective-permute-start(f32[88,384]{1,0:T(8,128)S(1)} %select_maximum_fusion), channel_id=1, source_target_pairs={{0,32},{1,33},{2,34},{3,35},{4,36},{5,37},{6,38},{7,39},{8,40},{9,... | collective-permute-start | bytes 405512 | tf_op jit(solution)/shard_map/ppermute | solution.py:92
  103.4 21.7 %all-to-all-start.3 = ((f32[16,16,128]{2,1,0:T(8,128)}), f32[16,16,128]{2,1,0:T(8,128)S(1)}, u32[]{:S(2)}, u32[]{:S(2)}) async-start(f32[16,16,128]{2,1,0:T(8,128)} %pad.22), calls=%async_computation.3 | async-start | bytes 262144 | tf_op jit(solution)/shard_map/all_to_all | solution.py:84
  143.8 18.0 %copy-start.4 = (s32[2,768]{1,0:T(2,128)S(1)}, s32[2,768]{1,0:T(2,128)}, u32[]{:S(2)}) copy-start(s32[2,768]{1,0:T(2,128)} %constant.221.clone.rows_ref) | copy-start | bytes 18436
  163.0 8.4 %collective-permute-start.10 = (bf16[1296,384]{1,0:T(8,128)(2,1)S(1)}, bf16[1296,384]{1,0:T(8,128)(2,1)S(1)}, u32[]{:S(2)}, u32[]{:S(2)}) collective-permute-start(bf16[1296,384]{1,0:T(8,128)(2,1)S(1)} %shard_map.115.half_ref), channel_id=1, source_target_pairs={{0,32},{1,33},{2,34},{3,35},{4,36},{5,37},{6,38},{7,39},{8,40},{9,... | collective-permute-start | bytes 2985992 | tf_op jit(solution)/shard_map/ppermute | solution.py:92
